TPU v7x, 32 devices: a whole 2x2x4 slice. The times are simulated.
32 devices in a mesh: dp: 4 (over y, x), expert: 8 (over z, core).
Axes of the slice: x: 2, y: 2, z: 4, core: 2. Of those that a mesh axis runs over, the one named last changes fastest.
Arguments:
- hidden: bfloat16 [16384, 1024], P(('dp', 'expert')), may hold values from -6 to 6
- segment_ids: int32 [32, 512], P(('dp', 'expert')), may hold values from 0 to 3, never falling along the last dimension, each value on 1 to 256 neighbouring positions
- routes: int32 [16384, 8], P(('dp', 'expert')), may hold values from 0 to 31, all different within a row; in each aligned block of 512 rows (0 to 511, 512 to 1023, ...) at most 192 rows name the same one
- norm_attn: bfloat16 [1024], P('expert'), may hold values from 0.5 to 1.5
- w_query: bfloat16 [1024, 1024], P('expert'), may hold values from -0.1875 to 0.1875
- key_weight: bfloat16 [1024, 512], P('expert'), may hold values from -0.1875 to 0.1875
- value_weight: bfloat16 [1024, 512], P('expert'), may hold values from -0.1875 to 0.1875
- w_out: bfloat16 [1024, 1024], P('expert'), may hold values from -0.75 to 0.75
- norm_moe: bfloat16 [1024], P('expert'), may hold values from 0.5 to 1.5
- w_router: bfloat16 [1024, 32], P('expert'), may hold values from -0.09375 to 0.09375
- w_gate: bfloat16 [32, 1024, 512], P('expert'), may hold values from -0.1875 to 0.1875
- w_up: bfloat16 [32, 1024, 512], P('expert'), may hold values from -0.1875 to 0.1875
- w_down: bfloat16 [32, 512, 1024], P('expert'), may hold values from -1 to 1
- cotangent: bfloat16 [16384, 1024], P(('dp', 'expert')), may hold values from -6 to 6
Outputs:
- output: bfloat16 [16384, 1024], P(('dp', 'expert'))
- grad_input: bfloat16 [16384, 1024], P(('dp', 'expert'))
- grad_norm_attn: float32 [1024], P('expert')
- grad_query: float32 [1024, 1024], P('expert')
- grad_key: float32 [1024, 512], P('expert')
- grad_value: float32 [1024, 512], P('expert')
- grad_out: float32 [1024, 1024], P('expert')
- grad_norm_moe: float32 [1024], P('expert')
- grad_router: float32 [1024, 32], P('expert')
- grad_gate: float32 [32, 1024, 512], P('expert')
- grad_up: float32 [32, 1024, 512], P('expert')
- grad_down: float32 [32, 512, 1024], P('expert')
Inputs may be any that keep to these rules, and one draw needn't show every extreme that they name: `segment_ids`: along each row the document numbers never fall; every document has 1 to half of the 512 tokens, and some has exactly that many. `routes`: each token names 8 different experts. Among the 512 tokens of one sequence no expert is named more than 192 times, and in some sequences one expert is named exactly 192 times.
All inputs are finite; a program needn't handle non-finite values.
Results may differ from a plain program's by a relative error of at most 0.022.
Values may be sent and summed in bfloat16 or wider, within the bound.
No kernel may reach another device: no remote copies, remote signals or barrier semaphores. Data moves between devices by JAX's collectives and lax.ppermute only.
A program may use at most 320 MiB of HBM per device.

v0:
```python
import jax
import jax.numpy as jnp
from jax import lax
from jax.sharding import PartitionSpec as P

QUERY_HEADS = 16
KEY_VALUE_HEADS = 8
HEAD_SIZE = 64
EXPERTS = 32
TOP = 8
CAP = 192


norm_eps = 1e-06
rope_base = 10000.0
masked_score = -1e30


def positions_of(segment_row):
    sequence_length = segment_row.shape[0]
    row_index = jnp.arange(sequence_length, dtype=jnp.int32)
    previous = jnp.concatenate([jnp.full((1,), -1, jnp.int32), segment_row[:-1]])
    starts = lax.cummax(jnp.where(segment_row != previous, row_index, 0), axis=0)
    return row_index - starts


def rope_tables(segment_row):
    position = positions_of(segment_row).astype(jnp.float32)
    half_size = HEAD_SIZE // 2
    frequency = rope_base ** (-jnp.arange(half_size, dtype=jnp.float32) / half_size)
    angles = position[:, None] * frequency[None, :]
    cosine_table = jnp.cos(angles)
    sine_lookup = jnp.sin(angles)
    return (
        jnp.concatenate([cosine_table, cosine_table], -1),
        jnp.concatenate([sine_lookup, sine_lookup], -1),
    )


def turn_half(vectors):
    half_size = vectors.shape[-1] // 2
    return jnp.concatenate([-vectors[..., half_size:], vectors[..., :half_size]], -1)


def apply_rotation(vectors, cosine_table, sine_lookup):
    return vectors * cosine_table[:, None, :] + turn_half(vectors) * sine_lookup[:, None, :]


def rotation_backward(gradient, cosine_table, sine_lookup):
    return gradient * cosine_table[:, None, :] - turn_half(gradient * sine_lookup[:, None, :])


def rms_scale(value_rows):
    return lax.rsqrt(jnp.mean(value_rows * value_rows, axis=-1, keepdims=True) + norm_eps)


def rms_backward(value_rows, inverse, gain, grad_normed):
    scaled = grad_normed * gain
    grad_gain = jnp.sum(grad_normed * value_rows * inverse, axis=0)
    value_rows_gradient = inverse * scaled - value_rows * inverse**3 * jnp.mean(
        scaled * value_rows, axis=-1, keepdims=True
    )
    return (value_rows_gradient, grad_gain)


def slot_index(route_rows):
    flat_routes = route_rows.reshape(-1)
    choose = (flat_routes[:, None] == jnp.arange(EXPERTS, dtype=jnp.int32)[None, :]).astype(
        jnp.int32
    )
    before = jnp.cumsum(choose, axis=0) - choose
    return flat_routes * CAP + jnp.sum(before * choose, axis=-1)


def block_scores(query_rows, keys_rot, segment_row, first_row, block_rows, score_scale):
    sequence_length = segment_row.shape[0]
    query_index = first_row + jnp.arange(block_rows, dtype=jnp.int32)
    key_index = jnp.arange(sequence_length, dtype=jnp.int32)
    allowed = (segment_row[:, None] == segment_row[None, :]) & (
        key_index[None, :] <= query_index[:, None]
    )
    scores = (
        jnp.einsum("qhgd,khd->hgqk", query_rows, keys_rot, preferred_element_type=jnp.float32)
        * score_scale
    )
    return (query_rows, jnp.where(allowed, scores, masked_score))


def attention_forward(query_rows, keys_rot, value_rows, segment_row, score_scale):
    sequence_length = query_rows.shape[0]
    block_rows = min(512, sequence_length)
    query_block, scores = block_scores(
        query_rows, keys_rot, segment_row, 0, block_rows, score_scale
    )
    largest = jnp.max(scores, axis=-1, keepdims=True)
    exponent = jnp.exp(scores - largest)
    row_total = jnp.sum(exponent, axis=-1, keepdims=True)
    probabilities = (exponent / row_total).astype(jnp.bfloat16)
    outputs = jnp.einsum(
        "hgqk,khd->qhgd", probabilities, value_rows, preferred_element_type=jnp.float32
    ).astype(jnp.bfloat16)
    row_sums = [largest + jnp.log(row_total)]
    return (outputs, row_sums)


def attention_backward(
    query_rows, keys_rot, value_rows, segment_row, score_scale, row_sums, mixed_gradient
):
    sequence_length = query_rows.shape[0]
    block_rows = min(512, sequence_length)
    grad_queries = []
    key_rows_gradient = jnp.zeros(keys_rot.shape, jnp.float32)
    value_rows_gradient = jnp.zeros(value_rows.shape, jnp.float32)
    for number, first_row in enumerate(range(0, sequence_length, block_rows)):
        query_block, scores = block_scores(
            query_rows, keys_rot, segment_row, first_row, block_rows, score_scale
        )
        probabilities = jnp.exp(scores - row_sums[number])
        probs_low = probabilities.astype(jnp.bfloat16)
        grad_probs = jnp.einsum(
            "qhgd,khd->hgqk", mixed_gradient, value_rows, preferred_element_type=jnp.float32
        )
        row_delta = jnp.sum(probabilities * grad_probs, axis=-1, keepdims=True)
        grad_scores = (probabilities * (grad_probs - row_delta)).astype(jnp.bfloat16)
        grad_queries.append(
            jnp.einsum("hgqk,khd->qhgd", grad_scores, keys_rot, preferred_element_type=jnp.float32)
            * score_scale
        )
        key_rows_gradient = (
            jnp.einsum(
                "hgqk,qhgd->khd", grad_scores, query_block, preferred_element_type=jnp.float32
            )
            * score_scale
        )
        value_rows_gradient = jnp.einsum(
            "hgqk,qhgd->khd", probs_low, mixed_gradient, preferred_element_type=jnp.float32
        )
    return (grad_queries[0], key_rows_gradient, value_rows_gradient)


def body(
    hidden,
    segment_ids,
    routes,
    norm_attn,
    w_query,
    key_weight,
    value_weight,
    w_out,
    norm_moe,
    w_router,
    w_gate,
    w_up,
    w_down,
    cotangent,
):
    gathered = (
        lax.all_gather(norm_attn, "expert", axis=0, tiled=True),
        lax.all_gather(w_query, "expert", axis=0, tiled=True),
        lax.all_gather(key_weight, "expert", axis=0, tiled=True),
        lax.all_gather(value_weight, "expert", axis=0, tiled=True),
        lax.all_gather(w_out, "expert", axis=0, tiled=True),
        lax.all_gather(w_router, "expert", axis=0, tiled=True),
        lax.all_gather(norm_moe, "expert", axis=0, tiled=True),
    )
    gain_attn = gathered[0].astype(jnp.float32)
    query_full = gathered[1]
    key_expanded = gathered[2]
    value_expanded = gathered[3]
    out_full = gathered[4]
    router_full = gathered[5]
    gain_moe = gathered[6].astype(jnp.float32)
    sequence_length = hidden.shape[0]
    model_width = hidden.shape[1]
    query_groups = QUERY_HEADS // KEY_VALUE_HEADS
    score_scale = HEAD_SIZE ** (-0.5)
    peer_count = lax.axis_size("expert")
    owned_experts = w_gate.shape[0]
    segment_row = segment_ids[0]
    cosine_table, sine_lookup = rope_tables(segment_row)
    inputs = hidden.astype(jnp.float32)
    inverse_one = rms_scale(inputs)
    attention_input = (inputs * inverse_one * gain_attn).astype(jnp.bfloat16)
    query_linear = jnp.dot(attention_input, query_full, preferred_element_type=jnp.float32).reshape(
        sequence_length, QUERY_HEADS, HEAD_SIZE
    )
    key_linear = jnp.dot(attention_input, key_expanded, preferred_element_type=jnp.float32).reshape(
        sequence_length, KEY_VALUE_HEADS, HEAD_SIZE
    )
    value_rows = (
        jnp.dot(attention_input, value_expanded, preferred_element_type=jnp.float32)
        .astype(jnp.bfloat16)
        .reshape(sequence_length, KEY_VALUE_HEADS, HEAD_SIZE)
    )
    query_rows = (
        apply_rotation(query_linear, cosine_table, sine_lookup)
        .astype(jnp.bfloat16)
        .reshape(sequence_length, KEY_VALUE_HEADS, query_groups, HEAD_SIZE)
    )
    keys_rot = apply_rotation(key_linear, cosine_table, sine_lookup).astype(jnp.bfloat16)
    mixed_heads, row_sums = attention_forward(
        query_rows, keys_rot, value_rows, segment_row, score_scale
    )
    mixed_flat = mixed_heads.reshape(sequence_length, QUERY_HEADS * HEAD_SIZE)
    residual = inputs + jnp.dot(mixed_flat, out_full, preferred_element_type=jnp.float32)
    inverse_two = rms_scale(residual)
    moe_in = (residual * inverse_two * gain_moe).astype(jnp.bfloat16)
    logits = jnp.dot(moe_in, router_full, preferred_element_type=jnp.float32)
    choose = routes[:, :, None] == jnp.arange(EXPERTS, dtype=jnp.int32)[None, None, :]
    chosen = jnp.sum(jnp.where(choose, logits[:, None, :], 0.0), axis=-1)
    gate_probs = jax.nn.softmax(chosen, axis=-1)
    flat_slot = slot_index(routes)
    token_rows = jnp.repeat(moe_in, TOP, axis=0)
    buffer = jnp.zeros((EXPERTS * CAP, model_width), jnp.bfloat16).at[flat_slot].set(token_rows)
    arrived = lax.all_to_all(
        buffer.reshape(peer_count, owned_experts * CAP, model_width),
        "expert",
        split_axis=0,
        concat_axis=0,
        tiled=True,
    )
    arrived = arrived.reshape(peer_count, owned_experts, CAP, model_width)
    gate_weights, up_weights, down_weights = (w_gate, w_up, w_down)
    gate_lin = jnp.einsum(
        "sjcd,jdf->sjcf", arrived, gate_weights, preferred_element_type=jnp.float32
    )
    up_lin = jnp.einsum("sjcd,jdf->sjcf", arrived, up_weights, preferred_element_type=jnp.float32)
    hidden_act = (jax.nn.silu(gate_lin) * up_lin).astype(jnp.bfloat16)
    expert_out = jnp.einsum(
        "sjcf,jfd->sjcd", hidden_act, down_weights, preferred_element_type=jnp.float32
    ).astype(jnp.bfloat16)
    returned = lax.all_to_all(
        expert_out.reshape(peer_count, owned_experts * CAP, model_width),
        "expert",
        split_axis=0,
        concat_axis=0,
        tiled=True,
    )
    returned = returned.reshape(EXPERTS * CAP, model_width)
    combined = returned[flat_slot].reshape(sequence_length, TOP, model_width).astype(jnp.float32)
    result = (residual + jnp.sum(gate_probs[:, :, None] * combined, axis=1)).astype(jnp.bfloat16)
    grad_result = cotangent.astype(jnp.float32)
    grad_expert = (gate_probs[:, :, None] * grad_result[:, None, :]).astype(jnp.bfloat16)
    grad_gate_probs = jnp.sum(grad_result[:, None, :] * combined, axis=-1)
    grad_chosen = gate_probs * (
        grad_gate_probs - jnp.sum(gate_probs * grad_gate_probs, axis=-1, keepdims=True)
    )
    grad_logits = jnp.sum(jnp.where(choose, grad_chosen[:, :, None], 0.0), axis=1).astype(
        jnp.bfloat16
    )
    grad_router = jnp.einsum("td,te->de", moe_in, grad_logits, preferred_element_type=jnp.float32)
    grad_moe_in = jnp.einsum(
        "te,de->td", grad_logits, router_full, preferred_element_type=jnp.float32
    )
    grad_buffer = (
        jnp.zeros((EXPERTS * CAP, model_width), jnp.bfloat16)
        .at[flat_slot]
        .set(grad_expert.reshape(sequence_length * TOP, model_width))
    )
    grad_arrived = lax.all_to_all(
        grad_buffer.reshape(peer_count, owned_experts * CAP, model_width),
        "expert",
        split_axis=0,
        concat_axis=0,
        tiled=True,
    )
    grad_arrived = grad_arrived.reshape(arrived.shape)
    grad_hidden = jnp.einsum(
        "sjcd,jfd->sjcf", grad_arrived, down_weights, preferred_element_type=jnp.float32
    )
    sigmoid_gate = jax.nn.sigmoid(gate_lin)
    activation = gate_lin * sigmoid_gate
    grad_gate_lin = (
        grad_hidden * up_lin * sigmoid_gate * (1.0 + gate_lin * (1.0 - sigmoid_gate))
    ).astype(jnp.bfloat16)
    grad_up_lin = (grad_hidden * activation).astype(jnp.bfloat16)
    grad_down = jnp.einsum(
        "sjcf,sjcd->jfd", hidden_act, grad_arrived, preferred_element_type=jnp.float32
    )
    grad_gate = jnp.einsum(
        "sjcd,sjcf->jdf", arrived, grad_gate_lin, preferred_element_type=jnp.float32
    )
    grad_up = jnp.einsum("sjcd,sjcf->jdf", arrived, grad_up_lin, preferred_element_type=jnp.float32)
    grad_rows = jnp.einsum(
        "sjcf,jdf->sjcd", grad_gate_lin, gate_weights, preferred_element_type=jnp.float32
    )
    grad_rows = (
        grad_rows
        + jnp.einsum("sjcf,jdf->sjcd", grad_up_lin, up_weights, preferred_element_type=jnp.float32)
    ).astype(jnp.bfloat16)
    grad_returned = lax.all_to_all(
        grad_rows.reshape(peer_count, owned_experts * CAP, model_width),
        "expert",
        split_axis=0,
        concat_axis=0,
        tiled=True,
    )
    grad_returned = grad_returned.reshape(EXPERTS * CAP, model_width)
    expert_grads = (grad_gate, grad_up, grad_down)
    grad_moe_in = grad_moe_in + jnp.sum(
        grad_returned[flat_slot].reshape(sequence_length, TOP, model_width).astype(jnp.float32),
        axis=1,
    )
    grad_resid_norm, grad_gain_moe = rms_backward(residual, inverse_two, gain_moe, grad_moe_in)
    grad_residual = grad_result + grad_resid_norm
    grad_branch = grad_residual.astype(jnp.bfloat16)
    grad_out = jnp.einsum("ti,to->io", mixed_flat, grad_branch, preferred_element_type=jnp.float32)
    mixed_gradient = jnp.einsum(
        "to,io->ti", grad_branch, out_full, preferred_element_type=jnp.float32
    ).astype(jnp.bfloat16)
    mixed_gradient = mixed_gradient.reshape(
        sequence_length, KEY_VALUE_HEADS, query_groups, HEAD_SIZE
    )
    grad_queries, key_rows_gradient, value_rows_gradient = attention_backward(
        query_rows, keys_rot, value_rows, segment_row, score_scale, row_sums, mixed_gradient
    )
    grad_query_lin = (
        rotation_backward(
            grad_queries.reshape(sequence_length, QUERY_HEADS, HEAD_SIZE), cosine_table, sine_lookup
        )
        .astype(jnp.bfloat16)
        .reshape(sequence_length, QUERY_HEADS * HEAD_SIZE)
    )
    grad_key_lin = (
        rotation_backward(key_rows_gradient, cosine_table, sine_lookup)
        .astype(jnp.bfloat16)
        .reshape(sequence_length, KEY_VALUE_HEADS * HEAD_SIZE)
    )
    value_linear_gradient = value_rows_gradient.astype(jnp.bfloat16).reshape(
        sequence_length, KEY_VALUE_HEADS * HEAD_SIZE
    )
    grad_query = jnp.einsum(
        "td,tq->dq", attention_input, grad_query_lin, preferred_element_type=jnp.float32
    )
    grad_key = jnp.einsum(
        "td,tq->dq", attention_input, grad_key_lin, preferred_element_type=jnp.float32
    )
    grad_value = jnp.einsum(
        "td,tq->dq", attention_input, value_linear_gradient, preferred_element_type=jnp.float32
    )
    grad_attn_in = jnp.einsum(
        "tq,dq->td", grad_query_lin, query_full, preferred_element_type=jnp.float32
    )
    grad_attn_in = grad_attn_in + jnp.einsum(
        "tq,dq->td", grad_key_lin, key_expanded, preferred_element_type=jnp.float32
    )
    grad_attn_in = grad_attn_in + jnp.einsum(
        "tq,dq->td", value_linear_gradient, value_expanded, preferred_element_type=jnp.float32
    )
    grad_input_norm, grad_gain_attn = rms_backward(inputs, inverse_one, gain_attn, grad_attn_in)
    grad_input = (grad_residual + grad_input_norm).astype(jnp.bfloat16)
    whole = (
        lax.psum(grad_gain_attn.astype(jnp.bfloat16), "dp").astype(jnp.float32),
        lax.psum(grad_query.astype(jnp.bfloat16), "dp").astype(jnp.float32),
        lax.psum(grad_key.astype(jnp.bfloat16), "dp").astype(jnp.float32),
        lax.psum(grad_value.astype(jnp.bfloat16), "dp").astype(jnp.float32),
        lax.psum(grad_out.astype(jnp.bfloat16), "dp").astype(jnp.float32),
        lax.psum(grad_gain_moe.astype(jnp.bfloat16), "dp").astype(jnp.float32),
        lax.psum(grad_router.astype(jnp.bfloat16), "dp").astype(jnp.float32),
        lax.psum(expert_grads[0].astype(jnp.bfloat16), "dp").astype(jnp.float32),
        lax.psum(expert_grads[1].astype(jnp.bfloat16), "dp").astype(jnp.float32),
        lax.psum(expert_grads[2].astype(jnp.bfloat16), "dp").astype(jnp.float32),
    )
    shares = (
        lax.psum_scatter(
            whole[0].astype(jnp.bfloat16), "expert", scatter_dimension=0, tiled=True
        ).astype(jnp.float32),
        lax.psum_scatter(
            whole[1].astype(jnp.bfloat16), "expert", scatter_dimension=0, tiled=True
        ).astype(jnp.float32),
        lax.psum_scatter(
            whole[2].astype(jnp.bfloat16), "expert", scatter_dimension=0, tiled=True
        ).astype(jnp.float32),
        lax.psum_scatter(
            whole[3].astype(jnp.bfloat16), "expert", scatter_dimension=0, tiled=True
        ).astype(jnp.float32),
        lax.psum_scatter(
            whole[4].astype(jnp.bfloat16), "expert", scatter_dimension=0, tiled=True
        ).astype(jnp.float32),
        lax.psum_scatter(
            whole[5].astype(jnp.bfloat16), "expert", scatter_dimension=0, tiled=True
        ).astype(jnp.float32),
        lax.psum_scatter(
            whole[6].astype(jnp.bfloat16), "expert", scatter_dimension=0, tiled=True
        ).astype(jnp.float32),
    )
    totals = (
        shares[0],
        shares[1],
        shares[2],
        shares[3],
        shares[4],
        shares[5],
        shares[6],
        whole[7],
        whole[8],
        whole[9],
    )
    return (
        result,
        grad_input,
        totals[0],
        totals[1],
        totals[2],
        totals[3],
        totals[4],
        totals[5],
        totals[6],
        totals[7],
        totals[8],
        totals[9],
    )


def solution(mesh):
    in_specs = (
        P(("dp", "expert"), None),
        P(("dp", "expert"), None),
        P(("dp", "expert"), None),
        P("expert"),
        P("expert", None),
        P("expert", None),
        P("expert", None),
        P("expert", None),
        P("expert"),
        P("expert", None),
        P("expert", None, None),
        P("expert", None, None),
        P("expert", None, None),
        P(("dp", "expert"), None),
    )
    out_specs = (
        P(("dp", "expert"), None),
        P(("dp", "expert"), None),
        P("expert"),
        P("expert", None),
        P("expert", None),
        P("expert", None),
        P("expert", None),
        P("expert"),
        P("expert", None),
        P("expert", None, None),
        P("expert", None, None),
        P("expert", None, None),
    )
    return jax.shard_map(body, mesh=mesh, in_specs=in_specs, out_specs=out_specs, check_vma=False)
```

profile of v0, /device:TPU:0, one launch (start us, length us, event | category | flops | bytes accessed | tf_op | source)
XLA Modules:
  0.0 1870.7 jit_solution(18140393939801816255)
XLA Ops:
  15.4 13.5 all-gather
  59.9 28.3 %all-gather.11.cloned.1.call-done = bf16[1024,1024]{1,0:T(8,128)(2,1)} async-done(((bf16[128,1024]{1,0:T(8,128)(2,1)}), bf16[1024,1024]{1,0:T(8,128)(2,1)}) %all-gather.11.cloned.1.call-update) | async-done | bytes 2097168 | tf_op jit(solution)/shard_map/all_gather | solution.py:159
  122.8 25.7 %scatter_custom_fusion = bf16[6144,1024]{1,0:T(8,128)(2,1)} fusion(s32[4096]{0:T(1024)S(1)} %bitcast.267, bf16[]{:T(256)} %constant.44.clone.1, bf16[512,1024]{1,0:T(8,128)(2,1)S(1)} %multiply_convert_fusion), kind=kCustom, calls=%fused_computation.53 | custom fusion | bytes 13631490 | tf_op jit(solution)/shard_map/scatter | solution.py:214
  155.5 278.1 %all_gather.27 = bf16[1024,32]{0,1:T(8,128)(2,1)S(1)} all-gather(bf16[128,32]{0,1:T(8,128)(2,1)S(1)} %copy-done.53), channel_id=1, replica_groups=mesh['dp'=4,'expert'=8] {'expert'}, dimensions={0}, use_global_device_ids=true | all-gather | bytes 73728 | tf_op jit(solution)/shard_map/all_gather | solution.py:163
  435.8 27.3 %scatter_custom_fusion.1 = bf16[6144,1024]{1,0:T(8,128)(2,1)} fusion(s32[4096]{0:T(1024)S(1)} %bitcast.268, f32[4096]{0:T(1024)S(1)} %div.59, f32[512,1024]{1,0:T(8,128)S(1)} %convert_element_type.220, bf16[]{:T(256)} %constant.44.clone.1), kind=kCustom, calls=%fused_computation.49 | custom fusion | flops 8388608 | bytes 14696450 | tf_op jit(solution)/shard_map/scatter | solution.py:258
  468.6 13.6 fusion.22
  482.2 12.3 fusion.24
  494.6 247.8 %all-to-all-done.2 = bf16[8,768,1024]{2,1,0:T(8,128)(2,1)} async-done(((bf16[8,768,1024]{2,1,0:T(8,128)(2,1)}), bf16[8,768,1024]{2,1,0:T(8,128)(2,1)}, u32[]{:S(2)}, u32[]{:S(2)}) %all-to-all-start.2) | async-done | bytes 12582944 | tf_op jit(solution)/shard_map/all_to_all | solution.py:260
  742.4 25.7 %fusion.12 = (bf16[8,4,192,512]{3,2,0,1:T(8,128)(2,1)}, bf16[8,4,192,512]{3,2,0,1:T(8,128)(2,1)}, bf16[8,4,192,512]{3,2,0,1:T(8,128)(2,1)}) fusion(f32[4,8,192,512]{3,2,1,0:T(8,128)} %fusion.24, f32[4,8,192,512]{3,2,1,0:T(8,128)} %fusion.22, bf16[4,512,1024]{2,1,0:T(8,128)(2,1)} %param.26, bf16[8,4,192,1024]{3,2,1,0:T(8,128)(2,1)} %bitcast.43), kind=kOutput, calls=%fused_computation.29 | convolution fusion | flops 6489636864 | bytes 60817408 | tf_op jit(solution)/shard_map/sjcd,jfd->sjcf/dot_general | solution.py:268
  789.0 14.9 fusion.44
  803.9 19.1 %fusion.8 = bf16[8,4,192,1024]{3,2,0,1:T(8,128)(2,1)} fusion(f32[4,8,192,1024]{3,2,1,0:T(8,128)} %fusion.44, bf16[8,4,192,512]{3,2,0,1:T(8,128)(2,1)} %get-tuple-element.30, bf16[4,1024,512]{2,1,0:T(8,128)(2,1)} %param.25), kind=kOutput, calls=%fused_computation.23 | convolution fusion | flops 6455033856 | bytes 48234496 | tf_op jit(solution)/shard_map/sjcf,jdf->sjcd/dot_general | solution.py:289
  833.7 229.1 %all-to-all-done.1 = bf16[8,768,1024]{2,1,0:T(8,128)(2,1)} async-done(((bf16[8,768,1024]{2,1,0:T(8,128)(2,1)}), bf16[8,768,1024]{2,1,0:T(8,128)(2,1)}, u32[]{:S(2)}, u32[]{:S(2)}) %all-to-all-start.1) | async-done | bytes 12582944 | tf_op jit(solution)/shard_map/all_to_all | solution.py:232
  1068.2 27.0 %gather_fusion = bf16[4096,1024]{1,0:T(8,128)(2,1)} fusion(bf16[6144,1024]{1,0:T(8,128)(2,1)} %bitcast.38, s32[4096]{0:T(1024)S(1)} %broadcast_clamp_fusion), kind=kCustom, calls=%fused_computation | custom fusion | bytes 16793600 | tf_op jit(solution)/shard_map/gather | solution.py:240
  1105.5 236.4 %all-to-all-done.3 = bf16[8,768,1024]{2,1,0:T(8,128)(2,1)} async-done(((bf16[8,768,1024]{2,1,0:T(8,128)(2,1)}), bf16[8,768,1024]{2,1,0:T(8,128)(2,1)}, u32[]{:S(2)}, u32[]{:S(2)}) %all-to-all-start.3) | async-done | bytes 12582944 | tf_op jit(solution)/shard_map/all_to_all | solution.py:291
  1341.9 27.4 %gather_fusion.1 = bf16[4096,1024]{1,0:T(8,128)(2,1)} fusion(bf16[6144,1024]{1,0:T(8,128)(2,1)} %bitcast.50, s32[4096]{0:T(1024)S(1)} %broadcast_clamp_fusion), kind=kCustom, calls=%fused_computation.1 | custom fusion | bytes 16793600 | tf_op jit(solution)/shard_map/gather | solution.py:301
  1369.3 12.0 convert_reduce_fusion
  1410.6 12.5 fusion.4
  1444.7 13.0 bitcast_convert_fusion.1
  1457.7 13.0 bitcast_convert_fusion.2
  1472.2 13.9 bitcast_convert_fusion
  1486.1 25.0 %reduce-scatter.14.cloned.1.call-done = bf16[128,1024]{1,0:T(8,128)(2,1)} async-done(((bf16[1024,1024]{1,0:T(8,128)(2,1)}), bf16[128,1024]{1,0:T(8,128)(2,1)}) %reduce-scatter.14.cloned.1.call-update) | async-done | bytes 262160 | tf_op jit(solution)/shard_map/reduce_scatter | solution.py:377
  1511.0 36.8 %reduce-scatter.8.cloned.1.call-done = bf16[128,1024]{1,0:T(8,128)(2,1)} async-done(((bf16[1024,1024]{1,0:T(8,128)(2,1)}), bf16[128,1024]{1,0:T(8,128)(2,1)}) %reduce-scatter.8.cloned.1.call-update) | async-done | bytes 262160 | tf_op jit(solution)/shard_map/reduce_scatter | solution.py:368
  1557.8 14.6 all-reduce.2
  1592.4 248.2 %all-reduce.7.cloned.1.call-done = (bf16[128,1024]{1,0:T(8,128)(2,1)}, bf16[128,512]{1,0:T(8,128)(2,1)}, bf16[128,512]{1,0:T(8,128)(2,1)}, bf16[128,1024]{1,0:T(...) async-done(((bf16[128,1024]{1,0:T(8,128)(2,1)}, bf16[128,512]{1,0:T(8,128)(2,1)}, ...) | async-done | bytes 13369360 | tf_op jit(solution)/shard_map/psum | solution.py:354
  (244 shorter events, 239.3 us)
Async XLA Ops:
  7.2 44.5 %copy-start.7 = (bf16[512,1024]{1,0:T(8,128)(2,1)S(1)}, bf16[512,1024]{1,0:T(8,128)(2,1)}, u32[]{:S(2)}) copy-start(bf16[512,1024]{1,0:T(8,128)(2,1)} %param.14) | copy-start | bytes 3145732
  7.2 44.5 %all-gather.9.cloned.1.call-start = ((), (), s32[]{:S(2)}) async-start(), calls=%async_computation.10 | async-start | bytes 1179648 | tf_op jit(solution)/shard_map/all_gather | solution.py:160
  7.9 49.9 %all-gather.7.cloned.1.call-start = ((), (), s32[]{:S(2)}) async-start(), calls=%async_computation.9 | async-start | bytes 1179648 | tf_op jit(solution)/shard_map/all_gather | solution.py:161
  8.7 79.5 %all-gather.11.cloned.1.call-start = ((), (), s32[]{:S(2)}) async-start(), calls=%async_computation.11 | async-start | bytes 2359296 | tf_op jit(solution)/shard_map/all_gather | solution.py:159
  9.4 108.8 %all-gather.13.cloned.1.call-start = ((), (), s32[]{:S(2)}) async-start(), calls=%async_computation.12 | async-start | bytes 2359296 | tf_op jit(solution)/shard_map/all_gather | solution.py:162
  15.4 72.7 %copy-start.49 = (f32[512]{0:T(512)}, f32[512]{0:T(512)S(1)}, u32[]{:S(2)}) copy-start(f32[512]{0:T(512)S(1)} %get-tuple-element.50) | copy-start | bytes 6148
  29.0 59.2 %copy-start.43 = (f32[8,1,128]{2,1,0:T(1,128)}, f32[8,1,128]{2,1,0:T(1,128)S(1)}, u32[]{:S(2)}) copy-start(f32[8,1,128]{2,1,0:T(1,128)S(1)} %convert_element_type.260) | copy-start | bytes 12292
  37.8 84.1 %copy-start.39 = (f32[8,1,128]{2,1,0:T(1,128)}, f32[8,1,128]{2,1,0:T(1,128)S(1)}, u32[]{:S(2)}) copy-start(f32[8,1,128]{2,1,0:T(1,128)S(1)} %convert_element_type.261) | copy-start | bytes 12292
  38.8 52.7 %copy-start.24 = (f32[512,64]{0,1:T(8,128)}, f32[512,64]{0,1:T(8,128)S(1)}, u32[]{:S(2)}) copy-start(f32[512,64]{0,1:T(8,128)S(1)} %get-tuple-element.44) | copy-start | bytes 393220
  40.7 50.8 %copy-start.20 = (f32[512,64]{0,1:T(8,128)}, f32[512,64]{0,1:T(8,128)S(1)}, u32[]{:S(2)}) copy-start(f32[512,64]{0,1:T(8,128)S(1)} %get-tuple-element.46) | copy-start | bytes 393220
  54.2 38.0 %copy-start.12 = (bf16[512,8,64,1]{0,2,3,1:T(8,128)(2,1)}, bf16[512,8,64,1]{0,2,3,1:T(8,128)(2,1)S(1)}, u32[]{:S(2)}) copy-start(bf16[512,8,64,1]{0,2,3,1:T(8,128)(2,1)S(1)} %fusion.81) | copy-start | bytes 1572868
  59.9 48.1 %copy-start.34 = (bf16[512,512]{0,1:T(8,128)(2,1)}, bf16[512,512]{0,1:T(8,128)(2,1)S(1)}, u32[]{:S(2)}) copy-start(bf16[512,512]{0,1:T(8,128)(2,1)S(1)} %convolution_convert_fusion.5) | copy-start | bytes 1572868
  122.8 310.9 %copy-start.5 = (bf16[512,1024]{1,0:T(8,128)(2,1)}, bf16[512,1024]{1,0:T(8,128)(2,1)S(1)}, u32[]{:S(2)}) copy-start(bf16[512,1024]{1,0:T(8,128)(2,1)S(1)} %multiply_convert_fusion) | copy-start | bytes 3145732
  148.5 314.6 %all-to-all-start = ((bf16[8,768,1024]{2,1,0:T(8,128)(2,1)}), bf16[8,768,1024]{2,1,0:T(8,128)(2,1)}, u32[]{:S(2)}, u32[]{:S(2)}) async-start(bf16[8,768,1024]{2,1,0:T(8,128)(2,1)} %bitcast.237), calls=%async_computation | async-start | bytes 25165824 | tf_op jit(solution)/shard_map/all_to_all | solution.py:215
  154.0 280.2 %copy-start.37 = (s32[512,8]{0,1:T(8,128)S(1)}, s32[512,8]{0,1:T(8,128)}, u32[]{:S(2)}) copy-start(s32[512,8]{0,1:T(8,128)} %param.16) | copy-start | bytes 49156
  463.1 279.3 %all-to-all-start.2 = ((bf16[8,768,1024]{2,1,0:T(8,128)(2,1)}), bf16[8,768,1024]{2,1,0:T(8,128)(2,1)}, u32[]{:S(2)}, u32[]{:S(2)}) async-start(bf16[8,768,1024]{2,1,0:T(8,128)(2,1)} %bitcast.238), calls=%async_computation.2 | async-start | bytes 25165824 | tf_op jit(solution)/shard_map/all_to_all | solution.py:260
  783.4 279.4 %all-to-all-start.1 = ((bf16[8,768,1024]{2,1,0:T(8,128)(2,1)}), bf16[8,768,1024]{2,1,0:T(8,128)(2,1)}, u32[]{:S(2)}, u32[]{:S(2)}) async-start(bf16[8,768,1024]{2,1,0:T(8,128)(2,1)} %bitcast.239), calls=%async_computation.1 | async-start | bytes 25165824 | tf_op jit(solution)/shard_map/all_to_all | solution.py:232
  1062.8 279.2 %all-to-all-start.3 = ((bf16[8,768,1024]{2,1,0:T(8,128)(2,1)}), bf16[8,768,1024]{2,1,0:T(8,128)(2,1)}, u32[]{:S(2)}, u32[]{:S(2)}) async-start(bf16[8,768,1024]{2,1,0:T(8,128)(2,1)} %bitcast.236), calls=%async_computation.3 | async-start | bytes 25165824 | tf_op jit(solution)/shard_map/all_to_all | solution.py:291
  1068.1 417.9 %reduce-scatter.12.cloned.1.call-start = ((), (), s32[]{:S(2)}) async-start(), calls=%async_computation.15 | async-start | bytes 1179648 | tf_op jit(solution)/shard_map/reduce_scatter | solution.py:374
  1410.5 75.6 %reduce-scatter.10.cloned.1.call-start = ((), (), s32[]{:S(2)}) async-start(), calls=%async_computation.14 | async-start | bytes 1179648 | tf_op jit(solution)/shard_map/reduce_scatter | solution.py:371
  1429.7 81.3 %reduce-scatter.14.cloned.1.call-start = ((), (), s32[]{:S(2)}) async-start(), calls=%async_computation.16 | async-start | bytes 2359296 | tf_op jit(solution)/shard_map/reduce_scatter | solution.py:377
  1433.6 114.2 %reduce-scatter.8.cloned.1.call-start = ((), (), s32[]{:S(2)}) async-start(), calls=%async_computation.13 | async-start | bytes 2359296 | tf_op jit(solution)/shard_map/reduce_scatter | solution.py:368
  1444.7 135.0 %reduce-scatter.16.cloned.1.call-start = ((), (), s32[]{:S(2)}) async-start(), calls=%async_computation.17 | async-start | bytes 294912
  1471.9 368.7 %all-reduce.7.cloned.1.call-start = ((), (), s32[]{:S(2)}) async-start(), calls=%async_computation.18 | async-start | bytes 26738688 | tf_op jit(solution)/shard_map/psum | solution.py:354
  (46 other events, 365.6 us)
Sparse Core Ops, SparseCore 0:
  9.6 24.8 all-gather.8
  36.1 21.6 all-gather.6
  59.4 28.7 all-gather.10
  89.6 28.5 all-gather.12
  1410.6 31.0 reduce-scatter.11
  1443.9 30.7 reduce-scatter.9
  1477.0 34.0 reduce-scatter.13
  1513.3 34.4 reduce-scatter.7
  1550.6 29.0 reduce-scatter.15
  1585.7 254.8 all-reduce.6
where the time goes:
time: 1880 us; the launch traced here: 1870 us
  waiting for transfers between devices  1060 us (56%)
  blocking collectives  325 us (17%)
  matrix products  211 us (11%)
  other arithmetic  122 us (6%)
  local copies, waits for them, and re-layouts  109 us (6%)
  starting transfers between devices  22.8 us (1%)
    all_gather x1, blocking collectives, body(): lax.all_gather(w_router, 'expert', axis=0, tiled=True)  278 us
    psum x1, waiting for transfers between devices, body(): lax.psum(grad_query.astype(jnp.bfloat16), 'dp').astype(jnp.float32)  248 us
    all_to_all x1, waiting for transfers between devices, body(): lax.all_to_all(grad_buffer.reshape(peer_count, owned_experts * CAP, model...  248 us
    all_to_all x1, waiting for transfers between devices, body(): lax.all_to_all(grad_rows.reshape(peer_count, owned_experts * CAP, model_w...  236 us
    all_to_all x1, waiting for transfers between devices, body(): lax.all_to_all(expert_out.reshape(peer_count, owned_experts * CAP, model_...  229 us
  transfers between devices with their start and end apart: 14, of which 10 were waited for; matrix products, arithmetic and copies ran while one was open for 15% of the time, Pallas kernels for 0%

commit v1 on v0

--- a/solution.py
+++ b/solution.py
@@ -17,11 +17,11 @@
 
 
 def positions_of(segment_row):
-    sequence_length = segment_row.shape[0]
-    row_index = jnp.arange(sequence_length, dtype=jnp.int32)
-    previous = jnp.concatenate([jnp.full((1,), -1, jnp.int32), segment_row[:-1]])
-    starts = lax.cummax(jnp.where(segment_row != previous, row_index, 0), axis=0)
-    return row_index - starts
+    row_index = jnp.arange(segment_row.shape[0], dtype=jnp.int32)
+    earlier = (segment_row[:, None] == segment_row[None, :]) & (
+        row_index[None, :] < row_index[:, None]
+    )
+    return jnp.sum(earlier.astype(jnp.int32), axis=-1)
 
 
 def rope_tables(segment_row):
@@ -63,13 +63,11 @@
     return (value_rows_gradient, grad_gain)
 
 
-def slot_index(route_rows):
-    flat_routes = route_rows.reshape(-1)
-    choose = (flat_routes[:, None] == jnp.arange(EXPERTS, dtype=jnp.int32)[None, :]).astype(
-        jnp.int32
-    )
-    before = jnp.cumsum(choose, axis=0) - choose
-    return flat_routes * CAP + jnp.sum(before * choose, axis=-1)
+def masked_softmax(logits, member):
+    kept = jnp.where(member, logits, masked_score)
+    largest = jnp.max(kept, axis=-1, keepdims=True)
+    exponent = jnp.where(member, jnp.exp(kept - largest), 0.0)
+    return exponent / jnp.sum(exponent, axis=-1, keepdims=True)
 
 
 def block_scores(query_rows, keys_rot, segment_row, first_row, block_rows, score_scale):
@@ -154,27 +152,45 @@
     w_down,
     cotangent,
 ):
-    gathered = (
-        lax.all_gather(norm_attn, "expert", axis=0, tiled=True),
-        lax.all_gather(w_query, "expert", axis=0, tiled=True),
-        lax.all_gather(key_weight, "expert", axis=0, tiled=True),
-        lax.all_gather(value_weight, "expert", axis=0, tiled=True),
-        lax.all_gather(w_out, "expert", axis=0, tiled=True),
-        lax.all_gather(w_router, "expert", axis=0, tiled=True),
-        lax.all_gather(norm_moe, "expert", axis=0, tiled=True),
-    )
-    gain_attn = gathered[0].astype(jnp.float32)
-    query_full = gathered[1]
-    key_expanded = gathered[2]
-    value_expanded = gathered[3]
-    out_full = gathered[4]
-    router_full = gathered[5]
-    gain_moe = gathered[6].astype(jnp.float32)
+    own_rows = w_query.shape[0]
+    packed = jnp.concatenate(
+        [
+            w_query,
+            key_weight,
+            value_weight,
+            w_out,
+            w_router,
+            norm_attn[:, None],
+            norm_moe[:, None],
+            routes.astype(jnp.bfloat16).reshape(own_rows, -1),
+        ],
+        axis=1,
+    )
+    whole_weights = lax.all_gather(packed, "expert", axis=0, tiled=True)
+    columns = [
+        w_query.shape[1],
+        key_weight.shape[1],
+        value_weight.shape[1],
+        w_out.shape[1],
+        w_router.shape[1],
+        1,
+        1,
+    ]
+    pieces = []
+    first = 0
+    for width in columns:
+        pieces.append(whole_weights[:, first : first + width])
+        first += width
+    query_full, key_expanded, value_expanded, out_full, router_full = pieces[:5]
+    gain_attn = pieces[5][:, 0].astype(jnp.float32)
+    gain_moe = pieces[6][:, 0].astype(jnp.float32)
+    peers = lax.axis_size("expert")
+    routes_all = whole_weights[:, first:].astype(jnp.int32).reshape(peers, -1, TOP)
+    cotangent_all = lax.all_gather(cotangent, "expert", axis=0, tiled=True)
     sequence_length = hidden.shape[0]
     model_width = hidden.shape[1]
     query_groups = QUERY_HEADS // KEY_VALUE_HEADS
     score_scale = HEAD_SIZE ** (-0.5)
-    peer_count = lax.axis_size("expert")
     owned_experts = w_gate.shape[0]
     segment_row = segment_ids[0]
     cosine_table, sine_lookup = rope_tables(segment_row)
@@ -206,20 +222,34 @@
     inverse_two = rms_scale(residual)
     moe_in = (residual * inverse_two * gain_moe).astype(jnp.bfloat16)
     logits = jnp.dot(moe_in, router_full, preferred_element_type=jnp.float32)
-    choose = routes[:, :, None] == jnp.arange(EXPERTS, dtype=jnp.int32)[None, None, :]
-    chosen = jnp.sum(jnp.where(choose, logits[:, None, :], 0.0), axis=-1)
-    gate_probs = jax.nn.softmax(chosen, axis=-1)
-    flat_slot = slot_index(routes)
-    token_rows = jnp.repeat(moe_in, TOP, axis=0)
-    buffer = jnp.zeros((EXPERTS * CAP, model_width), jnp.bfloat16).at[flat_slot].set(token_rows)
-    arrived = lax.all_to_all(
-        buffer.reshape(peer_count, owned_experts * CAP, model_width),
-        "expert",
-        split_axis=0,
-        concat_axis=0,
-        tiled=True,
-    )
-    arrived = arrived.reshape(peer_count, owned_experts, CAP, model_width)
+    expert_ids = jnp.arange(EXPERTS, dtype=jnp.int32)
+    member = jnp.any(routes[:, :, None] == expert_ids[None, None, :], axis=1)
+    gate_probs = masked_softmax(logits, member)
+    moe_all = lax.all_gather(moe_in, "expert", axis=0, tiled=True)
+    logits_all = jnp.dot(moe_all, router_full, preferred_element_type=jnp.float32)
+    member_all = jnp.any(routes_all[:, :, :, None] == expert_ids, axis=2)
+    gate_all = masked_softmax(logits_all.reshape(member_all.shape), member_all)
+    first_expert = lax.axis_index("expert") * owned_experts
+    gate_own = lax.dynamic_slice_in_dim(gate_all, first_expert, owned_experts, 2)
+    member_own = lax.dynamic_slice_in_dim(member_all, first_expert, owned_experts, 2)
+    gate_own = jnp.swapaxes(gate_own, 1, 2)
+    member_own = jnp.swapaxes(member_own, 1, 2)
+    row_index = jnp.arange(sequence_length, dtype=jnp.int32)
+    before = (row_index[:, None] < row_index[None, :]).astype(jnp.bfloat16)
+    rank = jnp.einsum(
+        "sjt,tu->sju", member_own.astype(jnp.bfloat16), before, preferred_element_type=jnp.float32
+    ).astype(jnp.int32)
+    rank = jnp.where(member_own, rank, -1)
+    place = (rank[:, :, None, :] == jnp.arange(CAP, dtype=jnp.int32)[:, None]).astype(jnp.bfloat16)
+    moe_rows = moe_all.reshape(peers, sequence_length, model_width)
+    cotangent_rows = cotangent_all.reshape(peers, sequence_length, model_width)
+    arrived = jnp.einsum(
+        "sjct,std->sjcd", place, moe_rows, preferred_element_type=jnp.float32
+    ).astype(jnp.bfloat16)
+    dout_rows = jnp.einsum(
+        "sjct,std->sjcd", place, cotangent_rows, preferred_element_type=jnp.float32
+    ).astype(jnp.bfloat16)
+    gate_slot = jnp.sum(place.astype(jnp.float32) * gate_own[:, :, None, :], axis=-1)
     gate_weights, up_weights, down_weights = (w_gate, w_up, w_down)
     gate_lin = jnp.einsum(
         "sjcd,jdf->sjcf", arrived, gate_weights, preferred_element_type=jnp.float32
@@ -229,42 +259,28 @@
     expert_out = jnp.einsum(
         "sjcf,jfd->sjcd", hidden_act, down_weights, preferred_element_type=jnp.float32
     ).astype(jnp.bfloat16)
-    returned = lax.all_to_all(
-        expert_out.reshape(peer_count, owned_experts * CAP, model_width),
-        "expert",
-        split_axis=0,
-        concat_axis=0,
-        tiled=True,
-    )
-    returned = returned.reshape(EXPERTS * CAP, model_width)
-    combined = returned[flat_slot].reshape(sequence_length, TOP, model_width).astype(jnp.float32)
-    result = (residual + jnp.sum(gate_probs[:, :, None] * combined, axis=1)).astype(jnp.bfloat16)
+    weighted = (gate_slot[..., None] * expert_out).astype(jnp.bfloat16)
+    partial_out = jnp.einsum(
+        "sjct,sjcd->std", place, weighted, preferred_element_type=jnp.float32
+    ).astype(jnp.bfloat16)
+    moe_out = lax.psum_scatter(
+        partial_out.reshape(-1, model_width), "expert", scatter_dimension=0, tiled=True
+    ).astype(jnp.float32)
+    result = (residual + moe_out).astype(jnp.bfloat16)
     grad_result = cotangent.astype(jnp.float32)
-    grad_expert = (gate_probs[:, :, None] * grad_result[:, None, :]).astype(jnp.bfloat16)
-    grad_gate_probs = jnp.sum(grad_result[:, None, :] * combined, axis=-1)
+    slot_dot = jnp.sum(dout_rows.astype(jnp.float32) * expert_out, axis=-1)
+    token_dot = jnp.sum(place.astype(jnp.float32) * slot_dot[..., None], axis=2)
+    token_dot = lax.all_to_all(token_dot, "expert", split_axis=0, concat_axis=0, tiled=True)
+    grad_gate_probs = token_dot.reshape(EXPERTS, sequence_length).T
     grad_chosen = gate_probs * (
         grad_gate_probs - jnp.sum(gate_probs * grad_gate_probs, axis=-1, keepdims=True)
     )
-    grad_logits = jnp.sum(jnp.where(choose, grad_chosen[:, :, None], 0.0), axis=1).astype(
-        jnp.bfloat16
-    )
+    grad_logits = grad_chosen.astype(jnp.bfloat16)
     grad_router = jnp.einsum("td,te->de", moe_in, grad_logits, preferred_element_type=jnp.float32)
     grad_moe_in = jnp.einsum(
         "te,de->td", grad_logits, router_full, preferred_element_type=jnp.float32
     )
-    grad_buffer = (
-        jnp.zeros((EXPERTS * CAP, model_width), jnp.bfloat16)
-        .at[flat_slot]
-        .set(grad_expert.reshape(sequence_length * TOP, model_width))
-    )
-    grad_arrived = lax.all_to_all(
-        grad_buffer.reshape(peer_count, owned_experts * CAP, model_width),
-        "expert",
-        split_axis=0,
-        concat_axis=0,
-        tiled=True,
-    )
-    grad_arrived = grad_arrived.reshape(arrived.shape)
+    grad_arrived = (gate_slot[..., None] * dout_rows).astype(jnp.bfloat16)
     grad_hidden = jnp.einsum(
         "sjcd,jfd->sjcf", grad_arrived, down_weights, preferred_element_type=jnp.float32
     )
@@ -288,19 +304,14 @@
         grad_rows
         + jnp.einsum("sjcf,jdf->sjcd", grad_up_lin, up_weights, preferred_element_type=jnp.float32)
     ).astype(jnp.bfloat16)
-    grad_returned = lax.all_to_all(
-        grad_rows.reshape(peer_count, owned_experts * CAP, model_width),
-        "expert",
-        split_axis=0,
-        concat_axis=0,
-        tiled=True,
-    )
-    grad_returned = grad_returned.reshape(EXPERTS * CAP, model_width)
+    partial_grad = jnp.einsum(
+        "sjct,sjcd->std", place, grad_rows, preferred_element_type=jnp.float32
+    ).astype(jnp.bfloat16)
+    moe_grad = lax.psum_scatter(
+        partial_grad.reshape(-1, model_width), "expert", scatter_dimension=0, tiled=True
+    ).astype(jnp.float32)
     expert_grads = (grad_gate, grad_up, grad_down)
-    grad_moe_in = grad_moe_in + jnp.sum(
-        grad_returned[flat_slot].reshape(sequence_length, TOP, model_width).astype(jnp.float32),
-        axis=1,
-    )
+    grad_moe_in = grad_moe_in + moe_grad
     grad_resid_norm, grad_gain_moe = rms_backward(residual, inverse_two, gain_moe, grad_moe_in)
     grad_residual = grad_result + grad_resid_norm
     grad_branch = grad_residual.astype(jnp.bfloat16)
@@ -349,66 +360,32 @@
     )
     grad_input_norm, grad_gain_attn = rms_backward(inputs, inverse_one, gain_attn, grad_attn_in)
     grad_input = (grad_residual + grad_input_norm).astype(jnp.bfloat16)
-    whole = (
-        lax.psum(grad_gain_attn.astype(jnp.bfloat16), "dp").astype(jnp.float32),
-        lax.psum(grad_query.astype(jnp.bfloat16), "dp").astype(jnp.float32),
-        lax.psum(grad_key.astype(jnp.bfloat16), "dp").astype(jnp.float32),
-        lax.psum(grad_value.astype(jnp.bfloat16), "dp").astype(jnp.float32),
-        lax.psum(grad_out.astype(jnp.bfloat16), "dp").astype(jnp.float32),
-        lax.psum(grad_gain_moe.astype(jnp.bfloat16), "dp").astype(jnp.float32),
-        lax.psum(grad_router.astype(jnp.bfloat16), "dp").astype(jnp.float32),
-        lax.psum(expert_grads[0].astype(jnp.bfloat16), "dp").astype(jnp.float32),
-        lax.psum(expert_grads[1].astype(jnp.bfloat16), "dp").astype(jnp.float32),
-        lax.psum(expert_grads[2].astype(jnp.bfloat16), "dp").astype(jnp.float32),
-    )
-    shares = (
-        lax.psum_scatter(
-            whole[0].astype(jnp.bfloat16), "expert", scatter_dimension=0, tiled=True
-        ).astype(jnp.float32),
-        lax.psum_scatter(
-            whole[1].astype(jnp.bfloat16), "expert", scatter_dimension=0, tiled=True
-        ).astype(jnp.float32),
-        lax.psum_scatter(
-            whole[2].astype(jnp.bfloat16), "expert", scatter_dimension=0, tiled=True
-        ).astype(jnp.float32),
-        lax.psum_scatter(
-            whole[3].astype(jnp.bfloat16), "expert", scatter_dimension=0, tiled=True
-        ).astype(jnp.float32),
-        lax.psum_scatter(
-            whole[4].astype(jnp.bfloat16), "expert", scatter_dimension=0, tiled=True
-        ).astype(jnp.float32),
-        lax.psum_scatter(
-            whole[5].astype(jnp.bfloat16), "expert", scatter_dimension=0, tiled=True
-        ).astype(jnp.float32),
-        lax.psum_scatter(
-            whole[6].astype(jnp.bfloat16), "expert", scatter_dimension=0, tiled=True
-        ).astype(jnp.float32),
-    )
-    totals = (
+    small = jnp.concatenate(
+        [grad_query, grad_key, grad_value, grad_out, grad_router]
+        + [grad_gain_attn[:, None], grad_gain_moe[:, None]],
+        axis=1,
+    ).astype(jnp.bfloat16)
+    small = lax.psum_scatter(small, "expert", scatter_dimension=0, tiled=True)
+    small = lax.psum(small, "dp").astype(jnp.float32)
+    shares = []
+    first = 0
+    for width in columns:
+        shares.append(small[:, first : first + width])
+        first += width
+    big = [lax.psum(g.astype(jnp.bfloat16), "dp").astype(jnp.float32) for g in expert_grads]
+    return (
+        result,
+        grad_input,
+        shares[5][:, 0],
         shares[0],
         shares[1],
         shares[2],
         shares[3],
+        shares[6][:, 0],
         shares[4],
-        shares[5],
-        shares[6],
-        whole[7],
-        whole[8],
-        whole[9],
-    )
-    return (
-        result,
-        grad_input,
-        totals[0],
-        totals[1],
-        totals[2],
-        totals[3],
-        totals[4],
-        totals[5],
-        totals[6],
-        totals[7],
-        totals[8],
-        totals[9],
+        big[0],
+        big[1],
+        big[2],
     )
 
 

time: 1880 us -> 1020 us (0.54)
  waiting for transfers between devices: 1060 us -> 601 us
  blocking collectives: 325 us -> 0 us
  other arithmetic: 122 us -> 58.2 us
  matrix products: 211 us -> 268 us
  local copies, waits for them, and re-layouts: 109 us -> 63.6 us
  starting transfers between devices: 22.8 us -> 3.99 us
    all_to_all x4 -> x1, waiting for transfers between devices: 713 us -> 6.65 us  [body(): lax.all_to_all(token_dot, 'expert', split_axis=0, concat_axis=0, tiled=True)]
    all_gather x3 -> x0, blocking collectives: 300 us -> none  [the longest x1 278 us: body(): lax.all_gather(w_router, 'expert', axis=0, tiled=True)]
    all_gather x4 -> x3, waiting for transfers between devices: 34.3 us -> 160 us  [the longest x1 76.5 us: body(): moe_all = lax.all_gather(moe_in, 'expert', axis=0, tiled=True)]
    reduce_scatter x4 -> x2, waiting for transfers between devices: 61.7 us -> 150 us  [the longest x1 87.3 us: body(): lax.psum_scatter(partial_out.reshape(-1, model_width), 'expert', scatter_...]
    gather x2 -> x0, local copies, waits for them, and re-layouts: 54.4 us -> none  [the longest x1 27.4 us: body(): grad_returned[flat_slot].reshape(sequence_length, TOP, model_width)]
    dot_general x1 -> x6, matrix products: 19.1 us -> 69.9 us  [the longest x1 22.2 us: body(): jnp.einsum('sjct,sjcd->std', place, grad_rows, preferred_element_type=jnp...]
    concatenate x0 -> x2, local copies, waits for them, and re-layouts: none -> 30.2 us  [the longest x1 28.1 us: body(): jnp.concatenate([grad_query, grad_key, grad_value, grad_out, grad_router]...]
    scatter x1 -> x0, other arithmetic: 27.3 us -> none  [body(): grad_buffer = jnp.zeros((EXPERTS * CAP, model_width), jnp.bfloat16).at[fl...]
  transfers between devices with their start and end apart: 14 -> 8, of which waited for: 10 -> 8; matrix products, arithmetic and copies ran while one was open for 15% -> 13% of each run, Pallas kernels for 0% -> 0%
where the time goes in v1:
time: 1020 us; the launch traced here: 1010 us
  waiting for transfers between devices  601 us (59%)
  matrix products  268 us (26%)
  local copies, waits for them, and re-layouts  63.6 us (6%)
  other arithmetic  58.2 us (6%)
  between operations  15.5 us (2%)
    psum x1, waiting for transfers between devices, body(): small = lax.psum(small, 'dp').astype(jnp.float32)  251 us
    reduce_scatter x1, waiting for transfers between devices, body(): lax.psum_scatter(partial_out.reshape(-1, model_width), 'expert', scatter_...  87.3 us
    all_gather x1, waiting for transfers between devices, body(): moe_all = lax.all_gather(moe_in, 'expert', axis=0, tiled=True)  76.5 us
    all_gather x1, waiting for transfers between devices, body(): whole_weights = lax.all_gather(packed, 'expert', axis=0, tiled=True)  64.5 us
    reduce_scatter x1, waiting for transfers between devices, body(): lax.psum_scatter(partial_grad.reshape(-1, model_width), 'expert', scatter...  63.1 us
    unnamed x8, waiting for transfers between devices  33.5 us
    concatenate x1, local copies, waits for them, and re-layouts, body(): jnp.concatenate([grad_query, grad_key, grad_value, grad_out, grad_router]...  28.1 us
    unnamed x110, local copies, waits for them, and re-layouts  25.6 us
  transfers between devices with their start and end apart: 8, of which 8 were waited for; matrix products, arithmetic and copies ran while one was open for 13% of the time, Pallas kernels for 0%

profile of v1, /device:TPU:0, one launch (start us, length us, event | category | flops | bytes accessed | tf_op | source)
XLA Modules:
  0.0 1010.6 jit_solution(13708466984647233441)
XLA Ops:
  18.0 64.5 %all-gather.4.cloned.1.call-done = bf16[1024,3138]{1,0:T(8,128)(2,1)} async-done(((bf16[128,3138]{1,0:T(8,128)(2,1)}), bf16[1024,3138]{1,0:T(8,128)(2,1)}) %all-gather.4.cloned.1.call-update) | async-done | bytes 6426640 | tf_op jit(solution)/shard_map/all_gather | solution.py:169
  127.2 76.5 %all-gather.6.cloned.1.call-done = bf16[4096,1024]{1,0:T(8,128)(2,1)} async-done(((bf16[512,1024]{1,0:T(8,128)(2,1)}), bf16[4096,1024]{1,0:T(8,128)(2,1)}) %all-gather.6.cloned.1.call-update) | async-done | bytes 8388624 | tf_op jit(solution)/shard_map/all_gather | solution.py:228
  210.2 14.2 %fusion.42 = bf16[8,4,192,1024]{3,2,1,0:T(8,128)(2,1)} fusion(bf16[8,512,1024,1]{2,1,3,0:T(8,128)(2,1)} %bitcast.224, s32[8,4,512]{2,1,0:T(4,128)S(1)} %copy.113), kind=kOutput, calls=%fused_computation.60 | convolution fusion | flops 6451888128 | bytes 21037056 | tf_op jit(solution)/shard_map/sjct,std->sjcd/dot_general | solution.py:246
  224.5 12.4 %fusion.30 = f32[4,8,192,512]{3,2,1,0:T(8,128)} fusion(bf16[8,4,192,1024]{3,2,1,0:T(8,128)(2,1)} %fusion.42, bf16[4,1024,512]{2,1,0:T(8,128)(2,1)S(1)} %copy-done.41), kind=kOutput, calls=%fused_computation.50 | convolution fusion | flops 6442450944 | bytes 29360128 | tf_op jit(solution)/shard_map/sjcd,jdf->sjcf/dot_general | solution.py:254
  236.9 17.5 %fusion.17 = (bf16[8,4,192,512]{3,2,0,1:T(8,128)(2,1)}, f32[4,8,192,512]{3,2,1,0:T(8,128)}) fusion(f32[4,8,192,512]{3,2,1,0:T(8,128)} %fusion.30, bf16[4,1024,512]{2,1,0:T(8,128)(2,1)} %param.25, bf16[8,4,192,1024]{3,2,1,0:T(8,128)(2,1)} %fusion.42), kind=kOutput, calls=%fused_computation.33 | convolution fusion | flops 6461325312 | bytes 48234496 | tf_op jit(solution)/shard_map/sjcd,jdf->sjcf/dot_general | solution.py:257
  254.4 12.9 %convolution_convert_fusion = bf16[4,8,192,1024]{3,2,1,0:T(8,128)(2,1)} fusion(bf16[8,4,192,512]{3,2,0,1:T(8,128)(2,1)} %get-tuple-element.104, bf16[4,512,1024]{2,1,0:T(8,128)(2,1)} %param.26), kind=kOutput, calls=%fused_computation.61 | convolution fusion | flops 6448742400 | bytes 23068672 | tf_op jit(solution)/shard_map/sjcf,jfd->sjcd/dot_general | solution.py:259
  267.3 18.7 %all-gather.8.cloned.1.call-done = bf16[4096,1024]{1,0:T(8,128)(2,1)} async-done(((bf16[512,1024]{1,0:T(8,128)(2,1)}), bf16[4096,1024]{1,0:T(8,128)(2,1)}) %all-gather.8.cloned.1.call-update) | async-done | bytes 8388624 | tf_op jit(solution)/shard_map/all_gather | solution.py:189
  286.0 15.1 %fusion = (f32[8,4,192]{2,0,1:T(8,128)S(1)}, bf16[8,4,192,1024]{3,2,0,1:T(8,128)(2,1)}) fusion(bf16[4,8,192,1024]{3,2,1,0:T(8,128)(2,1)} %convolution_convert_fusion, bf16[8,512,1024,1]{2,1,0,3:T(8,128)(2,1)} %bitcast.257, s32[8,4,512]{2,1,0:T(4,128)S(1)} %copy.113), kind=kOutput, calls=%fused_computation.2 | convolution fusion | flops 6477047808 | bytes 33644544 | tf_op jit(solution)/shard_map/sjct,std->sjcd/dot_general | solution.py:249
  306.1 23.0 %fusion.16 = (bf16[8,4,192,512]{3,2,0,1:T(8,128)(2,1)}, bf16[8,4,192,512]{3,2,0,1:T(8,128)(2,1)}) fusion(f32[4,8,192,512]{3,2,1,0:T(8,128)} %fusion.30, f32[4,8,192,512]{3,2,1,0:T(8,128)} %get-tuple-element.105, bf16[4,512,1024]{2,1,0:T(8,128)(2,1)} %param.26, bf16[8,4,192,1024]{3,2,0,1:T(8,128)(2,1)} %get-tuple-element.107, f32[8,4,192]{2,0,1:T(8,128)S(1)} %copy.116), kind=kOutput, calls=%fused_computation.31 | convolution fusion | flops 6502219776 | bytes 54550528 | tf_op jit(solution)/shard_map/sjcd,jfd->sjcf/dot_general | solution.py:284
  329.1 15.4 %fusion.59 = f32[4,8,192,1024]{3,2,0,1:T(8,128)} fusion(bf16[8,4,192,512]{3,2,0,1:T(8,128)(2,1)} %get-tuple-element.73, bf16[4,1024,512]{2,1,0:T(8,128)(2,1)} %param.24), kind=kOutput, calls=%fused_computation.72 | convolution fusion | flops 6442450944 | bytes 35651584 | tf_op jit(solution)/shard_map/sjcf,jdf->sjcd/dot_general | solution.py:300
  344.4 22.2 %bitcast_convert_fusion = bf16[8,512,1024]{2,1,0:T(8,128)(2,1)} fusion(f32[4,8,192,1024]{3,2,0,1:T(8,128)} %fusion.59, s32[8,4,512]{2,1,0:T(4,128)S(1)} %copy.113, bf16[8,4,192,512]{3,2,0,1:T(8,128)(2,1)} %get-tuple-element.72, bf16[4,1024,512]{2,1,0:T(8,128)(2,1)} %param.25), kind=kOutput, calls=%fused_computation.12 | convolution fusion | flops 12904824832 | bytes 44105728 | tf_op jit(solution)/shard_map/sjct,sjcd->std/dot_general | solution.py:307
  366.7 12.2 %bitcast_convert_fusion.1 = bf16[8,512,1024]{2,1,0:T(8,128)(2,1)} fusion(s32[8,4,512]{2,1,0:T(4,128)S(1)} %copy.113, bf16[4,8,192,1024]{3,2,1,0:T(8,128)(2,1)} %convolution_convert_fusion, f32[8,4,192]{2,0,1:T(8,128)S(1)} %copy.116), kind=kOutput, calls=%fused_computation.13 | convolution fusion | flops 6468665344 | bytes 21061632 | tf_op jit(solution)/shard_map/sjct,sjcd->std/dot_general | solution.py:263
  392.9 63.1 %reduce-scatter.8.cloned.1.call-done = bf16[512,1024]{1,0:T(8,128)(2,1)} async-done(((bf16[4096,1024]{1,0:T(8,128)(2,1)}), bf16[512,1024]{1,0:T(8,128)(2,1)}) %reduce-scatter.8.cloned.1.call-update) | async-done | bytes 1048592 | tf_op jit(solution)/shard_map/reduce_scatter | solution.py:310
  459.4 87.3 %reduce-scatter.6.cloned.1.call-done = bf16[512,1024]{1,0:T(8,128)(2,1)} async-done(((bf16[4096,1024]{1,0:T(8,128)(2,1)}), bf16[512,1024]{1,0:T(8,128)(2,1)}) %reduce-scatter.6.cloned.1.call-update) | async-done | bytes 1048592 | tf_op jit(solution)/shard_map/reduce_scatter | solution.py:266
  555.3 13.9 %fusion.3 = (f32[8,2,512]{2,1,0:T(2,128)S(1)}, f32[8,512,512,2]{2,1,3,0:T(8,128)}) fusion(f32[8,2,512,512]{2,3,1,0:T(8,128)} %get-tuple-element.101, f32[8,2,512]{2,1,0:T(2,128)S(1)} %bitcast.248, bf16[512,8,64,1]{0,2,3,1:T(8,128)(2,1)S(1)} %bitcast.247, bf16[512,8,2,64]{0,3,2,1:T(8,128)(2,1)S(1)} %bitcast.225), kind=kOutput, calls=%fused_computation.9 | convolution fusion | flops 549445632 | bytes 35192832 | tf_op jit(solution)/shard_map/qhgd,khd->hgqk/dot_general | solution.py:118
  569.3 8.6 fusion.106
  582.5 8.6 fusion.5
  614.1 28.1 %concatenate.42 = bf16[1024,3106]{0,1:T(8,128)(2,1)} concatenate(bf16[1024,1024]{0,1:T(8,128)(2,1)} %convolution_convert_fusion.1, bf16[1024,512]{0,1:T(8,128)(2,1)S(1)} %convolution_convert_fusion.4, bf16[1024,512]{0,1:T(8,128)(2,1)} %convolution_convert_fusion.3, bf16[1024,1024]{0,1:T(8,128)(2,1)} %convolution_convert_fusion.2, bf16[1024,32]{0,1:T(8,128)(2,1)S(1)} %copy-done.25, ...), dimensions={1} | concatenate | bytes 12722176 | tf_op jit(solution)/shard_map/concatenate | solution.py:363
  642.2 9.3 copy.152
  652.3 13.1 %bitcast_convert_fusion.2 = bf16[4,512,1024]{2,1,0:T(8,128)(2,1)} fusion(bf16[8,4,192,512]{3,2,0,1:T(8,128)(2,1)} %get-tuple-element.104, bf16[8,4,192,1024]{3,2,0,1:T(8,128)(2,1)} %get-tuple-element.107, f32[8,4,192]{2,0,1:T(8,128)S(1)} %copy-done.36), kind=kOutput, calls=%fused_computation.55 | convolution fusion | flops 6463422464 | bytes 23093248 | tf_op jit(solution)/shard_map/sjcf,sjcd->jfd/dot_general | solution.py:293
  665.4 13.1 %bitcast_convert_fusion.3 = bf16[4,1024,512]{2,1,0:T(8,128)(2,1)} fusion(bf16[8,4,192,1024]{3,2,1,0:T(8,128)(2,1)} %fusion.42, bf16[8,4,192,512]{3,2,0,1:T(8,128)(2,1)} %get-tuple-element.72), kind=kOutput, calls=%fused_computation.56 | convolution fusion | flops 6444548096 | bytes 23068672 | tf_op jit(solution)/shard_map/sjcd,sjcf->jdf/dot_general | solution.py:299
  678.5 11.2 %bitcast_convert_fusion.4 = bf16[4,1024,512]{2,1,0:T(8,128)(2,1)} fusion(bf16[8,4,192,1024]{3,2,1,0:T(8,128)(2,1)} %fusion.42, bf16[8,4,192,512]{3,2,0,1:T(8,128)(2,1)S(1)} %bitcast.261), kind=kOutput, calls=%fused_computation.57 | convolution fusion | flops 6444548096 | bytes 23068672 | tf_op jit(solution)/shard_map/sjcd,sjcf->jdf/dot_general | solution.py:296
  689.7 32.7 %reduce-scatter.10.cloned.1.call-done = bf16[128,3106]{1,0:T(8,128)(2,1)} async-done(((bf16[1024,3106]{1,0:T(8,128)(2,1)}), bf16[128,3106]{1,0:T(8,128)(2,1)}) %reduce-scatter.10.cloned.1.call-update) | async-done | bytes 795152
  729.6 251.0 %all-reduce.3.cloned.1.call-done = (bf16[128,3106]{0,1:T(8,128)(2,1)}, bf16[4,1024,512]{2,1,0:T(8,128)(2,1)}, bf16[4,1024,512]{2,1,0:T(8,128)(2,1)}, bf16[4,512,1024]{2,1,0:T(8,128)(2,1)}) async-done(((bf16[128,3106]{0,1:T(8,128)(2,1)}, bf16[4,1024,512]{2,1,0:T(8,128)(2,1)}, bf16[4,1024,512]{2,1,0:T(8,128)(2,1)}, bf16[4,512,1024]{2,1,0:T(8,128)(2,1)}), (bf16[128,3106]{0,1:T(8,128)(2,1)}, ...) | async-done | bytes 13378064 | tf_op jit(solution)/shard_map/psum | solution.py:369
  (213 shorter events, 150.5 us)
Async XLA Ops:
  7.2 75.3 %all-gather.4.cloned.1.call-start = ((), (), s32[]{:S(2)}) async-start(), calls=%async_computation.4 | async-start | bytes 7372800 | tf_op jit(solution)/shard_map/all_gather | solution.py:169
  12.7 191.0 %all-gather.6.cloned.1.call-start = ((), (), s32[]{:S(2)}) async-start(), calls=%async_computation.5 | async-start | bytes 9437184 | tf_op jit(solution)/shard_map/all_gather | solution.py:228
  14.8 75.4 %copy-start.15 = (f32[512,64]{0,1:T(8,128)}, f32[512,64]{0,1:T(8,128)S(1)}, u32[]{:S(2)}) copy-start(f32[512,64]{0,1:T(8,128)S(1)} %get-tuple-element.93) | copy-start | bytes 393220
  14.8 75.4 %copy-start.17 = (f32[512,64]{0,1:T(8,128)}, f32[512,64]{0,1:T(8,128)S(1)}, u32[]{:S(2)}) copy-start(f32[512,64]{0,1:T(8,128)S(1)} %get-tuple-element.118) | copy-start | bytes 393220
  17.0 90.0 %copy-start.37 = (f32[512]{0:T(512)}, f32[512]{0:T(512)S(1)}, u32[]{:S(2)}) copy-start(f32[512]{0:T(512)S(1)} %get-tuple-element.97) | copy-start | bytes 6148
  83.9 23.1 %copy-start.31 = (f32[1024]{0:T(1024)}, f32[1024]{0:T(1024)S(1)}, u32[]{:S(2)}) copy-start(f32[1024]{0:T(1024)S(1)} %get-tuple-element.61) | copy-start | bytes 12292
  83.9 37.0 %copy-start.28 = (f32[1024]{0:T(1024)}, f32[1024]{0:T(1024)S(1)}, u32[]{:S(2)}) copy-start(f32[1024]{0:T(1024)S(1)} %get-tuple-element.60) | copy-start | bytes 12292
  122.9 163.1 %all-gather.8.cloned.1.call-start = ((), (), s32[]{:S(2)}) async-start(), calls=%async_computation.7 | async-start | bytes 9437184 | tf_op jit(solution)/shard_map/all_gather | solution.py:189
  123.6 332.4 %reduce-scatter.8.cloned.1.call-start = ((), (), s32[]{:S(2)}) async-start(), calls=%async_computation.8 | async-start | bytes 9437184 | tf_op jit(solution)/shard_map/reduce_scatter | solution.py:310
  210.2 14.2 %copy-start.41 = (bf16[4,1024,512]{2,1,0:T(8,128)(2,1)S(1)}, bf16[4,1024,512]{2,1,0:T(8,128)(2,1)}, u32[]{:S(2)}) copy-start(bf16[4,1024,512]{2,1,0:T(8,128)(2,1)} %param.24) | copy-start | bytes 12582916
  306.1 60.6 %copy-start.35 = (f32[8,4,192]{2,0,1:T(8,128)}, f32[8,4,192]{2,0,1:T(8,128)S(1)}, u32[]{:S(2)}) copy-start(f32[8,4,192]{2,0,1:T(8,128)S(1)} %copy.116) | copy-start | bytes 73732
  366.7 180.0 %reduce-scatter.6.cloned.1.call-start = ((), (), s32[]{:S(2)}) async-start(), calls=%async_computation.6 | async-start | bytes 9437184 | tf_op jit(solution)/shard_map/reduce_scatter | solution.py:266
  379.0 77.0 %copy-start.4 = (f32[512,1024]{1,0:T(8,128)S(1)}, f32[512,1024]{1,0:T(8,128)}, u32[]{:S(2)}) copy-start(f32[512,1024]{1,0:T(8,128)} %copy-done.3) | copy-start | bytes 6291460
  379.0 77.0 %copy-start.29 = (f32[1024]{0:T(1024)S(1)}, f32[1024]{0:T(1024)}, u32[]{:S(2)}) copy-start(f32[1024]{0:T(1024)} %copy-done.28) | copy-start | bytes 12292
  379.0 77.0 %copy-start.34 = (f32[512]{0:T(512)S(1)}, f32[512]{0:T(512)}, u32[]{:S(2)}) copy-start(f32[512]{0:T(512)} %copy-done.33) | copy-start | bytes 6148
  379.7 167.0 %copy-start.40 = (f32[512]{0:T(512)S(1)}, f32[512]{0:T(512)}, u32[]{:S(2)}) copy-start(f32[512]{0:T(512)} %get-tuple-element.98) | copy-start | bytes 6148
  381.6 10.3 %all-to-all-start = ((f32[8,4,512]{2,1,0:T(4,128)}), f32[8,4,512]{2,1,0:T(4,128)S(1)}, u32[]{:S(2)}, u32[]{:S(2)}) async-start(f32[8,4,512]{2,1,0:T(4,128)} %get-tuple-element.66), calls=%async_computation.1 | async-start | bytes 131072 | tf_op jit(solution)/shard_map/all_to_all | solution.py:273
  385.0 337.4 %reduce-scatter.10.cloned.1.call-start = ((), (), s32[]{:S(2)}) async-start(), calls=%async_computation.9 | async-start | bytes 7372800
  555.3 27.1 %slice-start = ((s8[16777216]{0:T(1024)(128)(4,1)}), s8[4194304]{0:T(1024)(128)(4,1)S(1)}, s32[]{:S(2)}) async-start(s8[16777216]{0:T(1024)(128)(4,1)} %bitcast.222), calls=%async_computation.11 | async-start | bytes 8388608
  555.3 27.1 %slice-start.1 = ((s8[16777216]{0:T(1024)(128)(4,1)}), s8[4194304]{0:T(1024)(128)(4,1)S(1)}, s32[]{:S(2)}) async-start(s8[16777216]{0:T(1024)(128)(4,1)} %bitcast.222), calls=%async_computation.12 | async-start | bytes 8388608
  555.3 27.1 %slice-start.2 = ((s8[16777216]{0:T(1024)(128)(4,1)}), s8[4194304]{0:T(1024)(128)(4,1)S(1)}, s32[]{:S(2)}) async-start(s8[16777216]{0:T(1024)(128)(4,1)} %bitcast.222), calls=%async_computation.13 | async-start | bytes 8388608
  569.3 13.2 %slice-start.3 = ((s8[16777216]{0:T(1024)(128)(4,1)}), s8[4194304]{0:T(1024)(128)(4,1)S(1)}, s32[]{:S(2)}) async-start(s8[16777216]{0:T(1024)(128)(4,1)} %bitcast.222), calls=%async_computation.14 | async-start | bytes 8388608
  651.6 328.9 %all-reduce.3.cloned.1.call-start = ((), (), s32[]{:S(2)}) async-start(), calls=%async_computation.10 | async-start | bytes 26759168 | tf_op jit(solution)/shard_map/psum | solution.py:369
  652.3 26.2 %slice-start.6 = ((s8[6291456]{0:T(1024)(128)(4,1)}), s8[4194304]{0:T(1024)(128)(4,1)S(1)}, s32[]{:S(2)}) async-start(s8[6291456]{0:T(1024)(128)(4,1)} %bitcast.260), calls=%async_computation.17 | async-start | bytes 8388608
  (35 other events, 138.6 us)
Sparse Core Ops, SparseCore 0:
  12.8 69.6 all-gather.3
  123.0 80.6 all-gather.5
  205.3 80.5 all-gather.7
  366.8 89.1 reduce-scatter.7
  458.7 87.9 reduce-scatter.5
  651.7 70.6 reduce-scatter.9
  727.0 253.5 all-reduce.2

commit v2 on v1

v2 whole, which is shorter than its diff:
```python
import functools

import jax
import jax.numpy as jnp
from jax import lax
from jax.experimental import pallas as pl
from jax.experimental.pallas import tpu as pltpu
from jax.sharding import PartitionSpec as P

EXPERTS = 32
TOP = 8
CAP = 192
HALF = 32
ROWS = 256
MISC = 16
F32 = jnp.float32
BF = jnp.bfloat16
COST = pl.CostEstimate(flops=1 << 20, bytes_accessed=1 << 20, transcendentals=0)
norm_eps = 1e-06
rope_base = 10000.0


def dot(a,b,ca=1,cb=0):
    return lax.dot_general(a,b,(((ca,),(cb,)),((),())),preferred_element_type=F32)

def step_kernel(aliased, *refs):
    (first_ref, x0_ref, x1_ref, d0_ref, d1_ref, r_ref, m_ref, rank_ref, key_ref,
     wg_ref, wu_ref, wd_ref) = refs[:12]
    (g0_ref, g1_ref, o0_ref, o1_ref, dot_ref, xs_ref, ge_ref, hs_ref, dgs_ref, dus_ref,
     t_s, gate_s, rg_s, ro_s) = refs[12 + aliased:]
    owned = gate_s.shape[0]
    E = m_ref.shape[1]
    T = x0_ref.shape[0]
    e = pl.program_id(0)
    x_refs = (x0_ref, x1_ref)
    d_refs = (d0_ref, d1_ref)

    @pl.when(e == 0)
    def _():
        for q in range(2):
            t_s[...] = dot(x_refs[q][...], r_ref[...]).T
            mem = m_ref[q] > 0.5
            kept = jnp.where(mem, t_s[:E, :], -1e30)
            ex = jnp.where(mem, jnp.exp(kept - jnp.max(kept, axis=0, keepdims=True)), 0.0)
            t_s[:E, :] = ex / jnp.sum(ex, axis=0, keepdims=True)
            for j in range(owned):
                gate_s[j, q] = t_s[pl.ds(first_ref[0] + j, 1), :]

    slot = lax.broadcasted_iota(jnp.int32, (CAP, T), 0)
    gs = []
    hits = []
    ds = []
    for q in range(2):
        rows = slice(q * CAP, (q + 1) * CAP)
        hit = slot == rank_ref[0, q]
        S = jnp.where(hit, 1.0, 0.0).astype(BF)
        xs_ref[0, rows, :] = dot(S, x_refs[q][...]).astype(BF)
        d = dot(S, d_refs[q][...])
        g = jnp.sum(jnp.where(hit, gate_s[e, q], 0.0), axis=1, keepdims=True)
        ge_ref[0, rows, :] = (g * d).astype(BF)
        gs.append(g)
        hits.append(hit)
        ds.append(d.astype(BF))
    x = xs_ref[0]
    gl = dot(x, wg_ref[0])
    ul = dot(x, wu_ref[0])
    sg = jax.nn.sigmoid(gl)
    act = gl * sg
    h = (act * ul).astype(BF)
    hs_ref[0] = h
    eo = dot(h, wd_ref[0]).astype(BF)
    for q in range(2):
        part = eo[q * CAP : (q + 1) * CAP].astype(F32)
        ro_s[q, pl.ds(pl.multiple_of(e * CAP, CAP), CAP), :] = (gs[q] * part).astype(BF)
        sd = jnp.sum(part * ds[q].astype(F32), axis=1, keepdims=True)
        dot_ref[0, q] = jnp.sum(jnp.where(hits[q], sd, 0.0), axis=0, keepdims=True)
    dh = dot(ge_ref[0], wd_ref[0], 1, 1)
    dgl = (dh * ul * sg * (1.0 + gl * (1.0 - sg))).astype(BF)
    dul = (dh * act).astype(BF)
    dgs_ref[0] = dgl
    dus_ref[0] = dul
    dr = (dot(dgl, wg_ref[0], 1, 1) + dot(dul, wu_ref[0], 1, 1)).astype(BF)
    for q in range(2):
        rg_s[q, pl.ds(pl.multiple_of(e * CAP, CAP), CAP), :] = dr[q * CAP : (q + 1) * CAP]

    @pl.when(e == owned - 1)
    def _():
        lane = lax.broadcasted_iota(jnp.int32, (T, owned * CAP), 1)
        for q, g_ref, o_ref in ((0, g0_ref, o0_ref), (1, g1_ref, o1_ref)):
            keys = key_ref[q]
            hit = lane == keys[:, 0:1]
            for j in range(1, owned):
                hit = hit | (lane == keys[:, j : j + 1])
            S = jnp.where(hit, 1.0, 0.0).astype(BF)
            g_ref[...] = dot(S, rg_s[q]).astype(BF)
            o_ref[...] = dot(S, ro_s[q]).astype(BF)


def expert_step(k, first, x, d, router, member, rank, keys, wg, wu, wd, kept):
    owned, peers, _, T = rank.shape
    D, F = wg.shape[1:]
    E = member.shape[1]
    M = 2 * CAP
    rows = peers * CAP
    full = lambda e, f: (0, 0)
    shapes = [
        jax.ShapeDtypeStruct((owned, rows, D), BF),
        jax.ShapeDtypeStruct((owned, rows, D), BF),
    ] + [jax.ShapeDtypeStruct((owned, rows, F), BF)] * 3
    token = jax.ShapeDtypeStruct((T, D), BF)
    aliased = 0 if kept is None else len(shapes)
    return pl.pallas_call(
        functools.partial(step_kernel, aliased),
        grid_spec=pltpu.PrefetchScalarGridSpec(
            num_scalar_prefetch=1,
            grid=(owned,),
            in_specs=[pl.BlockSpec((T, D), full)] * 4
            + [
                pl.BlockSpec((D, 128), lambda e, f: (0, D // 128)),
                pl.BlockSpec((2, E, T), lambda e, f: (k, 0, 0)),
                pl.BlockSpec((1, 2, 1, T), lambda e, f: (e, k, 0, 0)),
                pl.BlockSpec((2, T, owned), lambda e, f: (k, 0, 0)),
                pl.BlockSpec((1, D, F), lambda e, f: (e, 0, 0)),
                pl.BlockSpec((1, D, F), lambda e, f: (e, 0, 0)),
                pl.BlockSpec((1, F, D), lambda e, f: (e, 0, 0)),
            ]
            + [pl.BlockSpec(memory_space=pl.ANY)] * aliased,
            out_specs=[pl.BlockSpec((T, D), full)] * 4
            + [pl.BlockSpec((1, 2, 1, T), lambda e, f: (e, 0, 0, 0))]
            + [pl.BlockSpec((1, M, s.shape[2]), lambda e, f: (e, k, 0)) for s in shapes],
            scratch_shapes=[
                pltpu.VMEM((128, T), F32),
                pltpu.VMEM((owned, 2, 1, T), F32),
                pltpu.VMEM((2, owned * CAP, D), BF),
                pltpu.VMEM((2, owned * CAP, D), BF),
            ],
        ),
        out_shape=[token] * 4 + [jax.ShapeDtypeStruct((owned, 2, 1, T), F32)] + shapes,
        input_output_aliases={12 + i: 5 + i for i in range(aliased)},
        compiler_params=pltpu.CompilerParams(vmem_limit_bytes=60 << 20),
        cost_estimate=COST,
        name="expert_step",
    )(first, *x, *d, router, member, rank, keys, wg, wu, wd, *(kept or ()))


def weight_kernel(parts, bit_ref, xs_ref, ge_ref, hs_ref, dgs_ref, dus_ref, send_ref, keep_ref, *acc):
    at = pl.program_id(1)
    half = xs_ref.shape[2] // 2
    for n, o_ref in enumerate((send_ref, keep_ref)):
        bit = 1 - bit_ref[0] if n == 0 else bit_ref[0]
        off = pl.multiple_of(bit * half, half)
        x = xs_ref[0, :, pl.ds(off, half)]
        totals = (
            dot(x, dgs_ref[0], 0, 0),
            dot(x, dus_ref[0], 0, 0),
            dot(hs_ref[0], ge_ref[0, :, pl.ds(off, half)], 0, 0),
        )
        for i, total in enumerate(totals):
            if parts > 1:
                s = acc[0].at[3 * n + i]
                total = jnp.where(at == 0, 0.0, s[...]) + total
                s[...] = total
            o_ref[0, i] = total.astype(BF)


def weight_grads(bit, first, count, kept):
    rows, D = kept[0].shape[1:]
    F = kept[2].shape[2]
    half = D // 2
    assert half == F
    block = min(rows, 8 * CAP)
    parts = rows // block
    out = jax.ShapeDtypeStruct((count, 3, half, F), BF)
    return pl.pallas_call(
        functools.partial(weight_kernel, parts),
        grid_spec=pltpu.PrefetchScalarGridSpec(
            num_scalar_prefetch=1,
            grid=(count, parts),
            in_specs=[
                pl.BlockSpec((1, block, s.shape[2]), lambda e, i, b: (first + e, i, 0)) for s in kept
            ],
            out_specs=[pl.BlockSpec((1, 3, half, F), lambda e, i, b: (e, 0, 0, 0))] * 2,
            scratch_shapes=[pltpu.VMEM((6, half, F), F32)] if parts > 1 else [],
        ),
        out_shape=[out, out],
        compiler_params=pltpu.CompilerParams(vmem_limit_bytes=60 << 20),
        cost_estimate=COST,
        name="weight_grads",
    )(bit, *kept)


def halve_kernel(bit_ref, keep_ref, got_ref, send_ref, kept_ref):
    half = send_ref.shape[2]
    for n, o_ref in enumerate((send_ref, kept_ref)):
        bit = 1 - bit_ref[0] if n == 0 else bit_ref[0]
        rows = pl.ds(pl.multiple_of(bit * half, half), half)
        for i in range(keep_ref.shape[1]):
            o_ref[0, i] = (
                keep_ref[0, i, rows, :].astype(F32) + got_ref[0, i, rows, :].astype(F32)
            ).astype(BF)


def halve(bit, keep, got):
    count, mats, rows, F = keep.shape
    full = pl.BlockSpec((1, mats, rows, F), lambda e, b: (e, 0, 0, 0))
    part = pl.BlockSpec((1, mats, rows // 2, F), lambda e, b: (e, 0, 0, 0))
    out = jax.ShapeDtypeStruct((count, mats, rows // 2, F), BF)
    return pl.pallas_call(
        halve_kernel,
        grid_spec=pltpu.PrefetchScalarGridSpec(
            num_scalar_prefetch=1, grid=(count,), in_specs=[full, full], out_specs=[part, part]
        ),
        out_shape=[out, out],
        cost_estimate=COST,
        name="halve",
    )(bit, keep, got)


def place_kernel(bits_ref, q_ref, *refs):
    for i, o_ref in enumerate(refs[-3:]):
        o_ref[0] = q_ref[0, i].astype(F32)


def place_quarter(first, owned, bits, quarter, held):
    count, _, rows, F = quarter.shape
    D = 4 * rows
    shapes = [(owned, D, F), (owned, D, F), (owned, F, D)]
    tall = pl.BlockSpec((1, rows, F), lambda e, b: (first + e, 2 * b[0] + b[1], 0))
    wide = pl.BlockSpec((1, rows, F), lambda e, b: (first + e, b[1], b[0]))
    aliased = 0 if held is None else 3
    return pl.pallas_call(
        place_kernel,
        grid_spec=pltpu.PrefetchScalarGridSpec(
            num_scalar_prefetch=1,
            grid=(count,),
            in_specs=[pl.BlockSpec((1, 3, rows, F), lambda e, b: (e, 0, 0, 0))]
            + [pl.BlockSpec(memory_space=pl.ANY)] * aliased,
            out_specs=[tall, tall, wide],
        ),
        out_shape=[jax.ShapeDtypeStruct(s, F32) for s in shapes],
        input_output_aliases={2 + i: i for i in range(aliased)},
        cost_estimate=COST,
        name="place_quarter",
    )(bits, quarter, *(held or ()))


def assemble_kernel(place,p_ref,*refs):
    ins=refs[:-2]; o_ref,sem=refs[-2:]
    copies=[]
    for n,r in enumerate(ins):
        chips,sub,_=r.shape
        for k in range(chips):
            row=pl.multiple_of(p_ref[n*chips+k]*sub,sub)
            copies.append(pltpu.make_async_copy(r.at[k],o_ref.at[pl.ds(row,sub),:],sem.at[n*chips+k]))
    for c in copies: c.start()
    for c in copies: c.wait()

def assemble(places,pieces):
    n=len(pieces); chips,sub,W=pieces[0].shape
    return pl.pallas_call(functools.partial(assemble_kernel,None),
        grid_spec=pltpu.PrefetchScalarGridSpec(num_scalar_prefetch=1,grid=(1,),
          in_specs=[pl.BlockSpec(memory_space=pl.ANY)]*n,
          out_specs=pl.BlockSpec((n*chips*sub,W),lambda i,p:(0,0)),
          scratch_shapes=[pltpu.SemaphoreType.DMA((n*chips,))]),
        out_shape=jax.ShapeDtypeStruct((n*chips*sub,W),BF),cost_estimate=COST,
        compiler_params=pltpu.CompilerParams(vmem_limit_bytes=40<<20),
        name="assemble")(places,*pieces)

def ring_steps(v):
    n=lax.axis_size("expert")
    ring=[(i,(i+2)%n) for i in range(n)]
    blocks=[v]
    for _ in range(n//2-1):
        blocks.append(lax.ppermute(blocks[-1],"expert",ring))
    return blocks

def swap_pair(v):
    return lax.ppermute(v,"expert",[(i,i^1) for i in range(lax.axis_size("expert"))])

def swap_dp(v,r):
    return lax.ppermute(v,"dp",[(i,i^r) for i in range(lax.axis_size("dp"))])

def shift_chips(v,k):
    n=lax.axis_size("expert")
    return lax.ppermute(v,"expert",[(i,(i+2*k)%n) for i in range(n)])

def ring_gather(v):
    blocks=[]
    for b in ring_steps(v):
        blocks+=[b,swap_pair(b)]
    return blocks

def send_back(v,k,b):
    n=lax.axis_size("expert")
    return lax.ppermute(v,"expert",[(i,((i//2-k)%(n//2))*2+((i%2)^b)) for i in range(n)]) if k or b else v

def all_shifts(v):
    return [v]+[shift_chips(v,k) for k in range(1,lax.axis_size("expert")//2)]

def share_kernel(rows_ref, *refs):
    o_ref = refs[-1]
    for r, piece in enumerate(refs[:-1]):
        sub = piece.shape[0]
        row = pl.multiple_of(rows_ref[r], sub)
        o_ref[pl.ds(row, sub), :] = piece[...].astype(F32)


def place_share(rows, pieces):
    sub, W = pieces[0].shape
    n = len(pieces)
    return pl.pallas_call(
        share_kernel,
        grid_spec=pltpu.PrefetchScalarGridSpec(
            num_scalar_prefetch=1,
            grid=(1,),
            in_specs=[pl.BlockSpec((sub, W), lambda i, r: (0, 0))] * n,
            out_specs=pl.BlockSpec((n * sub, W), lambda i, r: (0, 0)),
        ),
        out_shape=jax.ShapeDtypeStruct((n * sub, W), F32),
        cost_estimate=COST,
        name="place_share",
    )(rows, *pieces)


def own_slice(pack):
    dp=lax.axis_size("dp")
    sub=pack.shape[0]//dp
    return lax.dynamic_slice_in_dim(pack,lax.axis_index("dp")*sub,sub,0)

def tie(*values):
    return lax.optimization_barrier(values)

def rotate(v):
    lane=lax.broadcasted_iota(jnp.int32,v.shape,1)
    width=v.shape[1]
    return jnp.where(lane%(2*HALF)<HALF,pltpu.roll(v,width-HALF,1),pltpu.roll(v,HALF,1))

def spread(v):
    lane=lax.broadcasted_iota(jnp.int32,v.shape,1)
    low=lane<2*HALF
    other=pltpu.roll(v,2*HALF,1)
    zero=jnp.zeros_like(v)
    return [jnp.where(low,v,zero).astype(BF),jnp.where(low,zero,other).astype(BF),
            jnp.where(low,other,zero).astype(BF),jnp.where(low,zero,v).astype(BF)]

def gain_row(misc_ref,which):
    return misc_ref[...].astype(F32).T[which:which+1,:]

def attend_kernel(gain_at,h_ref,misc_ref,wq_ref,wk_ref,wv_ref,cos_ref,sin_ref,segc_ref,segr_ref,
                  q_ref,k_ref,v_ref,mix_ref,lse_ref,x_s,bias_s):
    T=h_ref.shape[0]
    @pl.when(pl.program_id(0)==0)
    def _():
        inputs=h_ref[...].astype(F32)
        inv=lax.rsqrt(jnp.mean(inputs*inputs,axis=-1,keepdims=True)+norm_eps)
        x_s[...]=(inputs*inv*gain_row(misc_ref,gain_at)).astype(BF)
        r=lax.broadcasted_iota(jnp.int32,(T,T),0); c=lax.broadcasted_iota(jnp.int32,(T,T),1)
        bias_s[...]=jnp.where((segc_ref[...]==segr_ref[...])&(c<=r),0.0,-1e30)
    x=x_s[...]
    cos=cos_ref[...]; sin=sin_ref[...]
    ql=dot(x,wq_ref[...])
    qs=[]
    for c in range(2):
        part=ql[:,128*c:128*c+128]
        part=part*cos+rotate(part)*sin
        q_ref[:,128*c:128*c+128]=part.astype(BF)
        qs.append((part.astype(BF).astype(F32)*0.125).astype(BF))
    kl=dot(x,wk_ref[...])
    kl=(kl*cos+rotate(kl)*sin).astype(BF)
    k_ref[...]=kl
    vl=dot(x,wv_ref[...]).astype(BF)
    v_ref[...]=vl
    kp=spread(kl.astype(F32)); vp=spread(vl.astype(F32))
    lane=lax.broadcasted_iota(jnp.int32,(ROWS,128),1)
    for b in range(T//ROWS):
        rows=slice(b*ROWS,(b+1)*ROWS); nk=(b+1)*ROWS
        lse=jnp.zeros((ROWS,128),F32)
        for c in range(2):
            o=None
            for half in range(2):
                i=2*c+half
                s=dot(qs[c][rows],kp[i][:nk],1,1)+bias_s[rows,:nk]
                m=jnp.max(s,axis=1,keepdims=True)
                e=jnp.exp(s-m)
                l=jnp.sum(e,axis=1,keepdims=True)
                p=(e*(1.0/l)).astype(BF)
                part=dot(p,vp[i][:nk])
                o=part if o is None else o+part
                lse=jnp.where(lane==i,m+jnp.log(l),lse)
            mix_ref[rows,128*c:128*c+128]=o.astype(BF)
        lse_ref[0,:,rows]=lse.T[:8,:]

def attend(gain_at,h,w,cos,sin,segc,segr,kv_heads):
    T,D=h.shape
    steps=kv_heads//2
    full=lambda g:(0,0)
    qb=D//256; kb=D//128; vb=kb+kv_heads//2; mb=vb+kv_heads//2
    return pl.pallas_call(functools.partial(attend_kernel,gain_at),grid=(steps,),
        in_specs=[pl.BlockSpec((T,D),full),pl.BlockSpec((D,128),lambda g:(0,mb)),
                  pl.BlockSpec((D,256),lambda g:(0,g)),pl.BlockSpec((D,128),lambda g:(0,kb+g)),pl.BlockSpec((D,128),lambda g:(0,vb+g)),
                  pl.BlockSpec((T,128),full),pl.BlockSpec((T,128),full),pl.BlockSpec((T,1),full),pl.BlockSpec((1,T),full)],
        out_specs=[pl.BlockSpec((T,256),lambda g:(0,g)),pl.BlockSpec((T,128),lambda g:(0,g)),pl.BlockSpec((T,128),lambda g:(0,g)),
                   pl.BlockSpec((T,256),lambda g:(0,g)),pl.BlockSpec((1,8,T),lambda g:(g,0,0))],
        out_shape=[jax.ShapeDtypeStruct((T,D),BF),jax.ShapeDtypeStruct((T,64*kv_heads),BF),jax.ShapeDtypeStruct((T,64*kv_heads),BF),
                   jax.ShapeDtypeStruct((T,D),BF),jax.ShapeDtypeStruct((steps,8,T),F32)],
        scratch_shapes=[pltpu.VMEM((T,D),BF),pltpu.VMEM((T,T),F32)],
        cost_estimate=COST,
        name="attend")(h,w,w,w,w,cos,sin,segc,segr)


def project_kernel(gain_at,m_ref,w_ref,h_ref,misc_ref,res_ref,moe_ref):
    res=h_ref[...].astype(F32)+dot(m_ref[...],w_ref[...])
    res_ref[...]=res
    inv=lax.rsqrt(jnp.mean(res*res,axis=-1,keepdims=True)+norm_eps)
    moe_ref[...]=(res*inv*gain_row(misc_ref,gain_at)).astype(BF)

def project(gain_at,mixed,w2,h,w1):
    T,D=h.shape
    R=256
    return pl.pallas_call(functools.partial(project_kernel,gain_at),grid=(T//R,),
        in_specs=[pl.BlockSpec((R,D),lambda i:(i,0)),pl.BlockSpec((D,D),lambda i:(0,0)),pl.BlockSpec((R,D),lambda i:(i,0)),
                  pl.BlockSpec((D,128),lambda i:(0,MISC))],
        out_specs=[pl.BlockSpec((R,D),lambda i:(i,0)),pl.BlockSpec((R,D),lambda i:(i,0))],
        out_shape=[jax.ShapeDtypeStruct((T,D),F32),jax.ShapeDtypeStruct((T,D),BF)],
        cost_estimate=COST,
        name="project")(mixed,w2,h,w1)

def branch_kernel(gain_at,mg_ref,res_ref,moe_ref,mix_ref,cot_ref,wo_ref,r_ref,misc_ref,mem_ref,td_ref,
                  dres_ref,dmix_ref,out_ref,t_s):
    T,D=res_ref.shape
    E=mem_ref.shape[0]
    t_s[...]=dot(moe_ref[...],r_ref[...]).T
    mem=mem_ref[...]>0.5
    kept=jnp.where(mem,t_s[:E,:],-1e30)
    e=jnp.where(mem,jnp.exp(kept-jnp.max(kept,axis=0,keepdims=True)),0.0)
    g=e/jnp.sum(e,axis=0,keepdims=True)
    td=td_ref[...]
    t_s[...]=jnp.zeros_like(t_s)
    t_s[:E,:]=g*(td-jnp.sum(g*td,axis=0,keepdims=True))
    gl=t_s[...].T.astype(BF)
    dmoe=dot(gl,r_ref[...],1,1)+mg_ref[...].astype(F32)
    res=res_ref[...]
    inv=lax.rsqrt(jnp.mean(res*res,axis=-1,keepdims=True)+norm_eps)
    gain=gain_row(misc_ref,gain_at)
    scaled=dmoe*gain
    grad_gain=jnp.sum(dmoe*res*inv,axis=0,keepdims=True)
    dres=cot_ref[...].astype(F32)+inv*scaled-res*(inv*inv*inv*jnp.mean(scaled*res,axis=-1,keepdims=True))
    dres_ref[...]=dres
    br=dres.astype(BF)
    dmix_ref[...]=dot(br,wo_ref[...],1,1).astype(BF)
    out_ref[:,:D]=dot(mix_ref[...],br,0,0).astype(BF)
    lane=lax.broadcasted_iota(jnp.int32,(D,128),1)
    column=jnp.broadcast_to(grad_gain,(128,D)).T
    out_ref[:,D:]=jnp.where(lane==E,column,dot(moe_ref[...],gl,0,0)).astype(BF)

def branch(gain_at,mg,res,moe_in,mixed,cot,w2,w1,mem_t,td):
    T,D=res.shape
    E=mem_t.shape[0]
    full=lambda i:(0,0)
    return pl.pallas_call(functools.partial(branch_kernel,gain_at),grid=(1,),
        in_specs=[pl.BlockSpec((T,D),full)]*5+[pl.BlockSpec((D,D),full),pl.BlockSpec((D,128),lambda i:(0,D//128)),
                  pl.BlockSpec((D,128),lambda i:(0,MISC)),pl.BlockSpec((E,T),full),pl.BlockSpec((E,T),full)],
        out_specs=[pl.BlockSpec((T,D),full),pl.BlockSpec((T,D),full),pl.BlockSpec((D,D+128),full)],
        out_shape=[jax.ShapeDtypeStruct((T,D),F32),jax.ShapeDtypeStruct((T,D),BF),jax.ShapeDtypeStruct((D,D+128),BF)],
        scratch_shapes=[pltpu.VMEM((128,T),F32)],
        compiler_params=pltpu.CompilerParams(vmem_limit_bytes=60<<20),
        cost_estimate=COST,
        name="branch")(mg,res,moe_in,mixed,cot,w2,w2,w1,mem_t,td)

def fold(v):
    return v+pltpu.roll(v,2*HALF,1)

def attend_back_kernel(gain_at,h_ref,misc_ref,wq_ref,wk_ref,wv_ref,cos_ref,sin_ref,segc_ref,segr_ref,
                       q_ref,k_ref,v_ref,dm_ref,lse_ref,dres_ref,og_ref,
                       out_ref,gin_ref,x_s,bias_s,da_s):
    T,D=h_ref.shape
    step=pl.program_id(0)
    @pl.when(step==0)
    def _():
        inputs=h_ref[...].astype(F32)
        inv=lax.rsqrt(jnp.mean(inputs*inputs,axis=-1,keepdims=True)+norm_eps)
        x_s[...]=(inputs*inv*gain_row(misc_ref,gain_at)).astype(BF)
        r=lax.broadcasted_iota(jnp.int32,(T,T),0); c=lax.broadcasted_iota(jnp.int32,(T,T),1)
        bias_s[...]=jnp.where((segc_ref[...]==segr_ref[...])&(r<=c),0.0,-1e30)
        wide=og_ref.shape[1]
        out_ref[:,out_ref.shape[1]-128-wide:out_ref.shape[1]-128]=og_ref[...]
    cos=cos_ref[...]; sin=sin_ref[...]
    kp=spread(k_ref[...].astype(F32)); vp=spread(v_ref[...].astype(F32))
    low=lax.broadcasted_iota(jnp.int32,(T,128),1)<2*HALF
    dq_all=[];dk_all=[];dv_all=[]
    for c in range(2):
        cols=slice(128*c,128*c+128)
        qs=(q_ref[:,cols].astype(F32)*0.125).astype(BF)
        dm=dm_ref[:,cols]
        dks=[];dvs=[];dq=[None]*(T//ROWS)
        for half in range(2):
            i=2*c+half
            dk=None;dv=None
            for b in reversed(range(T//ROWS)):
                rows=slice(b*ROWS,(b+1)*ROWS); nk=(b+1)*ROWS
                s=dot(kp[i][:nk],qs[rows],1,1)+bias_s[:nk,rows]
                p=jnp.exp(s-lse_ref[0,i:i+1,rows])
                dp=dot(vp[i][:nk],dm[rows],1,1)
                delta=jnp.sum(p*dp,axis=0,keepdims=True)
                ds=(p*(dp-delta)).astype(BF)
                part=dot(ds,kp[i][:nk],0,0)
                dq[b]=part if dq[b] is None else dq[b]+part
                pk=dot(ds,qs[rows]); pv=dot(p.astype(BF),dm[rows])
                if dk is None:
                    dk,dv=pk,pv
                else:
                    dk=jnp.concatenate([dk[:nk]+pk,dk[nk:]],axis=0)
                    dv=jnp.concatenate([dv[:nk]+pv,dv[nk:]],axis=0)
            dks.append(dk);dvs.append(dv)
        dql=jnp.concatenate(dq,axis=0)*0.125
        dq_all.append((dql*cos-rotate(dql)*sin).astype(BF))
        dk_all.append(fold(jnp.where(low,dks[0],dks[1])))
        dv_all.append(fold(jnp.where(low,dvs[0],dvs[1])))
    dkl=jnp.where(low,dk_all[0],dk_all[1])
    dkl=(dkl*cos-rotate(dkl)*sin).astype(BF)
    dvl=jnp.where(low,dv_all[0],dv_all[1]).astype(BF)
    dql=jnp.concatenate(dq_all,axis=1)
    x=x_s[...]
    base=pl.multiple_of(step*512,512)
    out_ref[:,pl.ds(base,256)]=dot(x,dql,0,0).astype(BF)
    out_ref[:,pl.ds(base+256,128)]=dot(x,dkl,0,0).astype(BF)
    out_ref[:,pl.ds(base+384,128)]=dot(x,dvl,0,0).astype(BF)
    da=dot(dql,wq_ref[...],1,1)+dot(dkl,wk_ref[...],1,1)+dot(dvl,wv_ref[...],1,1)
    @pl.when(step==0)
    def _():
        da_s[...]=da
    @pl.when(step>0)
    def _():
        da_s[...]+=da
    @pl.when(step==pl.num_programs(0)-1)
    def _():
        inputs=h_ref[...].astype(F32)
        inv=lax.rsqrt(jnp.mean(inputs*inputs,axis=-1,keepdims=True)+norm_eps)
        dattn=da_s[...]
        scaled=dattn*gain_row(misc_ref,gain_at)
        grad_gain=jnp.sum(dattn*inputs*inv,axis=0,keepdims=True)
        gin_ref[...]=(dres_ref[...]+inv*scaled-inputs*(inv*inv*inv*jnp.mean(scaled*inputs,axis=-1,keepdims=True))).astype(BF)
        out_ref[:,out_ref.shape[1]-128:]=jnp.broadcast_to(grad_gain,(128,D)).T.astype(BF)

def attend_back(gain_at,h,w,cos,sin,segc,segr,q,k,v,dmix,lse,dres,og):
    T,D=h.shape
    kvw=k.shape[1]
    steps=lse.shape[0]
    full=lambda g:(0,0)
    kb=D//128; vb=kb+kvw//128
    wide=og.shape[1]
    width=D+2*kvw+wide+128
    return pl.pallas_call(functools.partial(attend_back_kernel,gain_at),grid=(steps,),
        in_specs=[pl.BlockSpec((T,D),full),pl.BlockSpec((D,128),lambda g:(0,MISC)),
                  pl.BlockSpec((D,256),lambda g:(0,g)),pl.BlockSpec((D,128),lambda g:(0,kb+g)),pl.BlockSpec((D,128),lambda g:(0,vb+g)),
                  pl.BlockSpec((T,128),full),pl.BlockSpec((T,128),full),pl.BlockSpec((T,1),full),pl.BlockSpec((1,T),full),
                  pl.BlockSpec((T,256),lambda g:(0,g)),pl.BlockSpec((T,128),lambda g:(0,g)),pl.BlockSpec((T,128),lambda g:(0,g)),
                  pl.BlockSpec((T,256),lambda g:(0,g)),pl.BlockSpec((1,8,T),lambda g:(g,0,0)),pl.BlockSpec((T,D),full),pl.BlockSpec((D,wide),full)],
        out_specs=[pl.BlockSpec((D,width),full),pl.BlockSpec((T,D),full)],
        out_shape=[jax.ShapeDtypeStruct((D,width),BF),jax.ShapeDtypeStruct((T,D),BF)],
        scratch_shapes=[pltpu.VMEM((T,D),BF),pltpu.VMEM((T,T),F32),pltpu.VMEM((T,D),F32)],
        compiler_params=pltpu.CompilerParams(vmem_limit_bytes=60<<20),
        cost_estimate=COST,
        name="attend_back")(h,w,w,w,w,cos,sin,segc,segr,q,k,v,dmix,lse,dres,og)

def rope_tables(segment_row):
    index = jnp.arange(segment_row.shape[0], dtype=jnp.int32)
    earlier = (segment_row[:, None] == segment_row[None, :]) & (index[None, :] < index[:, None])
    position = jnp.sum(earlier.astype(jnp.int32), axis=-1).astype(F32)
    frequency = rope_base ** (-jnp.arange(HALF, dtype=F32) / HALF)
    angles = position[:, None] * frequency[None, :]
    cosine = jnp.cos(angles)
    sine = jnp.sin(angles)
    return (
        jnp.concatenate([cosine] * 4, axis=1),
        jnp.concatenate([-sine, sine, -sine, sine], axis=1),
    )


def pad_columns(values):
    return jnp.pad(values, ((0, 0), (0, -values.shape[1] % 128)))


def body(
    hidden,
    segment_ids,
    routes,
    norm_attn,
    w_query,
    key_weight,
    value_weight,
    w_out,
    norm_moe,
    w_router,
    w_gate,
    w_up,
    w_down,
    cotangent,
):
    tokens, width = hidden.shape
    own_rows = w_query.shape[0]
    owned = w_gate.shape[0]
    peers = lax.axis_size("expert")
    me = lax.axis_index("expert")
    chips = peers // 2
    chip_order = (me // 2 - jnp.arange(chips, dtype=jnp.int32)) % chips
    core_order = (me % 2) ^ jnp.arange(2, dtype=jnp.int32)
    order = (chip_order[:, None] * 2 + core_order[None, :]).reshape(-1)
    dp_count = lax.axis_size("dp")
    dp_order = lax.axis_index("dp") ^ jnp.arange(dp_count, dtype=jnp.int32)
    places = (
        (chip_order[None, None, :] * 2 + core_order[None, :, None]) * dp_count
        + dp_order[:, None, None]
    ).reshape(-1)
    first_pack = pad_columns(
        jnp.concatenate(
            [
                w_query,
                key_weight,
                value_weight,
                norm_attn[:, None],
                norm_moe[:, None],
            ],
            axis=1,
        )
    )
    second_pack = pad_columns(jnp.concatenate([w_out, w_router], axis=1))
    cotangent_steps = [cotangent]
    routes_shifts = all_shifts(routes.astype(BF).reshape(-1, 128))
    shifts_one = all_shifts(own_slice(first_pack))
    shifts_one, routes_shifts, second_slice, cotangent_steps = tie(
        shifts_one, routes_shifts, own_slice(second_pack), cotangent_steps
    )
    shifts_two = all_shifts(second_slice)
    stack_one = jnp.stack(shifts_one)
    slices_one = [stack_one] + [swap_dp(stack_one, r) for r in range(1, dp_count)]
    cotangent_steps.append(shift_chips(cotangent_steps[0], 1))
    routes_all = []
    for s in routes_shifts:
        routes_all += [s, swap_pair(s)]
    routes_all = jnp.stack(routes_all).astype(jnp.int32).reshape(peers, tokens, TOP)
    expert_ids = jnp.arange(EXPERTS, dtype=jnp.int32)
    member_all = jnp.any(routes_all[:, None, :, :] == expert_ids[:, None, None], axis=3)
    first_expert = me * owned
    member_own = lax.dynamic_slice_in_dim(member_all, first_expert, owned, 1)
    index = jnp.arange(tokens, dtype=jnp.int32)
    before = (index[:, None] < index[None, :]).astype(BF)
    rank = jnp.einsum(
        "sjt,tu->sju", member_own.astype(BF), before, preferred_element_type=F32
    ).astype(jnp.int32)
    rank = jnp.where(member_own, rank, -1)
    first_slot = jnp.arange(owned, dtype=jnp.int32)[:, None] * CAP
    keys = jnp.swapaxes(jnp.where(member_own, rank + first_slot, -1), 1, 2)
    rank_rows = jnp.swapaxes(rank, 0, 1)[:, :, None, :]
    member_all = member_all.astype(F32)
    member_line = jnp.any(routes[None, :, :] == expert_ids[:, None, None], axis=2).astype(F32)
    segment_row = segment_ids[0]
    cosine, sine = rope_tables(segment_row)
    segment_column = segment_row[:, None]
    segment_line = segment_row[None, :]
    from_chip = (me // 2 + jnp.arange(chips, dtype=jnp.int32)) % chips
    from_order = (from_chip[:, None] * 2 + core_order[None, :]).reshape(-1)
    from_order = jnp.argsort(from_order)
    tables = [rank_rows, keys, member_all, member_line, cosine, sine, from_order]
    tables, slices_one, shifts_two = tie(tables, slices_one, shifts_two)
    rank_rows, keys, member_all, member_line, cosine, sine, from_order = tables
    pieces_one = []
    for s in slices_one:
        pieces_one += [s, swap_pair(s)]
    pieces_one, shifts_two, cotangent_steps = tie(pieces_one, shifts_two, cotangent_steps)
    for k in range(2, min(chips, 3)):
        cotangent_steps.append(shift_chips(cotangent_steps[k - 1], 1))
    stack_two = jnp.stack(shifts_two)
    slices_two = [stack_two] + [swap_dp(stack_two, r) for r in range(1, dp_count)]
    attn_weights = assemble(places, pieces_one)
    attn_weights, slices_two, cotangent_steps = tie(attn_weights, slices_two, cotangent_steps)
    pieces_two = []
    for s in slices_two:
        pieces_two += [s, swap_pair(s)]
    for k in range(3, chips):
        cotangent_steps.append(shift_chips(cotangent_steps[k - 1], 1))
    cotangent_pairs = [swap_pair(c) for c in cotangent_steps[: chips - 1]]
    kv_heads = key_weight.shape[1] // (2 * HALF)
    query, key, value, mixed, lse = attend(
        0, hidden, attn_weights, cosine, sine, segment_column, segment_line, kv_heads
    )
    mixed, pieces_two, cotangent_steps, cotangent_pairs = tie(
        mixed, pieces_two, cotangent_steps, cotangent_pairs
    )
    out_weights = assemble(places, pieces_two)
    residual, moe_in = project(1, mixed, out_weights, hidden, attn_weights)
    cotangent_pairs.append(swap_pair(cotangent_steps[-1]))
    x = [moe_in, swap_pair(moe_in)]
    x, moe_in = tie(x, moe_in)
    kept = None
    dots = []
    grad_parts = []
    out_parts = []
    hop = None
    for k in range(chips):
        following = shift_chips(x[0], 1) if k + 1 < chips else None
        if k == 3:
            hop = shift_chips(grad_parts[1], 1)
        outs = list(
            expert_step(
                k,
                first_expert[None],
                x,
                (cotangent_steps[k], cotangent_pairs[k]),
                out_weights,
                member_all,
                rank_rows,
                keys,
                w_gate,
                w_up,
                w_down,
                kept,
            )
        )
        kept = outs[5:]
        outs = outs[:5]
        outs, kept, following, hop, dots, grad_parts, out_parts = tie(
            outs, kept, following, hop, dots, grad_parts, out_parts
        )
        if following is not None:
            x = [following, swap_pair(following)]
        grad_part = (outs[0].astype(F32) + swap_pair(outs[1]).astype(F32)).astype(BF)
        out_parts = out_parts + [(outs[2], outs[3])]
        dots = dots + [outs[4]]
        if k + 1 < chips:
            x, grad_part = tie(x, grad_part)
        grad_parts = grad_parts + [grad_part]
    dp_me = lax.axis_index("dp")
    low = dp_me % 2
    high = dp_me // 2
    count = (owned + 1) // 2
    plans = [(0, count, 1, 2, low, high)]
    if owned > count:
        plans.append((count, owned - count, 2, 1, high, low))
    returned = [send_back(dots[k][:, b, 0], k, b) for k in range(chips) for b in range(2)]
    total = grad_parts[1]
    first_hop = 2
    if hop is not None:
        total, kept = tie((grad_parts[2].astype(F32) + hop.astype(F32)).astype(BF), kept)
        first_hop = 3
    halves = []
    gots = []
    for number, k in enumerate(range(first_hop, chips + 1)):
        moved = shift_chips(total, 1)
        if number < len(plans):
            first_of, many, one, two, bit_one, bit_two = plans[number]
            send, keep = weight_grads(bit_one[None], first_of, many, kept)
            halves.append((first_of, one, two, bit_one, bit_two, keep))
            moved, send, kept = tie(moved, send, kept)
            gots.append(swap_dp(send, one))
        if k < chips:
            total = (grad_parts[k].astype(F32) + moved.astype(F32)).astype(BF)
            total, kept = tie(total, kept)
    moe_grad = (grad_parts[0].astype(F32) + moved.astype(F32)).astype(BF)
    moe_grad, returned, out_parts = tie(moe_grad, returned, out_parts)
    out_parts = [(a.astype(F32) + swap_pair(b).astype(F32)).astype(BF) for a, b in out_parts]
    token_dot = jnp.stack(returned)[from_order].reshape(EXPERTS, tokens)
    grad_residual, mixed_gradient, out_grads = branch(
        1, moe_grad, residual, moe_in, mixed, cotangent, out_weights, attn_weights, member_line, token_dot
    )
    mixed_gradient, out_parts = tie(mixed_gradient, out_parts)
    out_sum = shift_chips(out_parts[1], 1)
    attn_grads, grad_input = attend_back(
        0,
        hidden,
        attn_weights,
        cosine,
        sine,
        segment_column,
        segment_line,
        query,
        key,
        value,
        mixed_gradient,
        lse,
        grad_residual,
        out_grads,
    )
    attn_grads, out_sum, gots = tie(attn_grads, out_sum, gots)

    def block_for(k, b):
        number = chip_order[k] * 2 + core_order[b]
        return lax.dynamic_slice_in_dim(attn_grads, number * own_rows, own_rows, 0)

    seconds = []
    keeps = []
    for (first_of, one, two, bit_one, bit_two, keep), got in zip(halves, gots):
        send, keep = halve(bit_two[None], keep, got)
        seconds.append(send)
        keeps.append(keep)
    parts = [(block_for(k, 0), swap_pair(block_for(k, 1))) for k in range(chips)]
    out_sum = (out_parts[2].astype(F32) + out_sum.astype(F32)).astype(BF)
    seconds, keeps, parts, out_sum = tie(seconds, keeps, parts, out_sum)
    parts = [(a.astype(F32) + b.astype(F32)).astype(BF) for a, b in parts]
    gots = [swap_dp(send, h[2]) for h, send in zip(halves, seconds)]
    running = shift_chips(parts[1], 1)
    gots, running = tie(gots, running)
    mine = [(k.astype(F32) + g.astype(F32)).astype(BF) for k, g in zip(keeps, gots)]
    running = (parts[2].astype(F32) + running.astype(F32)).astype(BF)
    mine, running, out_sum = tie(mine, running, out_sum)
    others = [swap_dp(m, h[2]) for h, m in zip(halves, mine)]
    running = shift_chips(running, 1)
    others, running, mine = tie(others, running, mine)
    thirds = [swap_dp(m, h[1]) for h, m in zip(halves, mine)]
    out_sum = shift_chips(out_sum, 1)
    for k in [*range(3, chips), 0]:
        running = (parts[k].astype(F32) + running.astype(F32)).astype(BF)
        if k:
            running = shift_chips(running, 1)
    part, thirds, others, mine, out_sum = tie(running, thirds, others, mine, out_sum)
    for o in out_parts[3:]:
        out_sum = shift_chips((o.astype(F32) + out_sum.astype(F32)).astype(BF), 1)
    result = (residual + out_parts[0].astype(F32) + out_sum.astype(F32)).astype(BF)
    sub = own_rows // dp_count

    def rows_of(r):
        return (dp_me ^ r) * sub

    fourths = [swap_dp(o, h[1]) for h, o in zip(halves, others)]
    sent = [lax.dynamic_slice_in_dim(part, rows_of(r), sub, 0) for r in range(dp_count)]
    received = [sent[0]] + [swap_dp(sent[r], r) for r in range(1, dp_count)]
    held = None
    for (first_of, one, two, bit_one, bit_two, _), m, other, third in zip(
        halves, mine, others, thirds
    ):
        held = place_quarter(first_of, owned, jnp.stack([bit_one, bit_two]), m, held)
        held = place_quarter(first_of, owned, jnp.stack([bit_one, 1 - bit_two]), other, held)
        held = place_quarter(first_of, owned, jnp.stack([1 - bit_one, bit_two]), third, held)
    held, received = tie(held, received)
    total = received[0].astype(F32)
    for piece in received[1:]:
        total = total + piece.astype(F32)
    total = total.astype(BF)
    pieces = [swap_dp(total, r) if r else total for r in range(dp_count)]
    for (first_of, one, two, bit_one, bit_two, _), fourth in zip(halves, fourths):
        held = place_quarter(first_of, owned, jnp.stack([1 - bit_one, 1 - bit_two]), fourth, held)
    big = held
    share = place_share(jnp.stack([rows_of(r) for r in range(dp_count)]), pieces)
    groups = share[:, : 2 * width].reshape(own_rows, -1, 512)
    out_share = share[:, 2 * width :]
    return (
        result,
        grad_input,
        share[:, -128],
        groups[:, :, :256].reshape(own_rows, -1),
        groups[:, :, 256:384].reshape(own_rows, -1),
        groups[:, :, 384:].reshape(own_rows, -1),
        out_share[:, :width],
        out_share[:, width + EXPERTS],
        out_share[:, width : width + EXPERTS],
        big[0],
        big[1],
        big[2],
    )


def solution(mesh):
    in_specs = (
        P(("dp", "expert"), None),
        P(("dp", "expert"), None),
        P(("dp", "expert"), None),
        P("expert"),
        P("expert", None),
        P("expert", None),
        P("expert", None),
        P("expert", None),
        P("expert"),
        P("expert", None),
        P("expert", None, None),
        P("expert", None, None),
        P("expert", None, None),
        P(("dp", "expert"), None),
    )
    out_specs = (
        P(("dp", "expert"), None),
        P(("dp", "expert"), None),
        P("expert"),
        P("expert", None),
        P("expert", None),
        P("expert", None),
        P("expert", None),
        P("expert"),
        P("expert", None),
        P("expert", None, None),
        P("expert", None, None),
        P("expert", None, None),
    )
    return jax.shard_map(body, mesh=mesh, in_specs=in_specs, out_specs=out_specs, check_vma=False)
```

time: 1020 us -> 638 us (0.63)
  waiting for transfers between devices: 601 us -> 205 us
  matrix products: 268 us -> 3.06 us
  Pallas kernels: 0 us -> 258 us
  starting transfers between devices: 3.99 us -> 67.3 us
  local copies, waits for them, and re-layouts: 63.6 us -> 41.5 us
  other arithmetic: 58.2 us -> 46 us
    dot_general x35 -> x1, matrix products: 268 us -> 3.06 us  [body(): jnp.einsum('sjt,tu->sju', member_own.astype(BF), before, preferred_elemen...]
    pallas_call x0 -> x23, Pallas kernels: none -> 258 us  [the longest x4 110 us: expert_step(): pl.pallas_call(functools.partial(step_kernel, aliased), grid_spec=pltpu.P...]
    psum x1 -> x0, waiting for transfers between devices: 251 us -> none  [body(): small = lax.psum(small, 'dp').astype(jnp.float32)]
    ppermute x0 -> x85, waiting for transfers between devices: none -> 205 us  [the longest x24 133 us: shift_chips(): return lax.ppermute(v, 'expert', [(i, (i + 2 * k) % n) for i in range(n)])]
    all_gather x3 -> x0, waiting for transfers between devices: 160 us -> none  [the longest x1 76.5 us: body(): moe_all = lax.all_gather(moe_in, 'expert', axis=0, tiled=True)]
    reduce_scatter x2 -> x0, waiting for transfers between devices: 150 us -> none  [the longest x1 87.3 us: body(): lax.psum_scatter(partial_out.reshape(-1, model_width), 'expert', scatter_...]
    ppermute x0 -> x85, starting transfers between devices: none -> 67.3 us  [the longest x24 28.9 us: shift_chips(): return lax.ppermute(v, 'expert', [(i, (i + 2 * k) % n) for i in range(n)])]
    unnamed x8 -> x0, waiting for transfers between devices: 33.5 us -> none
  transfers between devices with their start and end apart: 8 -> 85, of which waited for: 8 -> 34; matrix products, arithmetic and copies ran while one was open for 13% -> 9% of each run, Pallas kernels for 0% -> 39%
where the time goes in v2:
time: 638 us; the launch traced here: 630 us
  Pallas kernels  258 us (40%)
  waiting for transfers between devices  205 us (32%)
  starting transfers between devices  67.3 us (11%)
  other arithmetic  46 us (7%)
  local copies, waits for them, and re-layouts  41.5 us (7%)
  between operations  9.36 us (1%)
    ppermute x24, waiting for transfers between devices, shift_chips(): return lax.ppermute(v, 'expert', [(i, (i + 2 * k) % n) for i in range(n)])  133 us
    pallas_call x4, Pallas kernels, expert_step(): pl.pallas_call(functools.partial(step_kernel, aliased), grid_spec=pltpu.P...  110 us
    ppermute x22, waiting for transfers between devices, swap_dp(): lax.ppermute(v, 'dp', [(i, i ^ r) for i in range(lax.axis_size('dp'))])  53.2 us
    pallas_call x1, Pallas kernels, attend_back(): pl.pallas_call(functools.partial(attend_back_kernel, gain_at), grid=(step...  32.9 us
    pallas_call x2, Pallas kernels, weight_grads(): pl.pallas_call(functools.partial(weight_kernel, parts), grid_spec=pltpu.P...  31.4 us
    ppermute x24, starting transfers between devices, shift_chips(): return lax.ppermute(v, 'expert', [(i, (i + 2 * k) % n) for i in range(n)])  28.9 us
    pallas_call x8, Pallas kernels, place_quarter(): pl.pallas_call(place_kernel, grid_spec=pltpu.PrefetchScalarGridSpec(num_s...  28.4 us
    ppermute x22, starting transfers between devices, swap_dp(): lax.ppermute(v, 'dp', [(i, i ^ r) for i in range(lax.axis_size('dp'))])  24.2 us
  transfers between devices with their start and end apart: 85, of which 34 were waited for; matrix products, arithmetic and copies ran while one was open for 9% of the time, Pallas kernels for 39%

profile of v2, /device:TPU:0, one launch (start us, length us, event | category | flops | bytes accessed | tf_op | source)
XLA Modules:
  0.0 629.9 jit_solution(14331684867872039992)
XLA Ops:
  38.7 21.9 %collective-permute-done.14 = bf16[32,1152]{1,0:T(8,128)(2,1)S(1)} collective-permute-done((bf16[32,1152]{1,0:T(8,128)(2,1)S(1)}, bf16[32,1152]{1,0:T(8,128)(2,1)S(1)}, u32[]{:S(2)}, u32[]{:S(2)}) %collective-permute-start.14) | collective-permute-done | bytes 73760 | tf_op jit(solution)/shard_map/ppermute | solution.py:285
  79.7 7.6 %assemble.2.misc_ref.wq_ref.wk_ref.wv_ref = bf16[1024,2176]{1,0:T(8,128)(2,1)S(1)} custom-call(s32[32]{0:T(128)S(1)} %add.264.p_ref, bf16[4,32,2176]{2,1,0:T(8,128)(2,1)S(1)} %pad_maximum_fusion.refs_0_, bf16[4,32,2176]{2,1,0:T(8,128)(2,1)S(1)} %collective-permute-done.16.refs_1_, bf16[4,32,2176]{2,1,0:T(8,128)(2,1)S(1)} %collective-permute-done.10.refs_2_, ...), custom_call_target="tpu_custom_call" | custom-call | flops 1048576 | bytes 1048576 | tf_op jit(solution)/shard_map/assemble/pallas_call | solution.py:260
  89.5 9.5 %collective-permute-done.24.refs_3_ = bf16[512,1024]{1,0:T(8,128)(2,1)} collective-permute-done((bf16[512,1024]{1,0:T(8,128)(2,1)}, bf16[512,1024]{1,0:T(8,128)(2,1)}, u32[]{:S(2)}, u32[]{:S(2)}) %collective-permute-start.24) | collective-permute-done | bytes 1048608 | tf_op jit(solution)/shard_map/ppermute | solution.py:285
  107.7 17.2 %attend.1 = (bf16[512,1024]{1,0:T(8,128)(2,1)}, bf16[512,512]{1,0:T(8,128)(2,1)}, bf16[512,512]{1,0:T(8,128)(2,1)}, bf16[512,1024]{1,0:T(8,128)(2,1)}, f32[4,8,512]{2,1,0:T(8,128)}) custom-call(bf16[512,1024]{1,0:T(8,128)(2,1)} %h_ref.5, bf16[1024,2176]{1,0:T(8,128)(2,1)} %copy-done, bf16[1024,2176]{1,0:T(8,128)(2,1)} %copy-done, ...), custom_call_target="tpu_custom_call" | custom-call | flops 1048576 | bytes 1048576 | tf_op jit(solution)/shard_map/attend/pallas_call | solution.py:398
  133.6 4.9 project.1
  142.8 27.5 %expert_step.4 = (bf16[512,1024]{1,0:T(8,128)(2,1)}, bf16[512,1024]{1,0:T(8,128)(2,1)}, bf16[512,1024]{1,0:T(8,128)(2,1)}, bf16[512,1024]{1,0:T(8,128)(2,1)}, f3...) custom-call(s32[1]{0:T(128)} %bitcast.16.refs_0_, ...), custom_call_target="tpu_custom_call" | custom-call | flops 1048576 | bytes 1048576 | tf_op jit(solution)/shard_map/expert_step/pallas_call | solution.py:112
  175.2 27.5 %expert_step.5 = (bf16[512,1024]{1,0:T(8,128)(2,1)}, bf16[512,1024]{1,0:T(8,128)(2,1)}, bf16[512,1024]{1,0:T(8,128)(2,1)}, bf16[512,1024]{1,0:T(8,128)(2,1)}, f3...) custom-call(s32[1]{0:T(128)} %bitcast.16.refs_0_, ...), custom_call_target="tpu_custom_call", output_to_operand_aliasing={{5}: (12, {}), {6}: (13, {}), {7}: (14, {}), {8}: (15, {}),... | custom-call | flops 1048576 | bytes 1048576 | tf_op jit(solution)/shard_map/expert_step/pallas_call | solution.py:112
  213.1 27.5 %expert_step.6 = (bf16[512,1024]{1,0:T(8,128)(2,1)}, bf16[512,1024]{1,0:T(8,128)(2,1)}, bf16[512,1024]{1,0:T(8,128)(2,1)}, bf16[512,1024]{1,0:T(8,128)(2,1)}, f3...) custom-call(s32[1]{0:T(128)} %bitcast.16.refs_0_, ...), custom_call_target="tpu_custom_call", output_to_operand_aliasing={{5}: (12, {}), {6}: (13, {}), {7}: (14, {}), {8}: (15, {}),... | custom-call | flops 1048576 | bytes 1048576 | tf_op jit(solution)/shard_map/expert_step/pallas_call | solution.py:112
  246.5 27.5 %expert_step.7 = (bf16[512,1024]{1,0:T(8,128)(2,1)}, bf16[512,1024]{1,0:T(8,128)(2,1)}, bf16[512,1024]{1,0:T(8,128)(2,1)}, bf16[512,1024]{1,0:T(8,128)(2,1)}, f3...) custom-call(s32[1]{0:T(128)} %bitcast.16.refs_0_, ...), custom_call_target="tpu_custom_call", output_to_operand_aliasing={{5}: (12, {}), {6}: (13, {}), {7}: (14, {}), {8}: (15, {}),... | custom-call | flops 1048576 | bytes 1048576 | tf_op jit(solution)/shard_map/expert_step/pallas_call | solution.py:112
  278.7 15.8 %weight_grads.2 = (bf16[2,3,512,512]{3,2,1,0:T(8,128)(2,1)}, bf16[2,3,512,512]{3,2,1,0:T(8,128)(2,1)}) custom-call(s32[1]{0:T(128)} %bitcast.17.bit_ref, bf16[4,1536,1024]{2,1,0:T(8,128)(2,1)} %get-tuple-element.511.xs_ref, bf16[4,1536,1024]{2,1,0:T(8,128)(2,1)} %get-tuple-element.512.ge_ref, bf16[4,1536,512]{2,1,0:T(8,128)(2,1)} %get-tuple-element.513.hs_ref, ...), custom_call_target="tpu_custom_call" | custom-call | flops 1048576 | bytes 1048576 | tf_op jit(solution)/shard_map/weight_grads/pallas_call | solution.py:174
  294.5 8.8 %collective-permute-done.46 = bf16[512,1024]{1,0:T(8,128)(2,1)} collective-permute-done((bf16[512,1024]{1,0:T(8,128)(2,1)S(1)}, bf16[512,1024]{1,0:T(8,128)(2,1)}, u32[]{:S(2)}, u32[]{:S(2)}) %collective-permute-start.46) | collective-permute-done | bytes 1048608 | tf_op jit(solution)/shard_map/ppermute | solution.py:285
  310.0 15.6 %weight_grads.3 = (bf16[2,3,512,512]{3,2,1,0:T(8,128)(2,1)}, bf16[2,3,512,512]{3,2,1,0:T(8,128)(2,1)}) custom-call(s32[1]{0:T(128)} %bitcast.18.bit_ref, bf16[4,1536,1024]{2,1,0:T(8,128)(2,1)} %get-tuple-element.511.xs_ref, bf16[4,1536,1024]{2,1,0:T(8,128)(2,1)} %get-tuple-element.512.ge_ref, bf16[4,1536,512]{2,1,0:T(8,128)(2,1)} %get-tuple-element.513.hs_ref, ...), custom_call_target="tpu_custom_call" | custom-call | flops 1048576 | bytes 1048576 | tf_op jit(solution)/shard_map/weight_grads/pallas_call | solution.py:174
  325.6 6.7 %collective-permute-done.47 = bf16[512,1024]{1,0:T(8,128)(2,1)S(1)} collective-permute-done((bf16[512,1024]{1,0:T(8,128)(2,1)S(1)}, bf16[512,1024]{1,0:T(8,128)(2,1)S(1)}, u32[]{:S(2)}, u32[]{:S(2)}) %collective-permute-start.47) | collective-permute-done | bytes 1048608 | tf_op jit(solution)/shard_map/ppermute | solution.py:285
  343.2 9.6 %branch.1 = (f32[512,1024]{1,0:T(8,128)}, bf16[512,1024]{1,0:T(8,128)(2,1)}, bf16[1024,1152]{1,0:T(8,128)(2,1)}) custom-call(bf16[512,1024]{1,0:T(8,128)(2,1)} %add_convert_fusion.9.mg_ref, f32[512,1024]{1,0:T(8,128)} %get-tuple-element.379.res_ref, bf16[512,1024]{1,0:T(8,128)(2,1)} %get-tuple-element.531.refs_1_.moe_ref, ...), custom_call_target="tpu_custom_call" | custom-call | flops 1048576 | bytes 1048576 | tf_op jit(solution)/shard_map/branch/pallas_call | solution.py:460
  369.7 32.9 %attend_back.1 = (bf16[1024,3328]{1,0:T(8,128)(2,1)}, bf16[512,1024]{1,0:T(8,128)(2,1)}) custom-call(bf16[512,1024]{1,0:T(8,128)(2,1)} %h_ref.5, bf16[1024,2176]{1,0:T(8,128)(2,1)} %copy-done, bf16[1024,2176]{1,0:T(8,128)(2,1)} %copy-done, bf16[1024,2176]{1,0:T(8,128)(2,1)} %copy-done, bf16[1024,2176]{1,0:T(8,128)(2,1)} %copy-done, ...), custom_call_target="tpu_custom_call" | custom-call | flops 1048576 | bytes 1048576 | tf_op jit(solution)/shard_map/attend_back/pallas_call | solution.py:553
  409.7 5.6 constant_dynamic-slice_fusion.4
  430.8 21.5 %collective-permute-done.68 = bf16[128,3328]{1,0:T(8,128)(2,1)S(1)} collective-permute-done((bf16[128,3328]{1,0:T(8,128)(2,1)S(1)}, bf16[128,3328]{1,0:T(8,128)(2,1)S(1)}, u32[]{:S(2)}, u32[]{:S(2)}) %collective-permute-start.68) | collective-permute-done | bytes 852000 | tf_op jit(solution)/shard_map/ppermute | solution.py:285
  452.3 10.6 %collective-permute-done.66 = bf16[2,3,256,512]{3,2,1,0:T(8,128)(2,1)S(1)} collective-permute-done((bf16[2,3,256,512]{3,2,1,0:T(8,128)(2,1)}, bf16[2,3,256,512]{3,2,1,0:T(8,128)(2,1)S(1)}, u32[]{:S(2)}, u32[]{:S(2)}) %collective-permute-start.66) | collective-permute-done | bytes 1572896 | tf_op jit(solution)/shard_map/ppermute | solution.py:281
  470.5 20.7 %collective-permute-done.71 = bf16[128,3328]{1,0:T(8,128)(2,1)S(1)} collective-permute-done((bf16[128,3328]{1,0:T(8,128)(2,1)S(1)}, bf16[128,3328]{1,0:T(8,128)(2,1)S(1)}, u32[]{:S(2)}, u32[]{:S(2)}) %collective-permute-start.71) | collective-permute-done | bytes 852000 | tf_op jit(solution)/shard_map/ppermute | solution.py:285
  491.2 12.3 %collective-permute-done.69.q_ref = bf16[2,3,256,512]{3,2,1,0:T(8,128)(2,1)} collective-permute-done((bf16[2,3,256,512]{3,2,1,0:T(8,128)(2,1)S(1)}, bf16[2,3,256,512]{3,2,1,0:T(8,128)(2,1)}, u32[]{:S(2)}, u32[]{:S(2)}) %collective-permute-start.69) | collective-permute-done | bytes 1572896 | tf_op jit(solution)/shard_map/ppermute | solution.py:281
  511.5 19.0 %collective-permute-done.72 = bf16[128,3328]{1,0:T(8,128)(2,1)} collective-permute-done((bf16[128,3328]{1,0:T(8,128)(2,1)}, bf16[128,3328]{1,0:T(8,128)(2,1)}, u32[]{:S(2)}, u32[]{:S(2)}) %collective-permute-start.72) | collective-permute-done | bytes 852000 | tf_op jit(solution)/shard_map/ppermute | solution.py:285
  532.4 17.4 %collective-permute-done.75 = bf16[512,1024]{1,0:T(8,128)(2,1)} collective-permute-done((bf16[512,1024]{1,0:T(8,128)(2,1)}, bf16[512,1024]{1,0:T(8,128)(2,1)}, u32[]{:S(2)}, u32[]{:S(2)}) %collective-permute-start.75) | collective-permute-done | bytes 1048608 | tf_op jit(solution)/shard_map/ppermute | solution.py:285
  582.3 16.0 %collective-permute-done.80.refs_1_ = bf16[32,3328]{1,0:T(8,128)(2,1)S(1)} collective-permute-done((bf16[32,3328]{1,0:T(8,128)(2,1)S(1)}, bf16[32,3328]{1,0:T(8,128)(2,1)S(1)}, u32[]{:S(2)}, u32[]{:S(2)}) %collective-permute-start.80) | collective-permute-done | bytes 213024 | tf_op jit(solution)/shard_map/ppermute | solution.py:281
  599.9 5.1 collective-permute-done.82.refs_3_
  (384 shorter events, 231.8 us)
Async XLA Ops:
  24.6 41.8 %collective-permute-start.10 = (bf16[4,32,2176]{2,1,0:T(8,128)(2,1)S(1)}, bf16[4,32,2176]{2,1,0:T(8,128)(2,1)S(1)}, u32[]{:S(2)}, u32[]{:S(2)}) collective-permute-start(bf16[4,32,2176]{2,1,0:T(8,128)(2,1)S(1)} %pad_maximum_fusion.refs_0_), channel_id=1, source_target_pairs={{0,8},{8,0},{16,24},{24,16},{1,9},{9,1},{17,25},{25,17},{2,10},{10... | collective-permute-start | bytes 1671176 | tf_op jit(solution)/shard_map/ppermute | solution.py:281
  26.2 40.3 %collective-permute-start.11 = (bf16[4,32,2176]{2,1,0:T(8,128)(2,1)S(1)}, bf16[4,32,2176]{2,1,0:T(8,128)(2,1)S(1)}, u32[]{:S(2)}, u32[]{:S(2)}) collective-permute-start(bf16[4,32,2176]{2,1,0:T(8,128)(2,1)S(1)} %pad_maximum_fusion.refs_0_), channel_id=1, source_target_pairs={{0,16},{8,24},{16,0},{24,8},{1,17},{9,25},{17,1},{25,9},{2,18},{10... | collective-permute-start | bytes 1671176 | tf_op jit(solution)/shard_map/ppermute | solution.py:281
  27.9 38.5 %collective-permute-start.12 = (bf16[4,32,2176]{2,1,0:T(8,128)(2,1)S(1)}, bf16[4,32,2176]{2,1,0:T(8,128)(2,1)S(1)}, u32[]{:S(2)}, u32[]{:S(2)}) collective-permute-start(bf16[4,32,2176]{2,1,0:T(8,128)(2,1)S(1)} %pad_maximum_fusion.refs_0_), channel_id=1, source_target_pairs={{0,24},{8,16},{16,8},{24,0},{1,25},{9,17},{17,9},{25,1},{2,26},{10... | collective-permute-start | bytes 1671176 | tf_op jit(solution)/shard_map/ppermute | solution.py:281
  31.4 36.2 %collective-permute-start.20 = (bf16[512,1024]{1,0:T(8,128)(2,1)}, bf16[512,1024]{1,0:T(8,128)(2,1)}, u32[]{:S(2)}, u32[]{:S(2)}) collective-permute-start(bf16[512,1024]{1,0:T(8,128)(2,1)} %cot_ref.1), channel_id=1, source_target_pairs={{0,2},{1,3},{2,4},{3,5},{4,6},{5,7},{6,0},{7,1},{8,10},{9,11},{10,... | collective-permute-start | bytes 3145736 | tf_op jit(solution)/shard_map/ppermute | solution.py:285
  141.5 28.7 %collective-permute-start.34 = (bf16[512,1024]{1,0:T(8,128)(2,1)}, bf16[512,1024]{1,0:T(8,128)(2,1)S(1)}, u32[]{:S(2)}, u32[]{:S(2)}) collective-permute-start(bf16[512,1024]{1,0:T(8,128)(2,1)} %get-tuple-element.531.refs_1_.moe_ref), channel_id=1, source_target_pairs={{0,2},{1,3},{2,4},{3,5},{4,6},{5,7},{6,0},{7,1},{8,10},{9,11},{10,... | collective-permute-start | bytes 3145736 | tf_op jit(solution)/shard_map/ppermute | solution.py:285
  175.0 28.1 %collective-permute-start.37 = (bf16[512,1024]{1,0:T(8,128)(2,1)S(1)}, bf16[512,1024]{1,0:T(8,128)(2,1)S(1)}, u32[]{:S(2)}, u32[]{:S(2)}) collective-permute-start(bf16[512,1024]{1,0:T(8,128)(2,1)S(1)} %collective-permute-done.34.refs_1_), channel_id=1, source_target_pairs={{0,2},{1,3},{2,4},{3,5},{4,6},{5,7},{6,0},{7,1},{8,10},{9,11},{10,... | collective-permute-start | bytes 3145736 | tf_op jit(solution)/shard_map/ppermute | solution.py:285
  211.0 29.6 %collective-permute-start.40 = (bf16[512,1024]{1,0:T(8,128)(2,1)S(1)}, bf16[512,1024]{1,0:T(8,128)(2,1)}, u32[]{:S(2)}, u32[]{:S(2)}) collective-permute-start(bf16[512,1024]{1,0:T(8,128)(2,1)S(1)} %collective-permute-done.37.refs_1_), channel_id=1, source_target_pairs={{0,2},{1,3},{2,4},{3,5},{4,6},{5,7},{6,0},{7,1},{8,10},{9,11},{10,... | collective-permute-start | bytes 3145736 | tf_op jit(solution)/shard_map/ppermute | solution.py:285
  241.3 32.7 %collective-permute-start.44 = (bf16[512,1024]{1,0:T(8,128)(2,1)}, bf16[512,1024]{1,0:T(8,128)(2,1)}, u32[]{:S(2)}, u32[]{:S(2)}) collective-permute-start(bf16[512,1024]{1,0:T(8,128)(2,1)} %add_convert_fusion.14), channel_id=1, source_target_pairs={{0,2},{1,3},{2,4},{3,5},{4,6},{5,7},{6,0},{7,1},{8,10},{9,11},{10,... | collective-permute-start | bytes 3145736 | tf_op jit(solution)/shard_map/ppermute | solution.py:285
  309.8 28.4 %collective-permute-start.51 = (f32[4,512]{1,0:T(4,128)S(1)}, f32[4,512]{1,0:T(4,128)S(1)}, u32[]{:S(2)}, u32[]{:S(2)}) collective-permute-start(f32[4,512]{1,0:T(4,128)S(1)} %get-tuple-element.719), channel_id=1, source_target_pairs={{0,4},{1,5},{2,6},{3,7},{4,0},{5,1},{6,2},{7,3},{8,12},{9,13},{10,... | collective-permute-start | bytes 24584 | tf_op jit(solution)/shard_map/ppermute | solution.py:295
  336.8 68.8 %collective-permute-start.60 = (bf16[2,3,512,512]{3,2,1,0:T(8,128)(2,1)}, bf16[2,3,512,512]{3,2,1,0:T(8,128)(2,1)}, u32[]{:S(2)}, u32[]{:S(2)}) collective-permute-start(bf16[2,3,512,512]{3,2,1,0:T(8,128)(2,1)} %get-tuple-element.563), channel_id=1, source_target_pairs={{0,8},{8,0},{16,24},{24,16},{1,9},{9,1},{17,25},{25,17},{2,10},{10... | collective-permute-start | bytes 9437192 | tf_op jit(solution)/shard_map/ppermute | solution.py:281
  338.9 70.8 %collective-permute-start.61 = (bf16[2,3,512,512]{3,2,1,0:T(8,128)(2,1)}, bf16[2,3,512,512]{3,2,1,0:T(8,128)(2,1)}, u32[]{:S(2)}, u32[]{:S(2)}) collective-permute-start(bf16[2,3,512,512]{3,2,1,0:T(8,128)(2,1)} %get-tuple-element.564), channel_id=1, source_target_pairs={{0,16},{8,24},{16,0},{24,8},{1,17},{9,25},{17,1},{25,9},{2,18},{10... | collective-permute-start | bytes 9437192 | tf_op jit(solution)/shard_map/ppermute | solution.py:281
  360.8 41.8 %collective-permute-start.59 = (bf16[512,1024]{1,0:T(8,128)(2,1)}, bf16[512,1024]{1,0:T(8,128)(2,1)S(1)}, u32[]{:S(2)}, u32[]{:S(2)}) collective-permute-start(bf16[512,1024]{1,0:T(8,128)(2,1)} %add_convert_fusion.7), channel_id=1, source_target_pairs={{0,2},{1,3},{2,4},{3,5},{4,6},{5,7},{6,0},{7,1},{8,10},{9,11},{10,... | collective-permute-start | bytes 3145736 | tf_op jit(solution)/shard_map/ppermute | solution.py:285
  426.3 36.6 %collective-permute-start.66 = (bf16[2,3,256,512]{3,2,1,0:T(8,128)(2,1)}, bf16[2,3,256,512]{3,2,1,0:T(8,128)(2,1)S(1)}, u32[]{:S(2)}, u32[]{:S(2)}) collective-permute-start(bf16[2,3,256,512]{3,2,1,0:T(8,128)(2,1)} %get-tuple-element.580), channel_id=1, source_target_pairs={{0,16},{8,24},{16,0},{24,8},{1,17},{9,25},{17,1},{25,9},{2,18},{10... | collective-permute-start | bytes 4718600 | tf_op jit(solution)/shard_map/ppermute | solution.py:281
  427.9 36.0 %collective-permute-start.67 = (bf16[2,3,256,512]{3,2,1,0:T(8,128)(2,1)S(1)}, bf16[2,3,256,512]{3,2,1,0:T(8,128)(2,1)S(1)}, u32[]{:S(2)}, u32[]{:S(2)}) collective-permute-start(bf16[2,3,256,512]{3,2,1,0:T(8,128)(2,1)S(1)} %copy-done.42), channel_id=1, source_target_pairs={{0,8},{8,0},{16,24},{24,16},{1,9},{9,1},{17,25},{25,17},{2,10},{10... | collective-permute-start | bytes 4718600 | tf_op jit(solution)/shard_map/ppermute | solution.py:281
  468.2 35.3 %collective-permute-start.69 = (bf16[2,3,256,512]{3,2,1,0:T(8,128)(2,1)S(1)}, bf16[2,3,256,512]{3,2,1,0:T(8,128)(2,1)}, u32[]{:S(2)}, u32[]{:S(2)}) collective-permute-start(bf16[2,3,256,512]{3,2,1,0:T(8,128)(2,1)S(1)} %add_convert_fusion.1.q_ref), channel_id=1, source_target_pairs={{0,16},{8,24},{16,0},{24,8},{1,17},{9,25},{17,1},{25,9},{2,18},{10... | collective-permute-start | bytes 4718600 | tf_op jit(solution)/shard_map/ppermute | solution.py:281
  468.8 35.3 %collective-permute-start.70 = (bf16[2,3,256,512]{3,2,1,0:T(8,128)(2,1)S(1)}, bf16[2,3,256,512]{3,2,1,0:T(8,128)(2,1)}, u32[]{:S(2)}, u32[]{:S(2)}) collective-permute-start(bf16[2,3,256,512]{3,2,1,0:T(8,128)(2,1)S(1)} %add_convert_fusion.q_ref), channel_id=1, source_target_pairs={{0,8},{8,0},{16,24},{24,16},{1,9},{9,1},{17,25},{25,17},{2,10},{10... | collective-permute-start | bytes 4718600 | tf_op jit(solution)/shard_map/ppermute | solution.py:281
  506.8 43.0 %collective-permute-start.73 = (bf16[2,3,256,512]{3,2,1,0:T(8,128)(2,1)S(1)}, bf16[2,3,256,512]{3,2,1,0:T(8,128)(2,1)}, u32[]{:S(2)}, u32[]{:S(2)}) collective-permute-start(bf16[2,3,256,512]{3,2,1,0:T(8,128)(2,1)S(1)} %add_convert_fusion.1.q_ref), channel_id=1, source_target_pairs={{0,8},{8,0},{16,24},{24,16},{1,9},{9,1},{17,25},{25,17},{2,10},{10... | collective-permute-start | bytes 4718600 | tf_op jit(solution)/shard_map/ppermute | solution.py:281
  507.9 41.9 %collective-permute-start.74 = (bf16[2,3,256,512]{3,2,1,0:T(8,128)(2,1)S(1)}, bf16[2,3,256,512]{3,2,1,0:T(8,128)(2,1)}, u32[]{:S(2)}, u32[]{:S(2)}) collective-permute-start(bf16[2,3,256,512]{3,2,1,0:T(8,128)(2,1)S(1)} %add_convert_fusion.q_ref), channel_id=1, source_target_pairs={{0,16},{8,24},{16,0},{24,8},{1,17},{9,25},{17,1},{25,9},{2,18},{10... | collective-permute-start | bytes 4718600 | tf_op jit(solution)/shard_map/ppermute | solution.py:281
  510.4 39.4 %collective-permute-start.75 = (bf16[512,1024]{1,0:T(8,128)(2,1)}, bf16[512,1024]{1,0:T(8,128)(2,1)}, u32[]{:S(2)}, u32[]{:S(2)}) collective-permute-start(bf16[512,1024]{1,0:T(8,128)(2,1)} %add_convert_fusion.4), channel_id=1, source_target_pairs={{0,2},{1,3},{2,4},{3,5},{4,6},{5,7},{6,0},{7,1},{8,10},{9,11},{10,... | collective-permute-start | bytes 3145736 | tf_op jit(solution)/shard_map/ppermute | solution.py:285
  549.9 29.3 %collective-permute-start.77 = (bf16[32,3328]{1,0:T(8,128)(2,1)S(1)}, bf16[32,3328]{1,0:T(8,128)(2,1)S(1)}, u32[]{:S(2)}, u32[]{:S(2)}) collective-permute-start(bf16[32,3328]{1,0:T(8,128)(2,1)S(1)} %get-tuple-element.716), channel_id=1, source_target_pairs={{0,8},{8,0},{16,24},{24,16},{1,9},{9,1},{17,25},{25,17},{2,10},{10... | collective-permute-start | bytes 638984 | tf_op jit(solution)/shard_map/ppermute | solution.py:281
  550.9 28.4 %collective-permute-start.78 = (bf16[32,3328]{1,0:T(8,128)(2,1)S(1)}, bf16[32,3328]{1,0:T(8,128)(2,1)S(1)}, u32[]{:S(2)}, u32[]{:S(2)}) collective-permute-start(bf16[32,3328]{1,0:T(8,128)(2,1)S(1)} %get-tuple-element.715), channel_id=1, source_target_pairs={{0,16},{8,24},{16,0},{24,8},{1,17},{9,25},{17,1},{25,9},{2,18},{10... | collective-permute-start | bytes 638984 | tf_op jit(solution)/shard_map/ppermute | solution.py:281
  553.4 69.1 %collective-permute-start.84 = (bf16[2,3,256,512]{3,2,1,0:T(8,128)(2,1)}, bf16[2,3,256,512]{3,2,1,0:T(8,128)(2,1)}, u32[]{:S(2)}, u32[]{:S(2)}) collective-permute-start(bf16[2,3,256,512]{3,2,1,0:T(8,128)(2,1)} %collective-permute-done.69.q_ref), channel_id=1, source_target_pairs={{0,8},{8,0},{16,24},{24,16},{1,9},{9,1},{17,25},{25,17},{2,10},{10... | collective-permute-start | bytes 4718600 | tf_op jit(solution)/shard_map/ppermute | solution.py:281
  554.4 71.8 %collective-permute-start.83 = (bf16[2,3,256,512]{3,2,1,0:T(8,128)(2,1)}, bf16[2,3,256,512]{3,2,1,0:T(8,128)(2,1)}, u32[]{:S(2)}, u32[]{:S(2)}) collective-permute-start(bf16[2,3,256,512]{3,2,1,0:T(8,128)(2,1)} %collective-permute-done.70.q_ref), channel_id=1, source_target_pairs={{0,16},{8,24},{16,0},{24,8},{1,17},{9,25},{17,1},{25,9},{2,18},{10... | collective-permute-start | bytes 4718600 | tf_op jit(solution)/shard_map/ppermute | solution.py:281
  579.2 40.6 %collective-permute-start.76 = (bf16[512,1024]{1,0:T(8,128)(2,1)}, bf16[512,1024]{1,0:T(8,128)(2,1)}, u32[]{:S(2)}, u32[]{:S(2)}) collective-permute-start(bf16[512,1024]{1,0:T(8,128)(2,1)} %add_convert_fusion.3), channel_id=1, source_target_pairs={{0,2},{1,3},{2,4},{3,5},{4,6},{5,7},{6,0},{7,1},{8,10},{9,11},{10,... | collective-permute-start | bytes 3145736 | tf_op jit(solution)/shard_map/ppermute | solution.py:285
  (107 other events, 1252.7 us)

commit v3 on v2

--- a/solution.py
+++ b/solution.py
@@ -26,8 +26,8 @@
 def step_kernel(aliased, *refs):
     (first_ref, x0_ref, x1_ref, d0_ref, d1_ref, r_ref, m_ref, rank_ref, key_ref,
      wg_ref, wu_ref, wd_ref) = refs[:12]
-    (g0_ref, g1_ref, o0_ref, o1_ref, dot_ref, xs_ref, ge_ref, hs_ref, dgs_ref, dus_ref,
-     t_s, gate_s, rg_s, ro_s) = refs[12 + aliased:]
+    (g0_ref, g1_ref, o0_ref, o1_ref, xs_ref, ge_ref, hs_ref, dgs_ref, dus_ref,
+     t_s, gate_s, rg_s, ro_s, dot_s) = refs[12 + aliased:]
     owned = gate_s.shape[0]
     E = m_ref.shape[1]
     T = x0_ref.shape[0]
@@ -73,7 +73,7 @@
         part = eo[q * CAP : (q + 1) * CAP].astype(F32)
         ro_s[q, pl.ds(pl.multiple_of(e * CAP, CAP), CAP), :] = (gs[q] * part).astype(BF)
         sd = jnp.sum(part * ds[q].astype(F32), axis=1, keepdims=True)
-        dot_ref[0, q] = jnp.sum(jnp.where(hits[q], sd, 0.0), axis=0, keepdims=True)
+        dot_s[e, q] = jnp.sum(jnp.where(hits[q], sd, 0.0), axis=0, keepdims=True)
     dh = dot(ge_ref[0], wd_ref[0], 1, 1)
     dgl = (dh * ul * sg * (1.0 + gl * (1.0 - sg))).astype(BF)
     dul = (dh * act).astype(BF)
@@ -92,7 +92,19 @@
             for j in range(1, owned):
                 hit = hit | (lane == keys[:, j : j + 1])
             S = jnp.where(hit, 1.0, 0.0).astype(BF)
-            g_ref[...] = dot(S, rg_s[q]).astype(BF)
+            g_ref[:T, :] = dot(S, rg_s[q]).astype(BF)
+            half = E // 2
+            row = lax.broadcasted_iota(jnp.int32, (half, 2 * T), 0)
+            column = lax.broadcasted_iota(jnp.int32, (half, 2 * T), 1)
+            dots = jnp.zeros((half, 2 * T), F32)
+            for j in range(owned):
+                number = first_ref[0] + j
+                here = (row == number % half) & (column // T == number // half)
+                twice = jnp.concatenate([dot_s[j, q], dot_s[j, q]], axis=1)
+                dots = jnp.where(here, twice, dots)
+            high = dots.astype(BF)
+            g_ref[T : T + half, :] = high
+            g_ref[T + half :, :] = (dots - high.astype(F32)).astype(BF)
             o_ref[...] = dot(S, ro_s[q]).astype(BF)
 
 
@@ -108,6 +120,8 @@
         jax.ShapeDtypeStruct((owned, rows, D), BF),
     ] + [jax.ShapeDtypeStruct((owned, rows, F), BF)] * 3
     token = jax.ShapeDtypeStruct((T, D), BF)
+    longer = jax.ShapeDtypeStruct((T + E, D), BF)
+    assert 2 * T == D
     aliased = 0 if kept is None else len(shapes)
     return pl.pallas_call(
         functools.partial(step_kernel, aliased),
@@ -125,18 +139,19 @@
                 pl.BlockSpec((1, F, D), lambda e, f: (e, 0, 0)),
             ]
             + [pl.BlockSpec(memory_space=pl.ANY)] * aliased,
-            out_specs=[pl.BlockSpec((T, D), full)] * 4
-            + [pl.BlockSpec((1, 2, 1, T), lambda e, f: (e, 0, 0, 0))]
+            out_specs=[pl.BlockSpec((T + E, D), full)] * 2
+            + [pl.BlockSpec((T, D), full)] * 2
             + [pl.BlockSpec((1, M, s.shape[2]), lambda e, f: (e, k, 0)) for s in shapes],
             scratch_shapes=[
                 pltpu.VMEM((128, T), F32),
                 pltpu.VMEM((owned, 2, 1, T), F32),
                 pltpu.VMEM((2, owned * CAP, D), BF),
                 pltpu.VMEM((2, owned * CAP, D), BF),
+                pltpu.VMEM((owned, 2, 1, T), F32),
             ],
         ),
-        out_shape=[token] * 4 + [jax.ShapeDtypeStruct((owned, 2, 1, T), F32)] + shapes,
-        input_output_aliases={12 + i: 5 + i for i in range(aliased)},
+        out_shape=[longer] * 2 + [token] * 2 + shapes,
+        input_output_aliases={12 + i: 4 + i for i in range(aliased)},
         compiler_params=pltpu.CompilerParams(vmem_limit_bytes=60 << 20),
         cost_estimate=COST,
         name="expert_step",
@@ -216,32 +231,54 @@
     )(bit, keep, got)
 
 
-def place_kernel(bits_ref, q_ref, *refs):
-    for i, o_ref in enumerate(refs[-3:]):
-        o_ref[0] = q_ref[0, i].astype(F32)
-
-
-def place_quarter(first, owned, bits, quarter, held):
-    count, _, rows, F = quarter.shape
+def place_kernel(counts, bits_ref, *refs):
+    ins, (gg_ref, gu_ref, gd_ref) = refs[:-3], refs[-3:]
+    e = pl.program_id(0)
+    begin = 0
+    for n, many in enumerate(counts):
+
+        @pl.when((e >= begin) & (e < begin + many))
+        def _(n=n):
+            for i in range(4):
+                q_ref = ins[4 * n + i]
+                rows, half = q_ref.shape[2:]
+                one = bits_ref[2 * n] if i < 2 else 1 - bits_ref[2 * n]
+                two = bits_ref[2 * n + 1] if i % 2 == 0 else 1 - bits_ref[2 * n + 1]
+                at = pl.ds(pl.multiple_of((2 * one + two) * rows, rows), rows)
+                gg_ref[0, at, :] = q_ref[0, 0].astype(F32)
+                gu_ref[0, at, :] = q_ref[0, 1].astype(F32)
+                at = pl.ds(pl.multiple_of(two * rows, rows), rows)
+                columns = pl.ds(pl.multiple_of(one * half, half), half)
+                gd_ref[0, at, columns] = q_ref[0, 2].astype(F32)
+
+        begin += many
+
+
+def place_all(bits, quarters):
+    counts = [q[0].shape[0] for q in quarters]
+    owned = sum(counts)
+    _, _, rows, F = quarters[0][0].shape
     D = 4 * rows
-    shapes = [(owned, D, F), (owned, D, F), (owned, F, D)]
-    tall = pl.BlockSpec((1, rows, F), lambda e, b: (first + e, 2 * b[0] + b[1], 0))
-    wide = pl.BlockSpec((1, rows, F), lambda e, b: (first + e, b[1], b[0]))
-    aliased = 0 if held is None else 3
+    specs = []
+    begin = 0
+    for many in counts:
+        block = lambda e, b, begin=begin, many=many: (jnp.clip(e - begin, 0, many - 1), 0, 0, 0)
+        specs += [pl.BlockSpec((1, 3, rows, F), block)] * 4
+        begin += many
+    shapes = [(D, F), (D, F), (F, D)]
     return pl.pallas_call(
-        place_kernel,
+        functools.partial(place_kernel, counts),
         grid_spec=pltpu.PrefetchScalarGridSpec(
             num_scalar_prefetch=1,
-            grid=(count,),
-            in_specs=[pl.BlockSpec((1, 3, rows, F), lambda e, b: (e, 0, 0, 0))]
-            + [pl.BlockSpec(memory_space=pl.ANY)] * aliased,
-            out_specs=[tall, tall, wide],
+            grid=(owned,),
+            in_specs=specs,
+            out_specs=[pl.BlockSpec((1,) + s, lambda e, b: (e, 0, 0)) for s in shapes],
         ),
-        out_shape=[jax.ShapeDtypeStruct(s, F32) for s in shapes],
-        input_output_aliases={2 + i: i for i in range(aliased)},
+        out_shape=[jax.ShapeDtypeStruct((owned,) + s, F32) for s in shapes],
+        compiler_params=pltpu.CompilerParams(vmem_limit_bytes=60 << 20),
         cost_estimate=COST,
-        name="place_quarter",
-    )(bits, quarter, *(held or ()))
+        name="place_all",
+    )(bits, *[q for group in quarters for q in group])
 
 
 def assemble_kernel(place,p_ref,*refs):
@@ -290,33 +327,46 @@
         blocks+=[b,swap_pair(b)]
     return blocks
 
-def send_back(v,k,b):
-    n=lax.axis_size("expert")
-    return lax.ppermute(v,"expert",[(i,((i//2-k)%(n//2))*2+((i%2)^b)) for i in range(n)]) if k or b else v
-
 def all_shifts(v):
     return [v]+[shift_chips(v,k) for k in range(1,lax.axis_size("expert")//2)]
 
-def share_kernel(rows_ref, *refs):
-    o_ref = refs[-1]
-    for r, piece in enumerate(refs[:-1]):
+def share_kernel(count, rows_ref, *refs):
+    q_ref, k_ref, v_ref, o_ref, r_ref, m_ref, a_ref, s_ref, g_ref = refs[count:]
+    D = q_ref.shape[1]
+    groups = D // 256
+    for r, piece in enumerate(refs[:count]):
         sub = piece.shape[0]
-        row = pl.multiple_of(rows_ref[r], sub)
-        o_ref[pl.ds(row, sub), :] = piece[...].astype(F32)
-
-
-def place_share(rows, pieces):
+        rows = pl.ds(pl.multiple_of(rows_ref[r], sub), sub)
+        for g in range(groups):
+            at = 512 * g
+            q_ref[rows, 256 * g : 256 * g + 256] = piece[:, at : at + 256].astype(F32)
+            k_ref[rows, 128 * g : 128 * g + 128] = piece[:, at + 256 : at + 384].astype(F32)
+            v_ref[rows, 128 * g : 128 * g + 128] = piece[:, at + 384 : at + 512].astype(F32)
+        at = 512 * groups
+        o_ref[rows, :] = piece[:, at : at + D].astype(F32)
+        s_ref[rows, :] = piece[:, at + D : at + D + 128].astype(F32)
+        g_ref[rows, :] = piece[:, at + D + 128 : at + D + 256].astype(F32)
+    E = r_ref.shape[1]
+    r_ref[...] = s_ref[:, :E]
+    m_ref[...] = s_ref[...].T[E : E + 1, :]
+    a_ref[...] = g_ref[...].T[:1, :]
+
+
+def place_share(rows, pieces, D, kv):
     sub, W = pieces[0].shape
     n = len(pieces)
+    assert W == 2 * D + 2 * kv + 256 and D // 256 == kv // 128
+    shapes = [(n * sub, w) for w in (D, kv, kv, D, EXPERTS)] + [(1, n * sub)] * 2
     return pl.pallas_call(
-        share_kernel,
+        functools.partial(share_kernel, n),
         grid_spec=pltpu.PrefetchScalarGridSpec(
             num_scalar_prefetch=1,
             grid=(1,),
             in_specs=[pl.BlockSpec((sub, W), lambda i, r: (0, 0))] * n,
-            out_specs=pl.BlockSpec((n * sub, W), lambda i, r: (0, 0)),
+            out_specs=[pl.BlockSpec(s, lambda i, r: (0, 0)) for s in shapes],
+            scratch_shapes=[pltpu.VMEM((n * sub, 128), F32)] * 2,
         ),
-        out_shape=jax.ShapeDtypeStruct((n * sub, W), F32),
+        out_shape=[jax.ShapeDtypeStruct(s, F32) for s in shapes],
         cost_estimate=COST,
         name="place_share",
     )(rows, *pieces)
@@ -425,7 +475,7 @@
         cost_estimate=COST,
         name="project")(mixed,w2,h,w1)
 
-def branch_kernel(gain_at,mg_ref,res_ref,moe_ref,mix_ref,cot_ref,wo_ref,r_ref,misc_ref,mem_ref,td_ref,
+def branch_kernel(gain_at,mg_ref,res_ref,moe_ref,mix_ref,cot_ref,wo_ref,r_ref,misc_ref,mem_ref,
                   dres_ref,dmix_ref,out_ref,t_s):
     T,D=res_ref.shape
     E=mem_ref.shape[0]
@@ -434,11 +484,13 @@
     kept=jnp.where(mem,t_s[:E,:],-1e30)
     e=jnp.where(mem,jnp.exp(kept-jnp.max(kept,axis=0,keepdims=True)),0.0)
     g=e/jnp.sum(e,axis=0,keepdims=True)
-    td=td_ref[...]
+    half=E//2
+    sums=mg_ref[T:T+half,:].astype(F32)+mg_ref[T+half:,:].astype(F32)
+    td=jnp.concatenate([sums[:,:T],sums[:,T:]],axis=0)
     t_s[...]=jnp.zeros_like(t_s)
     t_s[:E,:]=g*(td-jnp.sum(g*td,axis=0,keepdims=True))
     gl=t_s[...].T.astype(BF)
-    dmoe=dot(gl,r_ref[...],1,1)+mg_ref[...].astype(F32)
+    dmoe=dot(gl,r_ref[...],1,1)+mg_ref[:T,:].astype(F32)
     res=res_ref[...]
     inv=lax.rsqrt(jnp.mean(res*res,axis=-1,keepdims=True)+norm_eps)
     gain=gain_row(misc_ref,gain_at)
@@ -453,19 +505,19 @@
     column=jnp.broadcast_to(grad_gain,(128,D)).T
     out_ref[:,D:]=jnp.where(lane==E,column,dot(moe_ref[...],gl,0,0)).astype(BF)
 
-def branch(gain_at,mg,res,moe_in,mixed,cot,w2,w1,mem_t,td):
+def branch(gain_at,mg,res,moe_in,mixed,cot,w2,w1,mem_t):
     T,D=res.shape
     E=mem_t.shape[0]
     full=lambda i:(0,0)
     return pl.pallas_call(functools.partial(branch_kernel,gain_at),grid=(1,),
-        in_specs=[pl.BlockSpec((T,D),full)]*5+[pl.BlockSpec((D,D),full),pl.BlockSpec((D,128),lambda i:(0,D//128)),
-                  pl.BlockSpec((D,128),lambda i:(0,MISC)),pl.BlockSpec((E,T),full),pl.BlockSpec((E,T),full)],
+        in_specs=[pl.BlockSpec((T+E,D),full)]+[pl.BlockSpec((T,D),full)]*4+[pl.BlockSpec((D,D),full),pl.BlockSpec((D,128),lambda i:(0,D//128)),
+                  pl.BlockSpec((D,128),lambda i:(0,MISC)),pl.BlockSpec((E,T),full)],
         out_specs=[pl.BlockSpec((T,D),full),pl.BlockSpec((T,D),full),pl.BlockSpec((D,D+128),full)],
         out_shape=[jax.ShapeDtypeStruct((T,D),F32),jax.ShapeDtypeStruct((T,D),BF),jax.ShapeDtypeStruct((D,D+128),BF)],
         scratch_shapes=[pltpu.VMEM((128,T),F32)],
         compiler_params=pltpu.CompilerParams(vmem_limit_bytes=60<<20),
         cost_estimate=COST,
-        name="branch")(mg,res,moe_in,mixed,cot,w2,w2,w1,mem_t,td)
+        name="branch")(mg,res,moe_in,mixed,cot,w2,w2,w1,mem_t)
 
 def fold(v):
     return v+pltpu.roll(v,2*HALF,1)
@@ -627,12 +679,12 @@
     second_pack = pad_columns(jnp.concatenate([w_out, w_router], axis=1))
     cotangent_steps = [cotangent]
     routes_shifts = all_shifts(routes.astype(BF).reshape(-1, 128))
-    shifts_one = all_shifts(own_slice(first_pack))
-    shifts_one, routes_shifts, second_slice, cotangent_steps = tie(
-        shifts_one, routes_shifts, own_slice(second_pack), cotangent_steps
-    )
-    shifts_two = all_shifts(second_slice)
-    stack_one = jnp.stack(shifts_one)
+    both_shifts = all_shifts(own_slice(jnp.concatenate([first_pack, second_pack], axis=1)))
+    both_shifts, routes_shifts, cotangent_steps = tie(both_shifts, routes_shifts, cotangent_steps)
+    stacks = jnp.stack(both_shifts)
+    first_width = first_pack.shape[1]
+    stack_one = stacks[:, :, :first_width]
+    stack_two = stacks[:, :, first_width:]
     slices_one = [stack_one] + [swap_dp(stack_one, r) for r in range(1, dp_count)]
     cotangent_steps.append(shift_chips(cotangent_steps[0], 1))
     routes_all = []
@@ -658,42 +710,35 @@
     cosine, sine = rope_tables(segment_row)
     segment_column = segment_row[:, None]
     segment_line = segment_row[None, :]
-    from_chip = (me // 2 + jnp.arange(chips, dtype=jnp.int32)) % chips
-    from_order = (from_chip[:, None] * 2 + core_order[None, :]).reshape(-1)
-    from_order = jnp.argsort(from_order)
-    tables = [rank_rows, keys, member_all, member_line, cosine, sine, from_order]
-    tables, slices_one, shifts_two = tie(tables, slices_one, shifts_two)
-    rank_rows, keys, member_all, member_line, cosine, sine, from_order = tables
+    tables = [rank_rows, keys, member_all, member_line, cosine, sine]
+    tables, slices_one, stack_two = tie(tables, slices_one, stack_two)
+    rank_rows, keys, member_all, member_line, cosine, sine = tables
     pieces_one = []
     for s in slices_one:
         pieces_one += [s, swap_pair(s)]
-    pieces_one, shifts_two, cotangent_steps = tie(pieces_one, shifts_two, cotangent_steps)
-    for k in range(2, min(chips, 3)):
+    pieces_one, stack_two, cotangent_steps = tie(pieces_one, stack_two, cotangent_steps)
+    for k in range(2, chips - 1):
         cotangent_steps.append(shift_chips(cotangent_steps[k - 1], 1))
-    stack_two = jnp.stack(shifts_two)
+    if chips > 2:
+        cotangent_steps.append(shift_chips(cotangent_steps[0], chips - 1))
+    attn_weights = assemble(places, pieces_one)
+    attn_weights, stack_two = tie(attn_weights, stack_two)
     slices_two = [stack_two] + [swap_dp(stack_two, r) for r in range(1, dp_count)]
-    attn_weights = assemble(places, pieces_one)
-    attn_weights, slices_two, cotangent_steps = tie(attn_weights, slices_two, cotangent_steps)
-    pieces_two = []
-    for s in slices_two:
-        pieces_two += [s, swap_pair(s)]
-    for k in range(3, chips):
-        cotangent_steps.append(shift_chips(cotangent_steps[k - 1], 1))
-    cotangent_pairs = [swap_pair(c) for c in cotangent_steps[: chips - 1]]
     kv_heads = key_weight.shape[1] // (2 * HALF)
     query, key, value, mixed, lse = attend(
         0, hidden, attn_weights, cosine, sine, segment_column, segment_line, kv_heads
     )
-    mixed, pieces_two, cotangent_steps, cotangent_pairs = tie(
-        mixed, pieces_two, cotangent_steps, cotangent_pairs
-    )
+    mixed, slices_two, cotangent_steps = tie(mixed, slices_two, cotangent_steps)
+    pieces_two = []
+    for s in slices_two:
+        pieces_two += [s, swap_pair(s)]
+    d = [cotangent_steps[0], swap_pair(cotangent_steps[0])]
+    mixed, pieces_two, d = tie(mixed, pieces_two, d)
     out_weights = assemble(places, pieces_two)
     residual, moe_in = project(1, mixed, out_weights, hidden, attn_weights)
-    cotangent_pairs.append(swap_pair(cotangent_steps[-1]))
     x = [moe_in, swap_pair(moe_in)]
     x, moe_in = tie(x, moe_in)
     kept = None
-    dots = []
     grad_parts = []
     out_parts = []
     hop = None
@@ -706,7 +751,7 @@
                 k,
                 first_expert[None],
                 x,
-                (cotangent_steps[k], cotangent_pairs[k]),
+                d,
                 out_weights,
                 member_all,
                 rank_rows,
@@ -717,18 +762,18 @@
                 kept,
             )
         )
-        kept = outs[5:]
-        outs = outs[:5]
-        outs, kept, following, hop, dots, grad_parts, out_parts = tie(
-            outs, kept, following, hop, dots, grad_parts, out_parts
+        kept = outs[4:]
+        outs = outs[:4]
+        outs, kept, following, hop, grad_parts, out_parts = tie(
+            outs, kept, following, hop, grad_parts, out_parts
         )
         if following is not None:
             x = [following, swap_pair(following)]
+            d = [cotangent_steps[k + 1], swap_pair(cotangent_steps[k + 1])]
         grad_part = (outs[0].astype(F32) + swap_pair(outs[1]).astype(F32)).astype(BF)
         out_parts = out_parts + [(outs[2], outs[3])]
-        dots = dots + [outs[4]]
         if k + 1 < chips:
-            x, grad_part = tie(x, grad_part)
+            x, d, grad_part = tie(x, d, grad_part)
         grad_parts = grad_parts + [grad_part]
     dp_me = lax.axis_index("dp")
     low = dp_me % 2
@@ -737,34 +782,29 @@
     plans = [(0, count, 1, 2, low, high)]
     if owned > count:
         plans.append((count, owned - count, 2, 1, high, low))
-    returned = [send_back(dots[k][:, b, 0], k, b) for k in range(chips) for b in range(2)]
     total = grad_parts[1]
     first_hop = 2
     if hop is not None:
         total, kept = tie((grad_parts[2].astype(F32) + hop.astype(F32)).astype(BF), kept)
         first_hop = 3
+    moved = shift_chips(total, 1)
     halves = []
-    gots = []
-    for number, k in enumerate(range(first_hop, chips + 1)):
-        moved = shift_chips(total, 1)
-        if number < len(plans):
-            first_of, many, one, two, bit_one, bit_two = plans[number]
-            send, keep = weight_grads(bit_one[None], first_of, many, kept)
-            halves.append((first_of, one, two, bit_one, bit_two, keep))
-            moved, send, kept = tie(moved, send, kept)
-            gots.append(swap_dp(send, one))
-        if k < chips:
-            total = (grad_parts[k].astype(F32) + moved.astype(F32)).astype(BF)
-            total, kept = tie(total, kept)
+    sends = []
+    for first_of, many, one, two, bit_one, bit_two in plans:
+        send, keep = weight_grads(bit_one[None], first_of, many, kept)
+        halves.append((first_of, one, two, bit_one, bit_two, keep))
+        sends.append(send)
+    moved, sends = tie(moved, sends)
+    gots = [swap_dp(send, h[1]) for h, send in zip(halves, sends)]
+    for k in range(first_hop, chips):
+        moved = shift_chips((grad_parts[k].astype(F32) + moved.astype(F32)).astype(BF), 1)
     moe_grad = (grad_parts[0].astype(F32) + moved.astype(F32)).astype(BF)
-    moe_grad, returned, out_parts = tie(moe_grad, returned, out_parts)
-    out_parts = [(a.astype(F32) + swap_pair(b).astype(F32)).astype(BF) for a, b in out_parts]
-    token_dot = jnp.stack(returned)[from_order].reshape(EXPERTS, tokens)
+    out_sum = (out_parts[1][0].astype(F32) + swap_pair(out_parts[1][1]).astype(F32)).astype(BF)
+    moe_grad, out_sum = tie(moe_grad, out_sum)
     grad_residual, mixed_gradient, out_grads = branch(
-        1, moe_grad, residual, moe_in, mixed, cotangent, out_weights, attn_weights, member_line, token_dot
+        1, moe_grad, residual, moe_in, mixed, cotangent, out_weights, attn_weights, member_line
     )
-    mixed_gradient, out_parts = tie(mixed_gradient, out_parts)
-    out_sum = shift_chips(out_parts[1], 1)
+    out_sum = shift_chips(out_sum, 1)
     attn_grads, grad_input = attend_back(
         0,
         hidden,
@@ -781,7 +821,7 @@
         grad_residual,
         out_grads,
     )
-    attn_grads, out_sum, gots = tie(attn_grads, out_sum, gots)
+    attn_grads, out_sum, gots, out_parts = tie(attn_grads, out_sum, gots, out_parts)
 
     def block_for(k, b):
         number = chip_order[k] * 2 + core_order[b]
@@ -794,12 +834,12 @@
         seconds.append(send)
         keeps.append(keep)
     parts = [(block_for(k, 0), swap_pair(block_for(k, 1))) for k in range(chips)]
-    out_sum = (out_parts[2].astype(F32) + out_sum.astype(F32)).astype(BF)
-    seconds, keeps, parts, out_sum = tie(seconds, keeps, parts, out_sum)
+    seconds, keeps, parts, out_parts = tie(seconds, keeps, parts, out_parts)
     parts = [(a.astype(F32) + b.astype(F32)).astype(BF) for a, b in parts]
     gots = [swap_dp(send, h[2]) for h, send in zip(halves, seconds)]
     running = shift_chips(parts[1], 1)
-    gots, running = tie(gots, running)
+    out_parts = [(a.astype(F32) + swap_pair(b).astype(F32)).astype(BF) for a, b in out_parts]
+    gots, running, out_parts = tie(gots, running, out_parts)
     mine = [(k.astype(F32) + g.astype(F32)).astype(BF) for k, g in zip(keeps, gots)]
     running = (parts[2].astype(F32) + running.astype(F32)).astype(BF)
     mine, running, out_sum = tie(mine, running, out_sum)
@@ -807,52 +847,48 @@
     running = shift_chips(running, 1)
     others, running, mine = tie(others, running, mine)
     thirds = [swap_dp(m, h[1]) for h, m in zip(halves, mine)]
-    out_sum = shift_chips(out_sum, 1)
     for k in [*range(3, chips), 0]:
         running = (parts[k].astype(F32) + running.astype(F32)).astype(BF)
         if k:
             running = shift_chips(running, 1)
-    part, thirds, others, mine, out_sum = tie(running, thirds, others, mine, out_sum)
-    for o in out_parts[3:]:
-        out_sum = shift_chips((o.astype(F32) + out_sum.astype(F32)).astype(BF), 1)
-    result = (residual + out_parts[0].astype(F32) + out_sum.astype(F32)).astype(BF)
+    part, others, mine, out_sum = tie(running, others, mine, out_sum)
     sub = own_rows // dp_count
 
     def rows_of(r):
         return (dp_me ^ r) * sub
 
-    fourths = [swap_dp(o, h[1]) for h, o in zip(halves, others)]
     sent = [lax.dynamic_slice_in_dim(part, rows_of(r), sub, 0) for r in range(dp_count)]
     received = [sent[0]] + [swap_dp(sent[r], r) for r in range(1, dp_count)]
-    held = None
-    for (first_of, one, two, bit_one, bit_two, _), m, other, third in zip(
-        halves, mine, others, thirds
-    ):
-        held = place_quarter(first_of, owned, jnp.stack([bit_one, bit_two]), m, held)
-        held = place_quarter(first_of, owned, jnp.stack([bit_one, 1 - bit_two]), other, held)
-        held = place_quarter(first_of, owned, jnp.stack([1 - bit_one, bit_two]), third, held)
-    held, received = tie(held, received)
+    if chips > 2:
+        out_sum = shift_chips((out_parts[2].astype(F32) + out_sum.astype(F32)).astype(BF), 1)
+    received, thirds, others = tie(received, thirds, others)
+    fourths = [swap_dp(o, h[1]) for h, o in zip(halves, others)]
     total = received[0].astype(F32)
     for piece in received[1:]:
         total = total + piece.astype(F32)
     total = total.astype(BF)
     pieces = [swap_dp(total, r) if r else total for r in range(dp_count)]
-    for (first_of, one, two, bit_one, bit_two, _), fourth in zip(halves, fourths):
-        held = place_quarter(first_of, owned, jnp.stack([1 - bit_one, 1 - bit_two]), fourth, held)
-    big = held
-    share = place_share(jnp.stack([rows_of(r) for r in range(dp_count)]), pieces)
-    groups = share[:, : 2 * width].reshape(own_rows, -1, 512)
-    out_share = share[:, 2 * width :]
+    for o in out_parts[3:]:
+        out_sum = shift_chips((o.astype(F32) + out_sum.astype(F32)).astype(BF), 1)
+    big = place_all(
+        jnp.stack([b for h in halves for b in h[3:5]]),
+        list(zip(mine, others, thirds, fourths)),
+    )
+    big, pieces, out_sum = tie(big, pieces, out_sum)
+    result = (residual + out_parts[0].astype(F32) + out_sum.astype(F32)).astype(BF)
+    share = place_share(
+        jnp.stack([rows_of(r) for r in range(dp_count)]), pieces, width, key_weight.shape[1]
+    )
     return (
         result,
         grad_input,
-        share[:, -128],
-        groups[:, :, :256].reshape(own_rows, -1),
-        groups[:, :, 256:384].reshape(own_rows, -1),
-        groups[:, :, 384:].reshape(own_rows, -1),
-        out_share[:, :width],
-        out_share[:, width + EXPERTS],
-        out_share[:, width : width + EXPERTS],
+        share[6][0],
+        share[0],
+        share[1],
+        share[2],
+        share[3],
+        share[5][0],
+        share[4],
         big[0],
         big[1],
         big[2],

time: 638 us -> 607 us (0.951)
  Pallas kernels: 258 us -> 242 us
  waiting for transfers between devices: 205 us -> 219 us
  local copies, waits for them, and re-layouts: 41.5 us -> 28.4 us
  other arithmetic: 46 us -> 37.4 us
    ppermute x22, waiting for transfers between devices: 53.2 us -> 86.4 us  [swap_dp(): lax.ppermute(v, 'dp', [(i, i ^ r) for i in range(lax.axis_size('dp'))])]
    ppermute x24 -> x21, waiting for transfers between devices: 133 us -> 114 us  [shift_chips(): return lax.ppermute(v, 'expert', [(i, (i + 2 * k) % n) for i in range(n)])]
    pallas_call x9 -> x2, Pallas kernels: 31.6 us -> 17.1 us  [the longest x1 14 us: place_all(): pl.pallas_call(functools.partial(place_kernel, counts), grid_spec=pltpu.P...]
    ppermute x7 -> x0, starting transfers between devices: 6.54 us -> none  [send_back(): lax.ppermute(v, 'expert', [(i, (i // 2 - k) % (n // 2) * 2 + (i % 2 ^ b))...]
    unnamed x110 -> x83, local copies, waits for them, and re-layouts: 19.4 us -> 14.9 us
    ppermute x24 -> x21, starting transfers between devices: 28.9 us -> 28.5 us  [shift_chips(): return lax.ppermute(v, 'expert', [(i, (i + 2 * k) % n) for i in range(n)])]
  transfers between devices with their start and end apart: 85 -> 75, of which waited for: 34 -> 32; matrix products, arithmetic and copies ran while one was open for 9% -> 6% of each run, Pallas kernels for 39% -> 38%
where the time goes in v3:
time: 607 us; the launch traced here: 600 us
  Pallas kernels  242 us (40%)
  waiting for transfers between devices  219 us (36%)
  starting transfers between devices  61.1 us (10%)
  other arithmetic  37.4 us (6%)
  local copies, waits for them, and re-layouts  28.4 us (5%)
  between operations  9.45 us (2%)
    ppermute x21, waiting for transfers between devices, shift_chips(): return lax.ppermute(v, 'expert', [(i, (i + 2 * k) % n) for i in range(n)])  114 us
    pallas_call x4, Pallas kernels, expert_step(): pl.pallas_call(functools.partial(step_kernel, aliased), grid_spec=pltpu.P...  110 us
    ppermute x22, waiting for transfers between devices, swap_dp(): lax.ppermute(v, 'dp', [(i, i ^ r) for i in range(lax.axis_size('dp'))])  86.4 us
    pallas_call x1, Pallas kernels, attend_back(): pl.pallas_call(functools.partial(attend_back_kernel, gain_at), grid=(step...  33 us
    pallas_call x2, Pallas kernels, weight_grads(): pl.pallas_call(functools.partial(weight_kernel, parts), grid_spec=pltpu.P...  31.5 us
    ppermute x21, starting transfers between devices, shift_chips(): return lax.ppermute(v, 'expert', [(i, (i + 2 * k) % n) for i in range(n)])  28.5 us
    ppermute x22, starting transfers between devices, swap_dp(): lax.ppermute(v, 'dp', [(i, i ^ r) for i in range(lax.axis_size('dp'))])  25.7 us
    ppermute x32, waiting for transfers between devices, swap_pair(): lax.ppermute(v, 'expert', [(i, i ^ 1) for i in range(lax.axis_size('exper...  17.8 us
  transfers between devices with their start and end apart: 75, of which 32 were waited for; matrix products, arithmetic and copies ran while one was open for 6% of the time, Pallas kernels for 38%

profile of v3, /device:TPU:0, one launch (start us, length us, event | category | flops | bytes accessed | tf_op | source)
XLA Modules:
  0.0 600.2 jit_solution(12170532388066647230)
XLA Ops:
  16.4 8.8 %collective-permute-done.3 = bf16[32,128]{1,0:T(8,128)(2,1)S(1)} collective-permute-done((bf16[32,128]{1,0:T(8,128)(2,1)S(1)}, bf16[32,128]{1,0:T(8,128)(2,1)S(1)}, u32[]{:S(2)}, u32[]{:S(2)}) %collective-permute-start.3) | collective-permute-done | bytes 8224 | tf_op jit(solution)/shard_map/ppermute | solution.py:322
  48.3 12.3 %collective-permute-done.11.refs_4_ = bf16[4,32,2176]{2,1,0:T(8,128)(2,1)S(1)} collective-permute-done((bf16[4,32,2176]{2,1,0:T(8,128)(2,1)S(1)}, bf16[4,32,2176]{2,1,0:T(8,128)(2,1)S(1)}, u32[]{:S(2)}, u32[]{:S(2)}) %collective-permute-start.11) | collective-permute-done | bytes 557088 | tf_op jit(solution)/shard_map/ppermute | solution.py:318
  69.4 6.0 %assemble.2.misc_ref.wq_ref.wk_ref.wv_ref = bf16[1024,2176]{1,0:T(8,128)(2,1)S(1)} custom-call(s32[32]{0:T(128)S(1)} %add.228.p_ref, bf16[4,32,2176]{2,1,0:T(8,128)(2,1)S(1)} %slice.42.refs_0_, bf16[4,32,2176]{2,1,0:T(8,128)(2,1)S(1)} %collective-permute-done.13.refs_1_, bf16[4,32,2176]{2,1,0:T(8,128)(2,1)S(1)} %collective-permute-done.10.refs_2_, ...), custom_call_target="tpu_custom_call" | custom-call | flops 1048576 | bytes 1048576 | tf_op jit(solution)/shard_map/assemble/pallas_call | solution.py:297
  81.8 17.2 %attend.1 = (bf16[512,1024]{1,0:T(8,128)(2,1)}, bf16[512,512]{1,0:T(8,128)(2,1)}, bf16[512,512]{1,0:T(8,128)(2,1)}, bf16[512,1024]{1,0:T(8,128)(2,1)}, f32[4,8,512]{2,1,0:T(8,128)}) custom-call(bf16[512,1024]{1,0:T(8,128)(2,1)} %h_ref.5, bf16[1024,2176]{1,0:T(8,128)(2,1)} %copy-done, bf16[1024,2176]{1,0:T(8,128)(2,1)} %copy-done, ...), custom_call_target="tpu_custom_call" | custom-call | flops 1048576 | bytes 1048576 | tf_op jit(solution)/shard_map/attend/pallas_call | solution.py:448
  99.1 15.8 %collective-permute-done.22.refs_3_ = bf16[512,1024]{1,0:T(8,128)(2,1)} collective-permute-done((bf16[512,1024]{1,0:T(8,128)(2,1)}, bf16[512,1024]{1,0:T(8,128)(2,1)}, u32[]{:S(2)}, u32[]{:S(2)}) %collective-permute-start.22) | collective-permute-done | bytes 1048608 | tf_op jit(solution)/shard_map/ppermute | solution.py:322
  125.1 4.9 project.1
  135.1 27.5 %expert_step.4 = (bf16[544,1024]{1,0:T(8,128)(2,1)}, bf16[544,1024]{1,0:T(8,128)(2,1)}, bf16[512,1024]{1,0:T(8,128)(2,1)}, bf16[512,1024]{1,0:T(8,128)(2,1)}, bf...) custom-call(s32[1]{0:T(128)} %bitcast.14.refs_0_, ...), custom_call_target="tpu_custom_call" | custom-call | flops 1048576 | bytes 1048576 | tf_op jit(solution)/shard_map/expert_step/pallas_call | solution.py:126
  173.3 27.5 %expert_step.5 = (bf16[544,1024]{1,0:T(8,128)(2,1)}, bf16[544,1024]{1,0:T(8,128)(2,1)}, bf16[512,1024]{1,0:T(8,128)(2,1)}, bf16[512,1024]{1,0:T(8,128)(2,1)}, bf...) custom-call(s32[1]{0:T(128)} %bitcast.14.refs_0_, ...), custom_call_target="tpu_custom_call", output_to_operand_aliasing={{4}: (12, {}), {5}: (13, {}), {6}: (14, {}), {7}: (15, {}),... | custom-call | flops 1048576 | bytes 1048576 | tf_op jit(solution)/shard_map/expert_step/pallas_call | solution.py:126
  210.0 27.5 %expert_step.6 = (bf16[544,1024]{1,0:T(8,128)(2,1)}, bf16[544,1024]{1,0:T(8,128)(2,1)}, bf16[512,1024]{1,0:T(8,128)(2,1)}, bf16[512,1024]{1,0:T(8,128)(2,1)}, bf...) custom-call(s32[1]{0:T(128)} %bitcast.14.refs_0_, ...), custom_call_target="tpu_custom_call", output_to_operand_aliasing={{4}: (12, {}), {5}: (13, {}), {6}: (14, {}), {7}: (15, {}),... | custom-call | flops 1048576 | bytes 1048576 | tf_op jit(solution)/shard_map/expert_step/pallas_call | solution.py:126
  243.7 27.5 %expert_step.7 = (bf16[544,1024]{1,0:T(8,128)(2,1)}, bf16[544,1024]{1,0:T(8,128)(2,1)}, bf16[512,1024]{1,0:T(8,128)(2,1)}, bf16[512,1024]{1,0:T(8,128)(2,1)}, bf...) custom-call(s32[1]{0:T(128)} %bitcast.14.refs_0_, ...), custom_call_target="tpu_custom_call", output_to_operand_aliasing={{4}: (12, {}), {5}: (13, {}), {6}: (14, {}), {7}: (15, {}),... | custom-call | flops 1048576 | bytes 1048576 | tf_op jit(solution)/shard_map/expert_step/pallas_call | solution.py:126
  275.4 15.7 %weight_grads.3 = (bf16[2,3,512,512]{3,2,1,0:T(8,128)(2,1)}, bf16[2,3,512,512]{3,2,1,0:T(8,128)(2,1)}) custom-call(s32[1]{0:T(128)} %bitcast.12.bit_ref, bf16[4,1536,1024]{2,1,0:T(8,128)(2,1)} %get-tuple-element.436.xs_ref, bf16[4,1536,1024]{2,1,0:T(8,128)(2,1)} %get-tuple-element.437.ge_ref, bf16[4,1536,512]{2,1,0:T(8,128)(2,1)} %get-tuple-element.438.hs_ref, ...), custom_call_target="tpu_custom_call" | custom-call | flops 1048576 | bytes 1048576 | tf_op jit(solution)/shard_map/weight_grads/pallas_call | solution.py:189
  291.1 15.8 %weight_grads.2 = (bf16[2,3,512,512]{3,2,1,0:T(8,128)(2,1)}, bf16[2,3,512,512]{3,2,1,0:T(8,128)(2,1)}) custom-call(s32[1]{0:T(128)} %bitcast.13.bit_ref, bf16[4,1536,1024]{2,1,0:T(8,128)(2,1)} %get-tuple-element.436.xs_ref, bf16[4,1536,1024]{2,1,0:T(8,128)(2,1)} %get-tuple-element.437.ge_ref, bf16[4,1536,512]{2,1,0:T(8,128)(2,1)} %get-tuple-element.438.hs_ref, ...), custom_call_target="tpu_custom_call" | custom-call | flops 1048576 | bytes 1048576 | tf_op jit(solution)/shard_map/weight_grads/pallas_call | solution.py:189
  313.0 26.8 %collective-permute-done.44 = bf16[544,1024]{1,0:T(8,128)(2,1)S(1)} collective-permute-done((bf16[544,1024]{1,0:T(8,128)(2,1)S(1)}, bf16[544,1024]{1,0:T(8,128)(2,1)S(1)}, u32[]{:S(2)}, u32[]{:S(2)}) %collective-permute-start.44) | collective-permute-done | bytes 1114144 | tf_op jit(solution)/shard_map/ppermute | solution.py:322
  350.2 9.6 %branch.1 = (f32[512,1024]{1,0:T(8,128)}, bf16[512,1024]{1,0:T(8,128)(2,1)}, bf16[1024,1152]{1,0:T(8,128)(2,1)}) custom-call(bf16[544,1024]{1,0:T(8,128)(2,1)} %add_convert_fusion.2.mg_ref, f32[512,1024]{1,0:T(8,128)} %get-tuple-element.327.res_ref, bf16[512,1024]{1,0:T(8,128)(2,1)} %get-tuple-element.455.refs_1_.moe_ref, ...), custom_call_target="tpu_custom_call" | custom-call | flops 1048576 | bytes 1048576 | tf_op jit(solution)/shard_map/branch/pallas_call | solution.py:512
  359.8 33.0 %attend_back.1 = (bf16[1024,3328]{1,0:T(8,128)(2,1)}, bf16[512,1024]{1,0:T(8,128)(2,1)}) custom-call(bf16[512,1024]{1,0:T(8,128)(2,1)} %h_ref.5, bf16[1024,2176]{1,0:T(8,128)(2,1)} %copy-done, bf16[1024,2176]{1,0:T(8,128)(2,1)} %copy-done, bf16[1024,2176]{1,0:T(8,128)(2,1)} %copy-done, bf16[1024,2176]{1,0:T(8,128)(2,1)} %copy-done, ...), custom_call_target="tpu_custom_call" | custom-call | flops 1048576 | bytes 1048576 | tf_op jit(solution)/shard_map/attend_back/pallas_call | solution.py:605
  417.9 17.5 %collective-permute-done.55 = bf16[128,3328]{1,0:T(8,128)(2,1)S(1)} collective-permute-done((bf16[128,3328]{1,0:T(8,128)(2,1)S(1)}, bf16[128,3328]{1,0:T(8,128)(2,1)S(1)}, u32[]{:S(2)}, u32[]{:S(2)}) %collective-permute-start.55) | collective-permute-done | bytes 852000 | tf_op jit(solution)/shard_map/ppermute | solution.py:322
  435.4 10.5 %collective-permute-done.53 = bf16[2,3,256,512]{3,2,1,0:T(8,128)(2,1)S(1)} collective-permute-done((bf16[2,3,256,512]{3,2,1,0:T(8,128)(2,1)}, bf16[2,3,256,512]{3,2,1,0:T(8,128)(2,1)S(1)}, u32[]{:S(2)}, u32[]{:S(2)}) %collective-permute-start.53) | collective-permute-done | bytes 1572896 | tf_op jit(solution)/shard_map/ppermute | solution.py:318
  454.6 20.7 %collective-permute-done.61 = bf16[128,3328]{1,0:T(8,128)(2,1)S(1)} collective-permute-done((bf16[128,3328]{1,0:T(8,128)(2,1)S(1)}, bf16[128,3328]{1,0:T(8,128)(2,1)S(1)}, u32[]{:S(2)}, u32[]{:S(2)}) %collective-permute-start.61) | collective-permute-done | bytes 852000 | tf_op jit(solution)/shard_map/ppermute | solution.py:322
  475.3 11.6 %collective-permute-done.59.refs_1_ = bf16[2,3,256,512]{3,2,1,0:T(8,128)(2,1)S(1)} collective-permute-done((bf16[2,3,256,512]{3,2,1,0:T(8,128)(2,1)S(1)}, bf16[2,3,256,512]{3,2,1,0:T(8,128)(2,1)S(1)}, u32[]{:S(2)}, u32[]{:S(2)}) %collective-permute-start.59) | collective-permute-done | bytes 1572896 | tf_op jit(solution)/shard_map/ppermute | solution.py:318
  493.8 18.4 %collective-permute-done.62 = bf16[128,3328]{1,0:T(8,128)(2,1)} collective-permute-done((bf16[128,3328]{1,0:T(8,128)(2,1)}, bf16[128,3328]{1,0:T(8,128)(2,1)}, u32[]{:S(2)}, u32[]{:S(2)}) %collective-permute-start.62) | collective-permute-done | bytes 852000 | tf_op jit(solution)/shard_map/ppermute | solution.py:322
  517.2 13.4 %collective-permute-done.63 = bf16[32,3328]{1,0:T(8,128)(2,1)S(1)} collective-permute-done((bf16[32,3328]{1,0:T(8,128)(2,1)S(1)}, bf16[32,3328]{1,0:T(8,128)(2,1)S(1)}, u32[]{:S(2)}, u32[]{:S(2)}) %collective-permute-start.63) | collective-permute-done | bytes 213024 | tf_op jit(solution)/shard_map/ppermute | solution.py:318
  532.5 5.4 collective-permute-done.65
  544.8 30.2 %collective-permute-done.68.refs_3_ = bf16[2,3,256,512]{3,2,1,0:T(8,128)(2,1)S(1)} collective-permute-done((bf16[2,3,256,512]{3,2,1,0:T(8,128)(2,1)S(1)}, bf16[2,3,256,512]{3,2,1,0:T(8,128)(2,1)S(1)}, u32[]{:S(2)}, u32[]{:S(2)}) %collective-permute-start.68) | collective-permute-done | bytes 1572896 | tf_op jit(solution)/shard_map/ppermute | solution.py:318
  577.9 14.0 %place_all.1 = (f32[4,1024,512]{2,1,0:T(8,128)}, f32[4,1024,512]{2,1,0:T(8,128)}, f32[4,512,1024]{2,1,0:T(8,128)}) custom-call(s32[4]{0:T(128)} %pad_add_fusion.bits_ref, bf16[2,3,256,512]{3,2,1,0:T(8,128)(2,1)} %copy-done.4, bf16[2,3,256,512]{3,2,1,0:T(8,128)(2,1)} %copy-done.11, bf16[2,3,256,512]{3,2,1,0:T(8,128)(2,1)} %copy-done.13, ...), custom_call_target="tpu_custom_call" | custom-call | flops 1048576 | bytes 1048576 | tf_op jit(solution)/shard_map/place_all/pallas_call | solution.py:269
  (299 shorter events, 173.1 us)
Async XLA Ops:
  36.9 26.5 %collective-permute-start.17 = (bf16[512,1024]{1,0:T(8,128)(2,1)}, bf16[512,1024]{1,0:T(8,128)(2,1)}, u32[]{:S(2)}, u32[]{:S(2)}) collective-permute-start(bf16[512,1024]{1,0:T(8,128)(2,1)} %cot_ref.1), channel_id=1, source_target_pairs={{0,2},{1,3},{2,4},{3,5},{4,6},{5,7},{6,0},{7,1},{8,10},{9,11},{10,... | collective-permute-start | bytes 3145736 | tf_op jit(solution)/shard_map/ppermute | solution.py:322
  65.1 34.0 %collective-permute-start.21 = (bf16[512,1024]{1,0:T(8,128)(2,1)}, bf16[512,1024]{1,0:T(8,128)(2,1)}, u32[]{:S(2)}, u32[]{:S(2)}) collective-permute-start(bf16[512,1024]{1,0:T(8,128)(2,1)} %collective-permute-done.17.refs_3_), channel_id=1, source_target_pairs={{0,2},{1,3},{2,4},{3,5},{4,6},{5,7},{6,0},{7,1},{8,10},{9,11},{10,... | collective-permute-start | bytes 3145736 | tf_op jit(solution)/shard_map/ppermute | solution.py:322
  67.6 47.3 %collective-permute-start.22 = (bf16[512,1024]{1,0:T(8,128)(2,1)}, bf16[512,1024]{1,0:T(8,128)(2,1)}, u32[]{:S(2)}, u32[]{:S(2)}) collective-permute-start(bf16[512,1024]{1,0:T(8,128)(2,1)} %cot_ref.1), channel_id=1, source_target_pairs={{0,6},{1,7},{2,0},{3,1},{4,2},{5,3},{6,4},{7,5},{8,14},{9,15},{10,... | collective-permute-start | bytes 3145736 | tf_op jit(solution)/shard_map/ppermute | solution.py:322
  133.0 29.5 %collective-permute-start.29 = (bf16[512,1024]{1,0:T(8,128)(2,1)}, bf16[512,1024]{1,0:T(8,128)(2,1)S(1)}, u32[]{:S(2)}, u32[]{:S(2)}) collective-permute-start(bf16[512,1024]{1,0:T(8,128)(2,1)} %get-tuple-element.455.refs_1_.moe_ref), channel_id=1, source_target_pairs={{0,2},{1,3},{2,4},{3,5},{4,6},{5,7},{6,0},{7,1},{8,10},{9,11},{10,... | collective-permute-start | bytes 3145736 | tf_op jit(solution)/shard_map/ppermute | solution.py:322
  170.6 30.2 %collective-permute-start.33 = (bf16[512,1024]{1,0:T(8,128)(2,1)}, bf16[512,1024]{1,0:T(8,128)(2,1)S(1)}, u32[]{:S(2)}, u32[]{:S(2)}) collective-permute-start(bf16[512,1024]{1,0:T(8,128)(2,1)} %copy-done.20), channel_id=1, source_target_pairs={{0,2},{1,3},{2,4},{3,5},{4,6},{5,7},{6,0},{7,1},{8,10},{9,11},{10,... | collective-permute-start | bytes 3145736 | tf_op jit(solution)/shard_map/ppermute | solution.py:322
  208.9 28.7 %collective-permute-start.37 = (bf16[512,1024]{1,0:T(8,128)(2,1)S(1)}, bf16[512,1024]{1,0:T(8,128)(2,1)}, u32[]{:S(2)}, u32[]{:S(2)}) collective-permute-start(bf16[512,1024]{1,0:T(8,128)(2,1)S(1)} %collective-permute-done.33.refs_1_), channel_id=1, source_target_pairs={{0,2},{1,3},{2,4},{3,5},{4,6},{5,7},{6,0},{7,1},{8,10},{9,11},{10,... | collective-permute-start | bytes 3145736 | tf_op jit(solution)/shard_map/ppermute | solution.py:322
  237.6 33.6 %collective-permute-start.41 = (bf16[544,1024]{1,0:T(8,128)(2,1)S(1)}, bf16[544,1024]{1,0:T(8,128)(2,1)}, u32[]{:S(2)}, u32[]{:S(2)}) collective-permute-start(bf16[544,1024]{1,0:T(8,128)(2,1)S(1)} %add_convert_fusion.7), channel_id=1, source_target_pairs={{0,2},{1,3},{2,4},{3,5},{4,6},{5,7},{6,0},{7,1},{8,10},{9,11},{10,... | collective-permute-start | bytes 3342344 | tf_op jit(solution)/shard_map/ppermute | solution.py:322
  273.9 33.0 %collective-permute-start.43 = (bf16[544,1024]{1,0:T(8,128)(2,1)}, bf16[544,1024]{1,0:T(8,128)(2,1)S(1)}, u32[]{:S(2)}, u32[]{:S(2)}) collective-permute-start(bf16[544,1024]{1,0:T(8,128)(2,1)} %add_convert_fusion.5), channel_id=1, source_target_pairs={{0,2},{1,3},{2,4},{3,5},{4,6},{5,7},{6,0},{7,1},{8,10},{9,11},{10,... | collective-permute-start | bytes 3342344 | tf_op jit(solution)/shard_map/ppermute | solution.py:322
  275.4 33.7 %collective-permute-start.42 = (bf16[544,1024]{1,0:T(8,128)(2,1)}, bf16[544,1024]{1,0:T(8,128)(2,1)}, u32[]{:S(2)}, u32[]{:S(2)}) collective-permute-start(bf16[544,1024]{1,0:T(8,128)(2,1)} %get-tuple-element.447), channel_id=1, source_target_pairs={{0,1},{1,0},{2,3},{3,2},{4,5},{5,4},{6,7},{7,6},{8,9},{9,8},{10,11... | collective-permute-start | bytes 3342344 | tf_op jit(solution)/shard_map/ppermute | solution.py:315
  307.0 85.9 %collective-permute-start.47 = (bf16[2,3,512,512]{3,2,1,0:T(8,128)(2,1)}, bf16[2,3,512,512]{3,2,1,0:T(8,128)(2,1)}, u32[]{:S(2)}, u32[]{:S(2)}) collective-permute-start(bf16[2,3,512,512]{3,2,1,0:T(8,128)(2,1)} %get-tuple-element.463), channel_id=1, source_target_pairs={{0,8},{8,0},{16,24},{24,16},{1,9},{9,1},{17,25},{25,17},{2,10},{10... | collective-permute-start | bytes 9437192 | tf_op jit(solution)/shard_map/ppermute | solution.py:318
  308.2 84.7 %collective-permute-start.48 = (bf16[2,3,512,512]{3,2,1,0:T(8,128)(2,1)}, bf16[2,3,512,512]{3,2,1,0:T(8,128)(2,1)}, u32[]{:S(2)}, u32[]{:S(2)}) collective-permute-start(bf16[2,3,512,512]{3,2,1,0:T(8,128)(2,1)} %get-tuple-element.464), channel_id=1, source_target_pairs={{0,16},{8,24},{16,0},{24,8},{1,17},{9,25},{17,1},{25,9},{2,18},{10... | collective-permute-start | bytes 9437192 | tf_op jit(solution)/shard_map/ppermute | solution.py:318
  311.0 28.8 %collective-permute-start.44 = (bf16[544,1024]{1,0:T(8,128)(2,1)S(1)}, bf16[544,1024]{1,0:T(8,128)(2,1)S(1)}, u32[]{:S(2)}, u32[]{:S(2)}) collective-permute-start(bf16[544,1024]{1,0:T(8,128)(2,1)S(1)} %add_convert_fusion.3), channel_id=1, source_target_pairs={{0,2},{1,3},{2,4},{3,5},{4,6},{5,7},{6,0},{7,1},{8,10},{9,11},{10,... | collective-permute-start | bytes 3342344 | tf_op jit(solution)/shard_map/ppermute | solution.py:322
  341.3 51.6 %collective-permute-start.46 = (bf16[512,1024]{1,0:T(8,128)(2,1)S(1)}, bf16[512,1024]{1,0:T(8,128)(2,1)S(1)}, u32[]{:S(2)}, u32[]{:S(2)}) collective-permute-start(bf16[512,1024]{1,0:T(8,128)(2,1)S(1)} %add_convert_fusion.15), channel_id=1, source_target_pairs={{0,2},{1,3},{2,4},{3,5},{4,6},{5,7},{6,0},{7,1},{8,10},{9,11},{10,... | collective-permute-start | bytes 3145736 | tf_op jit(solution)/shard_map/ppermute | solution.py:322
  409.0 37.0 %collective-permute-start.53 = (bf16[2,3,256,512]{3,2,1,0:T(8,128)(2,1)}, bf16[2,3,256,512]{3,2,1,0:T(8,128)(2,1)S(1)}, u32[]{:S(2)}, u32[]{:S(2)}) collective-permute-start(bf16[2,3,256,512]{3,2,1,0:T(8,128)(2,1)} %get-tuple-element.485), channel_id=1, source_target_pairs={{0,16},{8,24},{16,0},{24,8},{1,17},{9,25},{17,1},{25,9},{2,18},{10... | collective-permute-start | bytes 4718600 | tf_op jit(solution)/shard_map/ppermute | solution.py:318
  410.2 36.7 %collective-permute-start.54 = (bf16[2,3,256,512]{3,2,1,0:T(8,128)(2,1)}, bf16[2,3,256,512]{3,2,1,0:T(8,128)(2,1)S(1)}, u32[]{:S(2)}, u32[]{:S(2)}) collective-permute-start(bf16[2,3,256,512]{3,2,1,0:T(8,128)(2,1)} %get-tuple-element.486), channel_id=1, source_target_pairs={{0,8},{8,0},{16,24},{24,16},{1,9},{9,1},{17,25},{25,17},{2,10},{10... | collective-permute-start | bytes 4718600 | tf_op jit(solution)/shard_map/ppermute | solution.py:318
  451.2 35.7 %collective-permute-start.59 = (bf16[2,3,256,512]{3,2,1,0:T(8,128)(2,1)S(1)}, bf16[2,3,256,512]{3,2,1,0:T(8,128)(2,1)S(1)}, u32[]{:S(2)}, u32[]{:S(2)}) collective-permute-start(bf16[2,3,256,512]{3,2,1,0:T(8,128)(2,1)S(1)} %add_convert_fusion.1.refs_0_), channel_id=1, source_target_pairs={{0,16},{8,24},{16,0},{24,8},{1,17},{9,25},{17,1},{25,9},{2,18},{10... | collective-permute-start | bytes 4718600 | tf_op jit(solution)/shard_map/ppermute | solution.py:318
  452.1 36.0 %collective-permute-start.60 = (bf16[2,3,256,512]{3,2,1,0:T(8,128)(2,1)S(1)}, bf16[2,3,256,512]{3,2,1,0:T(8,128)(2,1)}, u32[]{:S(2)}, u32[]{:S(2)}) collective-permute-start(bf16[2,3,256,512]{3,2,1,0:T(8,128)(2,1)S(1)} %add_convert_fusion.refs_4_), channel_id=1, source_target_pairs={{0,8},{8,0},{16,24},{24,16},{1,9},{9,1},{17,25},{25,17},{2,10},{10... | collective-permute-start | bytes 4718600 | tf_op jit(solution)/shard_map/ppermute | solution.py:318
  491.5 46.3 %collective-permute-start.66 = (bf16[2,3,256,512]{3,2,1,0:T(8,128)(2,1)S(1)}, bf16[2,3,256,512]{3,2,1,0:T(8,128)(2,1)S(1)}, u32[]{:S(2)}, u32[]{:S(2)}) collective-permute-start(bf16[2,3,256,512]{3,2,1,0:T(8,128)(2,1)S(1)} %add_convert_fusion.1.refs_0_), channel_id=1, source_target_pairs={{0,8},{8,0},{16,24},{24,16},{1,9},{9,1},{17,25},{25,17},{2,10},{10... | collective-permute-start | bytes 4718600 | tf_op jit(solution)/shard_map/ppermute | solution.py:318
  492.4 45.4 %collective-permute-start.67 = (bf16[2,3,256,512]{3,2,1,0:T(8,128)(2,1)S(1)}, bf16[2,3,256,512]{3,2,1,0:T(8,128)(2,1)S(1)}, u32[]{:S(2)}, u32[]{:S(2)}) collective-permute-start(bf16[2,3,256,512]{3,2,1,0:T(8,128)(2,1)S(1)} %add_convert_fusion.refs_4_), channel_id=1, source_target_pairs={{0,16},{8,24},{16,0},{24,8},{1,17},{9,25},{17,1},{25,9},{2,18},{10... | collective-permute-start | bytes 4718600 | tf_op jit(solution)/shard_map/ppermute | solution.py:318
  537.9 37.1 %collective-permute-start.68 = (bf16[2,3,256,512]{3,2,1,0:T(8,128)(2,1)S(1)}, bf16[2,3,256,512]{3,2,1,0:T(8,128)(2,1)S(1)}, u32[]{:S(2)}, u32[]{:S(2)}) collective-permute-start(bf16[2,3,256,512]{3,2,1,0:T(8,128)(2,1)S(1)} %copy-done.12), channel_id=1, source_target_pairs={{0,8},{8,0},{16,24},{24,16},{1,9},{9,1},{17,25},{25,17},{2,10},{10... | collective-permute-start | bytes 4718600 | tf_op jit(solution)/shard_map/ppermute | solution.py:318
  538.4 39.4 %collective-permute-start.69 = (bf16[2,3,256,512]{3,2,1,0:T(8,128)(2,1)}, bf16[2,3,256,512]{3,2,1,0:T(8,128)(2,1)}, u32[]{:S(2)}, u32[]{:S(2)}) collective-permute-start(bf16[2,3,256,512]{3,2,1,0:T(8,128)(2,1)} %collective-permute-done.60.refs_5_), channel_id=1, source_target_pairs={{0,16},{8,24},{16,0},{24,8},{1,17},{9,25},{17,1},{25,9},{2,18},{10... | collective-permute-start | bytes 4718600 | tf_op jit(solution)/shard_map/ppermute | solution.py:318
  541.8 50.8 %collective-permute-start.74 = (bf16[512,1024]{1,0:T(8,128)(2,1)}, bf16[512,1024]{1,0:T(8,128)(2,1)}, u32[]{:S(2)}, u32[]{:S(2)}) collective-permute-start(bf16[512,1024]{1,0:T(8,128)(2,1)} %add_convert_fusion.10), channel_id=1, source_target_pairs={{0,2},{1,3},{2,4},{3,5},{4,6},{5,7},{6,0},{7,1},{8,10},{9,11},{10,... | collective-permute-start | bytes 3145736 | tf_op jit(solution)/shard_map/ppermute | solution.py:322
  543.2 48.6 %collective-permute-start.70 = (bf16[32,3328]{1,0:T(8,128)(2,1)S(1)}, bf16[32,3328]{1,0:T(8,128)(2,1)S(1)}, u32[]{:S(2)}, u32[]{:S(2)}) collective-permute-start(bf16[32,3328]{1,0:T(8,128)(2,1)S(1)} %add_convert_fusion.23.refs_0_), channel_id=1, source_target_pairs={{0,8},{8,0},{16,24},{24,16},{1,9},{9,1},{17,25},{25,17},{2,10},{10... | collective-permute-start | bytes 638984 | tf_op jit(solution)/shard_map/ppermute | solution.py:318
  543.4 48.5 %collective-permute-start.71 = (bf16[32,3328]{1,0:T(8,128)(2,1)S(1)}, bf16[32,3328]{1,0:T(8,128)(2,1)S(1)}, u32[]{:S(2)}, u32[]{:S(2)}) collective-permute-start(bf16[32,3328]{1,0:T(8,128)(2,1)S(1)} %add_convert_fusion.23.refs_0_), channel_id=1, source_target_pairs={{0,16},{8,24},{16,0},{24,8},{1,17},{9,25},{17,1},{25,9},{2,18},{10... | collective-permute-start | bytes 638984 | tf_op jit(solution)/shard_map/ppermute | solution.py:318
  (87 other events, 1008.2 us)

commit v4 on v3

--- a/solution.py
+++ b/solution.py
@@ -231,7 +231,7 @@
     )(bit, keep, got)
 
 
-def place_kernel(counts, bits_ref, *refs):
+def place_early_kernel(counts, bits_ref, *refs):
     ins, (gg_ref, gu_ref, gd_ref) = refs[:-3], refs[-3:]
     e = pl.program_id(0)
     begin = 0
@@ -239,11 +239,11 @@
 
         @pl.when((e >= begin) & (e < begin + many))
         def _(n=n):
-            for i in range(4):
-                q_ref = ins[4 * n + i]
+            for i in range(3):
+                q_ref = ins[3 * n + i]
                 rows, half = q_ref.shape[2:]
-                one = bits_ref[2 * n] if i < 2 else 1 - bits_ref[2 * n]
-                two = bits_ref[2 * n + 1] if i % 2 == 0 else 1 - bits_ref[2 * n + 1]
+                one = bits_ref[e, 0] if i < 2 else 1 - bits_ref[e, 0]
+                two = bits_ref[e, 1] if i % 2 == 0 else 1 - bits_ref[e, 1]
                 at = pl.ds(pl.multiple_of((2 * one + two) * rows, rows), rows)
                 gg_ref[0, at, :] = q_ref[0, 0].astype(F32)
                 gu_ref[0, at, :] = q_ref[0, 1].astype(F32)
@@ -254,31 +254,55 @@
         begin += many
 
 
-def place_all(bits, quarters):
+def place_late_kernel(counts, bits_ref, *refs):
+    n = len(counts)
+    ins, outs = refs[:n], refs[n + 3 :]
+    e = pl.program_id(0)
+    begin = 0
+    for q_ref, many in zip(ins, counts):
+
+        @pl.when((e >= begin) & (e < begin + many))
+        def _(q_ref=q_ref):
+            for i, o_ref in enumerate(outs):
+                o_ref[0] = q_ref[0, i].astype(F32)
+
+        begin += many
+
+
+def place(bits, quarters, held=None):
     counts = [q[0].shape[0] for q in quarters]
     owned = sum(counts)
     _, _, rows, F = quarters[0][0].shape
     D = 4 * rows
     specs = []
     begin = 0
-    for many in counts:
+    for many, group in zip(counts, quarters):
         block = lambda e, b, begin=begin, many=many: (jnp.clip(e - begin, 0, many - 1), 0, 0, 0)
-        specs += [pl.BlockSpec((1, 3, rows, F), block)] * 4
+        specs += [pl.BlockSpec((1, 3, rows, F), block)] * len(group)
         begin += many
     shapes = [(D, F), (D, F), (F, D)]
+    if held is None:
+        kernel = place_early_kernel
+        outs = [pl.BlockSpec((1,) + s, lambda e, b: (e, 0, 0)) for s in shapes]
+        aliases = {}
+    else:
+        kernel = place_late_kernel
+        tall = pl.BlockSpec((1, rows, F), lambda e, b: (e, 3 - 2 * b[e, 0] - b[e, 1], 0))
+        wide = pl.BlockSpec((1, rows, F), lambda e, b: (e, 1 - b[e, 1], 1 - b[e, 0]))
+        outs = [tall, tall, wide]
+        aliases = {1 + len(specs) + i: i for i in range(3)}
+        specs = specs + [pl.BlockSpec(memory_space=pl.ANY)] * 3
     return pl.pallas_call(
-        functools.partial(place_kernel, counts),
+        functools.partial(kernel, counts),
         grid_spec=pltpu.PrefetchScalarGridSpec(
-            num_scalar_prefetch=1,
-            grid=(owned,),
-            in_specs=specs,
-            out_specs=[pl.BlockSpec((1,) + s, lambda e, b: (e, 0, 0)) for s in shapes],
+            num_scalar_prefetch=1, grid=(owned,), in_specs=specs, out_specs=outs
         ),
         out_shape=[jax.ShapeDtypeStruct((owned,) + s, F32) for s in shapes],
+        input_output_aliases=aliases,
         compiler_params=pltpu.CompilerParams(vmem_limit_bytes=60 << 20),
         cost_estimate=COST,
-        name="place_all",
-    )(bits, *[q for group in quarters for q in group])
+        name="place_early" if held is None else "place_late",
+    )(bits, *[q for group in quarters for q in group], *(held or ()))
 
 
 def assemble_kernel(place,p_ref,*refs):
@@ -522,11 +546,13 @@
 def fold(v):
     return v+pltpu.roll(v,2*HALF,1)
 
-def attend_back_kernel(gain_at,h_ref,misc_ref,wq_ref,wk_ref,wv_ref,cos_ref,sin_ref,segc_ref,segr_ref,
+def attend_back_kernel(gain_at,pos_ref,h_ref,misc_ref,wq_ref,wk_ref,wv_ref,cos_ref,sin_ref,segc_ref,segr_ref,
                        q_ref,k_ref,v_ref,dm_ref,lse_ref,dres_ref,og_ref,
-                       out_ref,gin_ref,x_s,bias_s,da_s):
+                       own_ref,other_ref,gin_ref,x_s,bias_s,da_s,out_s,sem):
     T,D=h_ref.shape
     step=pl.program_id(0)
+    def put(column,value):
+        out_s[:,pl.ds(column,value.shape[1])]=value
     @pl.when(step==0)
     def _():
         inputs=h_ref[...].astype(F32)
@@ -535,7 +561,7 @@
         r=lax.broadcasted_iota(jnp.int32,(T,T),0); c=lax.broadcasted_iota(jnp.int32,(T,T),1)
         bias_s[...]=jnp.where((segc_ref[...]==segr_ref[...])&(r<=c),0.0,-1e30)
         wide=og_ref.shape[1]
-        out_ref[:,out_ref.shape[1]-128-wide:out_ref.shape[1]-128]=og_ref[...]
+        put(out_s.shape[1]-128-wide,og_ref[...])
     cos=cos_ref[...]; sin=sin_ref[...]
     kp=spread(k_ref[...].astype(F32)); vp=spread(v_ref[...].astype(F32))
     low=lax.broadcasted_iota(jnp.int32,(T,128),1)<2*HALF
@@ -574,9 +600,9 @@
     dql=jnp.concatenate(dq_all,axis=1)
     x=x_s[...]
     base=pl.multiple_of(step*512,512)
-    out_ref[:,pl.ds(base,256)]=dot(x,dql,0,0).astype(BF)
-    out_ref[:,pl.ds(base+256,128)]=dot(x,dkl,0,0).astype(BF)
-    out_ref[:,pl.ds(base+384,128)]=dot(x,dvl,0,0).astype(BF)
+    put(base,dot(x,dql,0,0).astype(BF))
+    put(base+256,dot(x,dkl,0,0).astype(BF))
+    put(base+384,dot(x,dvl,0,0).astype(BF))
     da=dot(dql,wq_ref[...],1,1)+dot(dkl,wk_ref[...],1,1)+dot(dvl,wv_ref[...],1,1)
     @pl.when(step==0)
     def _():
@@ -592,28 +618,44 @@
         scaled=dattn*gain_row(misc_ref,gain_at)
         grad_gain=jnp.sum(dattn*inputs*inv,axis=0,keepdims=True)
         gin_ref[...]=(dres_ref[...]+inv*scaled-inputs*(inv*inv*inv*jnp.mean(scaled*inputs,axis=-1,keepdims=True))).astype(BF)
-        out_ref[:,out_ref.shape[1]-128:]=jnp.broadcast_to(grad_gain,(128,D)).T.astype(BF)
-
-def attend_back(gain_at,h,w,cos,sin,segc,segr,q,k,v,dmix,lse,dres,og):
+        put(out_s.shape[1]-128,jnp.broadcast_to(grad_gain,(128,D)).T.astype(BF))
+        n=pos_ref.shape[0]
+        span=D//n
+        def copy(j,ref,at):
+            rows=pl.ds(pl.multiple_of(at*span,span),span)
+            return pltpu.make_async_copy(out_s.at[j*span:(j+1)*span,:],ref.at[rows,:],sem.at[j])
+        for go in (True,False):
+            for j in range(n):
+                for ref,first in ((own_ref,0),(other_ref,n//2)):
+                    @pl.when((pos_ref[j]>=first)&(pos_ref[j]<first+n//2))
+                    def _(j=j,ref=ref,first=first):
+                        c=copy(j,ref,pos_ref[j]-first)
+                        if go:
+                            c.start()
+                        else:
+                            c.wait()
+
+def attend_back(pos,gain_at,h,w,cos,sin,segc,segr,q,k,v,dmix,lse,dres,og):
     T,D=h.shape
     kvw=k.shape[1]
     steps=lse.shape[0]
-    full=lambda g:(0,0)
+    full=lambda g,_:(0,0)
     kb=D//128; vb=kb+kvw//128
     wide=og.shape[1]
     width=D+2*kvw+wide+128
-    return pl.pallas_call(functools.partial(attend_back_kernel,gain_at),grid=(steps,),
-        in_specs=[pl.BlockSpec((T,D),full),pl.BlockSpec((D,128),lambda g:(0,MISC)),
-                  pl.BlockSpec((D,256),lambda g:(0,g)),pl.BlockSpec((D,128),lambda g:(0,kb+g)),pl.BlockSpec((D,128),lambda g:(0,vb+g)),
+    return pl.pallas_call(functools.partial(attend_back_kernel,gain_at),
+        grid_spec=pltpu.PrefetchScalarGridSpec(num_scalar_prefetch=1,grid=(steps,),
+        in_specs=[pl.BlockSpec((T,D),full),pl.BlockSpec((D,128),lambda g,_:(0,MISC)),
+                  pl.BlockSpec((D,256),lambda g,_:(0,g)),pl.BlockSpec((D,128),lambda g,_:(0,kb+g)),pl.BlockSpec((D,128),lambda g,_:(0,vb+g)),
                   pl.BlockSpec((T,128),full),pl.BlockSpec((T,128),full),pl.BlockSpec((T,1),full),pl.BlockSpec((1,T),full),
-                  pl.BlockSpec((T,256),lambda g:(0,g)),pl.BlockSpec((T,128),lambda g:(0,g)),pl.BlockSpec((T,128),lambda g:(0,g)),
-                  pl.BlockSpec((T,256),lambda g:(0,g)),pl.BlockSpec((1,8,T),lambda g:(g,0,0)),pl.BlockSpec((T,D),full),pl.BlockSpec((D,wide),full)],
-        out_specs=[pl.BlockSpec((D,width),full),pl.BlockSpec((T,D),full)],
-        out_shape=[jax.ShapeDtypeStruct((D,width),BF),jax.ShapeDtypeStruct((T,D),BF)],
-        scratch_shapes=[pltpu.VMEM((T,D),BF),pltpu.VMEM((T,T),F32),pltpu.VMEM((T,D),F32)],
+                  pl.BlockSpec((T,256),lambda g,_:(0,g)),pl.BlockSpec((T,128),lambda g,_:(0,g)),pl.BlockSpec((T,128),lambda g,_:(0,g)),
+                  pl.BlockSpec((T,256),lambda g,_:(0,g)),pl.BlockSpec((1,8,T),lambda g,_:(g,0,0)),pl.BlockSpec((T,D),full),pl.BlockSpec((D,wide),full)],
+        out_specs=[pl.BlockSpec(memory_space=pl.ANY)]*2+[pl.BlockSpec((T,D),full)],
+        scratch_shapes=[pltpu.VMEM((T,D),BF),pltpu.VMEM((T,T),F32),pltpu.VMEM((T,D),F32),pltpu.VMEM((D,width),BF),pltpu.SemaphoreType.DMA((pos.shape[0],))]),
+        out_shape=[jax.ShapeDtypeStruct((D//2,width),BF)]*2+[jax.ShapeDtypeStruct((T,D),BF)],
         compiler_params=pltpu.CompilerParams(vmem_limit_bytes=60<<20),
         cost_estimate=COST,
-        name="attend_back")(h,w,w,w,w,cos,sin,segc,segr,q,k,v,dmix,lse,dres,og)
+        name="attend_back")(pos,h,w,w,w,w,cos,sin,segc,segr,q,k,v,dmix,lse,dres,og)
 
 def rope_tables(segment_row):
     index = jnp.arange(segment_row.shape[0], dtype=jnp.int32)
@@ -658,6 +700,7 @@
     chip_order = (me // 2 - jnp.arange(chips, dtype=jnp.int32)) % chips
     core_order = (me % 2) ^ jnp.arange(2, dtype=jnp.int32)
     order = (chip_order[:, None] * 2 + core_order[None, :]).reshape(-1)
+    slot_of = jnp.argsort(order.reshape(chips, 2).T.reshape(-1))
     dp_count = lax.axis_size("dp")
     dp_order = lax.axis_index("dp") ^ jnp.arange(dp_count, dtype=jnp.int32)
     places = (
@@ -710,9 +753,9 @@
     cosine, sine = rope_tables(segment_row)
     segment_column = segment_row[:, None]
     segment_line = segment_row[None, :]
-    tables = [rank_rows, keys, member_all, member_line, cosine, sine]
+    tables = [rank_rows, keys, member_all, member_line, cosine, sine, slot_of]
     tables, slices_one, stack_two = tie(tables, slices_one, stack_two)
-    rank_rows, keys, member_all, member_line, cosine, sine = tables
+    rank_rows, keys, member_all, member_line, cosine, sine, slot_of = tables
     pieces_one = []
     for s in slices_one:
         pieces_one += [s, swap_pair(s)]
@@ -732,8 +775,8 @@
     pieces_two = []
     for s in slices_two:
         pieces_two += [s, swap_pair(s)]
-    d = [cotangent_steps[0], swap_pair(cotangent_steps[0])]
-    mixed, pieces_two, d = tie(mixed, pieces_two, d)
+    d_pairs = [swap_pair(c) for c in cotangent_steps[:2]]
+    mixed, pieces_two, d_pairs = tie(mixed, pieces_two, d_pairs)
     out_weights = assemble(places, pieces_two)
     residual, moe_in = project(1, mixed, out_weights, hidden, attn_weights)
     x = [moe_in, swap_pair(moe_in)]
@@ -742,16 +785,24 @@
     grad_parts = []
     out_parts = []
     hop = None
+
+    def sum_of(*terms):
+        total = terms[0].astype(F32)
+        for t in terms[1:]:
+            total = total + t.astype(F32)
+        return total.astype(BF)
+
     for k in range(chips):
         following = shift_chips(x[0], 1) if k + 1 < chips else None
+        later = swap_pair(cotangent_steps[k + 2]) if k + 2 < chips else None
         if k == 3:
-            hop = shift_chips(grad_parts[1], 1)
+            hop = shift_chips(sum_of(*grad_parts[1]), 1)
         outs = list(
             expert_step(
                 k,
                 first_expert[None],
                 x,
-                d,
+                (cotangent_steps[k], d_pairs[k]),
                 out_weights,
                 member_all,
                 rank_rows,
@@ -764,17 +815,14 @@
         )
         kept = outs[4:]
         outs = outs[:4]
-        outs, kept, following, hop, grad_parts, out_parts = tie(
-            outs, kept, following, hop, grad_parts, out_parts
+        outs, kept, following, hop, later, grad_parts, out_parts = tie(
+            outs, kept, following, hop, later, grad_parts, out_parts
         )
+        d_pairs.append(later)
         if following is not None:
             x = [following, swap_pair(following)]
-            d = [cotangent_steps[k + 1], swap_pair(cotangent_steps[k + 1])]
-        grad_part = (outs[0].astype(F32) + swap_pair(outs[1]).astype(F32)).astype(BF)
+        grad_parts = grad_parts + [(outs[0], swap_pair(outs[1]))]
         out_parts = out_parts + [(outs[2], outs[3])]
-        if k + 1 < chips:
-            x, d, grad_part = tie(x, d, grad_part)
-        grad_parts = grad_parts + [grad_part]
     dp_me = lax.axis_index("dp")
     low = dp_me % 2
     high = dp_me // 2
@@ -782,11 +830,9 @@
     plans = [(0, count, 1, 2, low, high)]
     if owned > count:
         plans.append((count, owned - count, 2, 1, high, low))
-    total = grad_parts[1]
-    first_hop = 2
-    if hop is not None:
-        total, kept = tie((grad_parts[2].astype(F32) + hop.astype(F32)).astype(BF), kept)
-        first_hop = 3
+    first_hop = 2 if hop is None else 3
+    total = sum_of(*grad_parts[first_hop - 1], *([] if hop is None else [hop]))
+    total, kept = tie(total, kept)
     moved = shift_chips(total, 1)
     halves = []
     sends = []
@@ -797,15 +843,16 @@
     moved, sends = tie(moved, sends)
     gots = [swap_dp(send, h[1]) for h, send in zip(halves, sends)]
     for k in range(first_hop, chips):
-        moved = shift_chips((grad_parts[k].astype(F32) + moved.astype(F32)).astype(BF), 1)
-    moe_grad = (grad_parts[0].astype(F32) + moved.astype(F32)).astype(BF)
+        moved = shift_chips(sum_of(*grad_parts[k], moved), 1)
+    moe_grad = sum_of(*grad_parts[0], moved)
     out_sum = (out_parts[1][0].astype(F32) + swap_pair(out_parts[1][1]).astype(F32)).astype(BF)
     moe_grad, out_sum = tie(moe_grad, out_sum)
     grad_residual, mixed_gradient, out_grads = branch(
         1, moe_grad, residual, moe_in, mixed, cotangent, out_weights, attn_weights, member_line
     )
     out_sum = shift_chips(out_sum, 1)
-    attn_grads, grad_input = attend_back(
+    own_half, other_half, grad_input = attend_back(
+        slot_of,
         0,
         hidden,
         attn_weights,
@@ -821,11 +868,9 @@
         grad_residual,
         out_grads,
     )
-    attn_grads, out_sum, gots, out_parts = tie(attn_grads, out_sum, gots, out_parts)
-
-    def block_for(k, b):
-        number = chip_order[k] * 2 + core_order[b]
-        return lax.dynamic_slice_in_dim(attn_grads, number * own_rows, own_rows, 0)
+    own_half, other_half, out_sum, gots, out_parts = tie(
+        own_half, other_half, out_sum, gots, out_parts
+    )
 
     seconds = []
     keeps = []
@@ -833,9 +878,15 @@
         send, keep = halve(bit_two[None], keep, got)
         seconds.append(send)
         keeps.append(keep)
-    parts = [(block_for(k, 0), swap_pair(block_for(k, 1))) for k in range(chips)]
+    parts = [own_half, swap_pair(other_half)]
     seconds, keeps, parts, out_parts = tie(seconds, keeps, parts, out_parts)
-    parts = [(a.astype(F32) + b.astype(F32)).astype(BF) for a, b in parts]
+    parts = [
+        (
+            parts[0][k * own_rows : (k + 1) * own_rows].astype(F32)
+            + parts[1][k * own_rows : (k + 1) * own_rows].astype(F32)
+        ).astype(BF)
+        for k in range(chips)
+    ]
     gots = [swap_dp(send, h[2]) for h, send in zip(halves, seconds)]
     running = shift_chips(parts[1], 1)
     out_parts = [(a.astype(F32) + swap_pair(b).astype(F32)).astype(BF) for a, b in out_parts]
@@ -870,12 +921,12 @@
     pieces = [swap_dp(total, r) if r else total for r in range(dp_count)]
     for o in out_parts[3:]:
         out_sum = shift_chips((o.astype(F32) + out_sum.astype(F32)).astype(BF), 1)
-    big = place_all(
-        jnp.stack([b for h in halves for b in h[3:5]]),
-        list(zip(mine, others, thirds, fourths)),
-    )
-    big, pieces, out_sum = tie(big, pieces, out_sum)
     result = (residual + out_parts[0].astype(F32) + out_sum.astype(F32)).astype(BF)
+    bits = jnp.stack([jnp.stack(h[3:5]) for h in halves for _ in range(h[5].shape[0])])
+    big = place(bits, list(zip(mine, others, thirds)))
+    big, fourths, result = tie(big, fourths, result)
+    big = place(bits, [(f,) for f in fourths], big)
+    big, pieces = tie(big, pieces)
     share = place_share(
         jnp.stack([rows_of(r) for r in range(dp_count)]), pieces, width, key_weight.shape[1]
     )

time: 607 us -> 578 us (0.952)
  waiting for transfers between devices: 219 us -> 191 us
  between operations: 9.45 us -> 1.68 us
  Pallas kernels: 242 us -> 249 us
    ppermute x22, waiting for transfers between devices: 86.4 us -> 58.9 us  [swap_dp(): lax.ppermute(v, 'dp', [(i, i ^ r) for i in range(lax.axis_size('dp'))])]
    unnamed x83 -> x89, local copies, waits for them, and re-layouts: 14.9 us -> 21.4 us
    pallas_call x2 -> x3, Pallas kernels: 47 us -> 52.5 us  [the longest x1 34.3 us: attend_back(): pl.pallas_call(functools.partial(attend_back_kernel, gain_at), grid_spec=...]
    convert_element_type x7 -> x5, other arithmetic: 12.4 us -> 8.96 us  [the longest x4 7.61 us: sum_of(): return total.astype(BF)]
    ppermute x32 -> x29, waiting for transfers between devices: 17.8 us -> 16.4 us  [swap_pair(): lax.ppermute(v, 'expert', [(i, i ^ 1) for i in range(lax.axis_size('exper...]
  transfers between devices with their start and end apart: 75 -> 72, of which waited for: 32 -> 29; matrix products, arithmetic and copies ran while one was open for 6% -> 6% of each run, Pallas kernels for 38% -> 42%
where the time goes in v4:
time: 578 us; the launch traced here: 570 us
  Pallas kernels  249 us (43%)
  waiting for transfers between devices  191 us (33%)
  starting transfers between devices  61.4 us (11%)
  other arithmetic  34.3 us (6%)
  local copies, waits for them, and re-layouts  29 us (5%)
    ppermute x21, waiting for transfers between devices, shift_chips(): return lax.ppermute(v, 'expert', [(i, (i + 2 * k) % n) for i in range(n)])  116 us
    pallas_call x4, Pallas kernels, expert_step(): pl.pallas_call(functools.partial(step_kernel, aliased), grid_spec=pltpu.P...  110 us
    ppermute x22, waiting for transfers between devices, swap_dp(): lax.ppermute(v, 'dp', [(i, i ^ r) for i in range(lax.axis_size('dp'))])  58.9 us
    pallas_call x1, Pallas kernels, attend_back(): pl.pallas_call(functools.partial(attend_back_kernel, gain_at), grid_spec=...  34.3 us
    pallas_call x2, Pallas kernels, weight_grads(): pl.pallas_call(functools.partial(weight_kernel, parts), grid_spec=pltpu.P...  31.3 us
    ppermute x21, starting transfers between devices, shift_chips(): return lax.ppermute(v, 'expert', [(i, (i + 2 * k) % n) for i in range(n)])  28.8 us
    ppermute x22, starting transfers between devices, swap_dp(): lax.ppermute(v, 'dp', [(i, i ^ r) for i in range(lax.axis_size('dp'))])  26.1 us
    unnamed x89, local copies, waits for them, and re-layouts  21.4 us
  transfers between devices with their start and end apart: 72, of which 29 were waited for; matrix products, arithmetic and copies ran while one was open for 6% of the time, Pallas kernels for 42%

profile of v4, /device:TPU:0, one launch (start us, length us, event | category | flops | bytes accessed | tf_op | source)
XLA Modules:
  0.0 570.1 jit_solution(12537557096164371437)
XLA Ops:
  16.5 8.7 %collective-permute-done.3 = bf16[32,128]{1,0:T(8,128)(2,1)S(1)} collective-permute-done((bf16[32,128]{1,0:T(8,128)(2,1)S(1)}, bf16[32,128]{1,0:T(8,128)(2,1)S(1)}, u32[]{:S(2)}, u32[]{:S(2)}) %collective-permute-start.3) | collective-permute-done | bytes 8224 | tf_op jit(solution)/shard_map/ppermute | solution.py:346
  48.3 12.3 %collective-permute-done.11.refs_4_ = bf16[4,32,2176]{2,1,0:T(8,128)(2,1)S(1)} collective-permute-done((bf16[4,32,2176]{2,1,0:T(8,128)(2,1)S(1)}, bf16[4,32,2176]{2,1,0:T(8,128)(2,1)S(1)}, u32[]{:S(2)}, u32[]{:S(2)}) %collective-permute-start.11) | collective-permute-done | bytes 557088 | tf_op jit(solution)/shard_map/ppermute | solution.py:342
  73.1 7.6 %assemble.2.misc_ref.wq_ref.wk_ref.wv_ref = bf16[1024,2176]{1,0:T(8,128)(2,1)S(1)} custom-call(s32[32]{0:T(128)S(1)} %add.189.p_ref, bf16[4,32,2176]{2,1,0:T(8,128)(2,1)S(1)} %slice.40.refs_0_, bf16[4,32,2176]{2,1,0:T(8,128)(2,1)S(1)} %collective-permute-done.13.refs_1_, bf16[4,32,2176]{2,1,0:T(8,128)(2,1)S(1)} %collective-permute-done.10.refs_2_, ...), custom_call_target="tpu_custom_call" | custom-call | flops 1048576 | bytes 1048576 | tf_op jit(solution)/shard_map/assemble/pallas_call | solution.py:321
  87.2 17.2 %attend.1 = (bf16[512,1024]{1,0:T(8,128)(2,1)}, bf16[512,512]{1,0:T(8,128)(2,1)}, bf16[512,512]{1,0:T(8,128)(2,1)}, bf16[512,1024]{1,0:T(8,128)(2,1)}, f32[4,8,512]{2,1,0:T(8,128)}) custom-call(bf16[512,1024]{1,0:T(8,128)(2,1)} %h_ref.5, bf16[1024,2176]{1,0:T(8,128)(2,1)} %copy-done, bf16[1024,2176]{1,0:T(8,128)(2,1)} %copy-done, ...), custom_call_target="tpu_custom_call" | custom-call | flops 1048576 | bytes 1048576 | tf_op jit(solution)/shard_map/attend/pallas_call | solution.py:472
  104.5 11.1 %collective-permute-done.22.refs_3_ = bf16[512,1024]{1,0:T(8,128)(2,1)} collective-permute-done((bf16[512,1024]{1,0:T(8,128)(2,1)}, bf16[512,1024]{1,0:T(8,128)(2,1)}, u32[]{:S(2)}, u32[]{:S(2)}) %collective-permute-start.22) | collective-permute-done | bytes 1048608 | tf_op jit(solution)/shard_map/ppermute | solution.py:346
  128.6 4.9 project.1
  138.8 27.5 %expert_step.4 = (bf16[544,1024]{1,0:T(8,128)(2,1)}, bf16[544,1024]{1,0:T(8,128)(2,1)}, bf16[512,1024]{1,0:T(8,128)(2,1)}, bf16[512,1024]{1,0:T(8,128)(2,1)}, bf...) custom-call(s32[1]{0:T(128)} %bitcast.4.refs_0_, ...), custom_call_target="tpu_custom_call" | custom-call | flops 1048576 | bytes 1048576 | tf_op jit(solution)/shard_map/expert_step/pallas_call | solution.py:126
  172.1 27.5 %expert_step.5 = (bf16[544,1024]{1,0:T(8,128)(2,1)}, bf16[544,1024]{1,0:T(8,128)(2,1)}, bf16[512,1024]{1,0:T(8,128)(2,1)}, bf16[512,1024]{1,0:T(8,128)(2,1)}, bf...) custom-call(s32[1]{0:T(128)} %bitcast.4.refs_0_, ...), custom_call_target="tpu_custom_call", output_to_operand_aliasing={{4}: (12, {}), {5}: (13, {}), {6}: (14, {}), {7}: (15, {}),... | custom-call | flops 1048576 | bytes 1048576 | tf_op jit(solution)/shard_map/expert_step/pallas_call | solution.py:126
  205.2 27.5 %expert_step.6 = (bf16[544,1024]{1,0:T(8,128)(2,1)}, bf16[544,1024]{1,0:T(8,128)(2,1)}, bf16[512,1024]{1,0:T(8,128)(2,1)}, bf16[512,1024]{1,0:T(8,128)(2,1)}, bf...) custom-call(s32[1]{0:T(128)} %bitcast.4.refs_0_, ...), custom_call_target="tpu_custom_call", output_to_operand_aliasing={{4}: (12, {}), {5}: (13, {}), {6}: (14, {}), {7}: (15, {}),... | custom-call | flops 1048576 | bytes 1048576 | tf_op jit(solution)/shard_map/expert_step/pallas_call | solution.py:126
  241.0 27.5 %expert_step.7 = (bf16[544,1024]{1,0:T(8,128)(2,1)}, bf16[544,1024]{1,0:T(8,128)(2,1)}, bf16[512,1024]{1,0:T(8,128)(2,1)}, bf16[512,1024]{1,0:T(8,128)(2,1)}, bf...) custom-call(s32[1]{0:T(128)} %bitcast.4.refs_0_, ...), custom_call_target="tpu_custom_call", output_to_operand_aliasing={{4}: (12, {}), {5}: (13, {}), {6}: (14, {}), {7}: (15, {}),... | custom-call | flops 1048576 | bytes 1048576 | tf_op jit(solution)/shard_map/expert_step/pallas_call | solution.py:126
  272.8 15.7 %weight_grads.2 = (bf16[2,3,512,512]{3,2,1,0:T(8,128)(2,1)}, bf16[2,3,512,512]{3,2,1,0:T(8,128)(2,1)}) custom-call(s32[1]{0:T(128)} %bitcast.bit_ref, bf16[4,1536,1024]{2,1,0:T(8,128)(2,1)} %get-tuple-element.425.xs_ref, bf16[4,1536,1024]{2,1,0:T(8,128)(2,1)} %get-tuple-element.426.ge_ref, bf16[4,1536,512]{2,1,0:T(8,128)(2,1)} %get-tuple-element.427.hs_ref, ...), custom_call_target="tpu_custom_call" | custom-call | flops 1048576 | bytes 1048576 | tf_op jit(solution)/shard_map/weight_grads/pallas_call | solution.py:189
  288.5 15.6 %weight_grads.3 = (bf16[2,3,512,512]{3,2,1,0:T(8,128)(2,1)}, bf16[2,3,512,512]{3,2,1,0:T(8,128)(2,1)}) custom-call(s32[1]{0:T(128)} %bitcast.1.bit_ref, bf16[4,1536,1024]{2,1,0:T(8,128)(2,1)} %get-tuple-element.425.xs_ref, bf16[4,1536,1024]{2,1,0:T(8,128)(2,1)} %get-tuple-element.426.ge_ref, bf16[4,1536,512]{2,1,0:T(8,128)(2,1)} %get-tuple-element.427.hs_ref, ...), custom_call_target="tpu_custom_call" | custom-call | flops 1048576 | bytes 1048576 | tf_op jit(solution)/shard_map/weight_grads/pallas_call | solution.py:189
  312.7 26.1 %collective-permute-done.44 = bf16[544,1024]{1,0:T(8,128)(2,1)S(1)} collective-permute-done((bf16[544,1024]{1,0:T(8,128)(2,1)S(1)}, bf16[544,1024]{1,0:T(8,128)(2,1)S(1)}, u32[]{:S(2)}, u32[]{:S(2)}) %collective-permute-start.44) | collective-permute-done | bytes 1114144 | tf_op jit(solution)/shard_map/ppermute | solution.py:346
  340.5 9.6 %branch.1 = (f32[512,1024]{1,0:T(8,128)}, bf16[512,1024]{1,0:T(8,128)(2,1)}, bf16[1024,1152]{1,0:T(8,128)(2,1)}) custom-call(bf16[544,1024]{1,0:T(8,128)(2,1)} %add_convert_fusion.2.mg_ref, f32[512,1024]{1,0:T(8,128)} %get-tuple-element.446.res_ref, bf16[512,1024]{1,0:T(8,128)(2,1)} %get-tuple-element.447.refs_1_.moe_ref, ...), custom_call_target="tpu_custom_call" | custom-call | flops 1048576 | bytes 1048576 | tf_op jit(solution)/shard_map/branch/pallas_call | solution.py:536
  350.1 34.3 %attend_back.1 = (bf16[512,3328]{1,0:T(8,128)(2,1)}, bf16[512,3328]{1,0:T(8,128)(2,1)}, bf16[512,1024]{1,0:T(8,128)(2,1)}) custom-call(s32[8]{0:T(128)} %get-tuple-element.431.pos_ref, bf16[512,1024]{1,0:T(8,128)(2,1)} %h_ref.5, bf16[1024,2176]{1,0:T(8,128)(2,1)} %copy-done, bf16[1024,2176]{1,0:T(8,128)(2,1)} %copy-done, bf16[1024,2176]{1,0:T(8,128)(2,1)} %copy-done, ...), custom_call_target="tpu_custom_call" | custom-call | flops 1048576 | bytes 1048576 | tf_op jit(solution)/shard_map/attend_back/pallas_call | solution.py:646
  402.6 19.7 %collective-permute-done.52 = bf16[128,3328]{1,0:T(8,128)(2,1)S(1)} collective-permute-done((bf16[128,3328]{1,0:T(8,128)(2,1)S(1)}, bf16[128,3328]{1,0:T(8,128)(2,1)S(1)}, u32[]{:S(2)}, u32[]{:S(2)}) %collective-permute-start.52) | collective-permute-done | bytes 852000 | tf_op jit(solution)/shard_map/ppermute | solution.py:346
  422.3 9.6 %collective-permute-done.50 = bf16[2,3,256,512]{3,2,1,0:T(8,128)(2,1)S(1)} collective-permute-done((bf16[2,3,256,512]{3,2,1,0:T(8,128)(2,1)}, bf16[2,3,256,512]{3,2,1,0:T(8,128)(2,1)S(1)}, u32[]{:S(2)}, u32[]{:S(2)}) %collective-permute-start.50) | collective-permute-done | bytes 1572896 | tf_op jit(solution)/shard_map/ppermute | solution.py:342
  439.8 21.2 %collective-permute-done.58 = bf16[128,3328]{1,0:T(8,128)(2,1)S(1)} collective-permute-done((bf16[128,3328]{1,0:T(8,128)(2,1)S(1)}, bf16[128,3328]{1,0:T(8,128)(2,1)S(1)}, u32[]{:S(2)}, u32[]{:S(2)}) %collective-permute-start.58) | collective-permute-done | bytes 852000 | tf_op jit(solution)/shard_map/ppermute | solution.py:346
  461.0 11.6 %collective-permute-done.56.refs_1_ = bf16[2,3,256,512]{3,2,1,0:T(8,128)(2,1)S(1)} collective-permute-done((bf16[2,3,256,512]{3,2,1,0:T(8,128)(2,1)S(1)}, bf16[2,3,256,512]{3,2,1,0:T(8,128)(2,1)S(1)}, u32[]{:S(2)}, u32[]{:S(2)}) %collective-permute-start.56) | collective-permute-done | bytes 1572896 | tf_op jit(solution)/shard_map/ppermute | solution.py:342
  476.5 18.6 %collective-permute-done.59 = bf16[128,3328]{1,0:T(8,128)(2,1)S(1)} collective-permute-done((bf16[128,3328]{1,0:T(8,128)(2,1)S(1)}, bf16[128,3328]{1,0:T(8,128)(2,1)S(1)}, u32[]{:S(2)}, u32[]{:S(2)}) %collective-permute-start.59) | collective-permute-done | bytes 852000 | tf_op jit(solution)/shard_map/ppermute | solution.py:346
  500.5 12.6 %collective-permute-done.60 = bf16[32,3328]{1,0:T(8,128)(2,1)S(1)} collective-permute-done((bf16[32,3328]{1,0:T(8,128)(2,1)S(1)}, bf16[32,3328]{1,0:T(8,128)(2,1)S(1)}, u32[]{:S(2)}, u32[]{:S(2)}) %collective-permute-start.60) | collective-permute-done | bytes 213024 | tf_op jit(solution)/shard_map/ppermute | solution.py:342
  531.1 12.2 %place_early.1 = (f32[4,1024,512]{2,1,0:T(8,128)}, f32[4,1024,512]{2,1,0:T(8,128)}, f32[4,512,1024]{2,1,0:T(8,128)}) custom-call(s32[4,2]{1,0:T(4,128)} %pad_add_fusion.bits_ref, bf16[2,3,256,512]{3,2,1,0:T(8,128)(2,1)} %copy-done.9, bf16[2,3,256,512]{3,2,1,0:T(8,128)(2,1)} %copy-done.16, bf16[2,3,256,512]{3,2,1,0:T(8,128)(2,1)} %collective-permute-done.63.refs_2_, ...), custom_call_target="tpu_custom_call" | custom-call | flops 1048576 | bytes 1048576 | tf_op jit(solution)/shard_map/place_early/pallas_call | solution.py:295
  543.3 5.6 collective-permute-done.68
  558.4 6.0 %place_late.1 = (f32[4,1024,512]{2,1,0:T(8,128)}, f32[4,1024,512]{2,1,0:T(8,128)}, f32[4,512,1024]{2,1,0:T(8,128)}) custom-call(s32[4,2]{1,0:T(4,128)} %pad_add_fusion.bits_ref, bf16[2,3,256,512]{3,2,1,0:T(8,128)(2,1)} %collective-permute-done.65.refs_0_, ...), custom_call_target="tpu_custom_call", output_to_operand_aliasing={{0}: (3, {}), {1}: (4, {}), {2}: (5, {})} | custom-call | flops 1048576 | bytes 1048576 | tf_op jit(solution)/shard_map/place_late/pallas_call | solution.py:295
  (299 shorter events, 178.3 us)
Async XLA Ops:
  65.8 38.7 %collective-permute-start.21 = (bf16[512,1024]{1,0:T(8,128)(2,1)}, bf16[512,1024]{1,0:T(8,128)(2,1)}, u32[]{:S(2)}, u32[]{:S(2)}) collective-permute-start(bf16[512,1024]{1,0:T(8,128)(2,1)} %collective-permute-done.17.refs_3_), channel_id=1, source_target_pairs={{0,2},{1,3},{2,4},{3,5},{4,6},{5,7},{6,0},{7,1},{8,10},{9,11},{10,... | collective-permute-start | bytes 3145736 | tf_op jit(solution)/shard_map/ppermute | solution.py:346
  68.3 47.3 %collective-permute-start.22 = (bf16[512,1024]{1,0:T(8,128)(2,1)}, bf16[512,1024]{1,0:T(8,128)(2,1)}, u32[]{:S(2)}, u32[]{:S(2)}) collective-permute-start(bf16[512,1024]{1,0:T(8,128)(2,1)} %cot_ref.1), channel_id=1, source_target_pairs={{0,6},{1,7},{2,0},{3,1},{4,2},{5,3},{6,4},{7,5},{8,14},{9,15},{10,... | collective-permute-start | bytes 3145736 | tf_op jit(solution)/shard_map/ppermute | solution.py:346
  133.7 32.6 %collective-permute-start.31 = (bf16[512,1024]{1,0:T(8,128)(2,1)}, bf16[512,1024]{1,0:T(8,128)(2,1)S(1)}, u32[]{:S(2)}, u32[]{:S(2)}) collective-permute-start(bf16[512,1024]{1,0:T(8,128)(2,1)} %collective-permute-done.21.refs_3_), channel_id=1, source_target_pairs={{0,1},{1,0},{2,3},{3,2},{4,5},{5,4},{6,7},{7,6},{8,9},{9,8},{10,11... | collective-permute-start | bytes 3145736 | tf_op jit(solution)/shard_map/ppermute | solution.py:339
  166.3 33.3 %collective-permute-start.35 = (bf16[544,1024]{1,0:T(8,128)(2,1)}, bf16[544,1024]{1,0:T(8,128)(2,1)S(1)}, u32[]{:S(2)}, u32[]{:S(2)}) collective-permute-start(bf16[544,1024]{1,0:T(8,128)(2,1)} %get-tuple-element.362), channel_id=1, source_target_pairs={{0,1},{1,0},{2,3},{3,2},{4,5},{5,4},{6,7},{7,6},{8,9},{9,8},{10,11... | collective-permute-start | bytes 3342344 | tf_op jit(solution)/shard_map/ppermute | solution.py:339
  166.9 32.7 %collective-permute-start.34 = (bf16[512,1024]{1,0:T(8,128)(2,1)}, bf16[512,1024]{1,0:T(8,128)(2,1)S(1)}, u32[]{:S(2)}, u32[]{:S(2)}) collective-permute-start(bf16[512,1024]{1,0:T(8,128)(2,1)} %collective-permute-done.22.refs_3_), channel_id=1, source_target_pairs={{0,1},{1,0},{2,3},{3,2},{4,5},{5,4},{6,7},{7,6},{8,9},{9,8},{10,11... | collective-permute-start | bytes 3145736 | tf_op jit(solution)/shard_map/ppermute | solution.py:339
  167.0 32.7 %collective-permute-start.33 = (bf16[512,1024]{1,0:T(8,128)(2,1)}, bf16[512,1024]{1,0:T(8,128)(2,1)}, u32[]{:S(2)}, u32[]{:S(2)}) collective-permute-start(bf16[512,1024]{1,0:T(8,128)(2,1)} %collective-permute-done.30.refs_1_), channel_id=1, source_target_pairs={{0,2},{1,3},{2,4},{3,5},{4,6},{5,7},{6,0},{7,1},{8,10},{9,11},{10,... | collective-permute-start | bytes 3145736 | tf_op jit(solution)/shard_map/ppermute | solution.py:346
  200.6 32.1 %collective-permute-start.38 = (bf16[544,1024]{1,0:T(8,128)(2,1)}, bf16[544,1024]{1,0:T(8,128)(2,1)S(1)}, u32[]{:S(2)}, u32[]{:S(2)}) collective-permute-start(bf16[544,1024]{1,0:T(8,128)(2,1)} %get-tuple-element.384), channel_id=1, source_target_pairs={{0,1},{1,0},{2,3},{3,2},{4,5},{5,4},{6,7},{7,6},{8,9},{9,8},{10,11... | collective-permute-start | bytes 3342344 | tf_op jit(solution)/shard_map/ppermute | solution.py:339
  234.2 34.3 %collective-permute-start.40 = (bf16[544,1024]{1,0:T(8,128)(2,1)}, bf16[544,1024]{1,0:T(8,128)(2,1)S(1)}, u32[]{:S(2)}, u32[]{:S(2)}) collective-permute-start(bf16[544,1024]{1,0:T(8,128)(2,1)} %add_convert_fusion.5), channel_id=1, source_target_pairs={{0,2},{1,3},{2,4},{3,5},{4,6},{5,7},{6,0},{7,1},{8,10},{9,11},{10,... | collective-permute-start | bytes 3342344 | tf_op jit(solution)/shard_map/ppermute | solution.py:346
  236.4 32.1 %collective-permute-start.41 = (bf16[544,1024]{1,0:T(8,128)(2,1)}, bf16[544,1024]{1,0:T(8,128)(2,1)S(1)}, u32[]{:S(2)}, u32[]{:S(2)}) collective-permute-start(bf16[544,1024]{1,0:T(8,128)(2,1)} %get-tuple-element.410), channel_id=1, source_target_pairs={{0,1},{1,0},{2,3},{3,2},{4,5},{5,4},{6,7},{7,6},{8,9},{9,8},{10,11... | collective-permute-start | bytes 3342344 | tf_op jit(solution)/shard_map/ppermute | solution.py:339
  271.4 32.7 %collective-permute-start.43 = (bf16[544,1024]{1,0:T(8,128)(2,1)S(1)}, bf16[544,1024]{1,0:T(8,128)(2,1)S(1)}, u32[]{:S(2)}, u32[]{:S(2)}) collective-permute-start(bf16[544,1024]{1,0:T(8,128)(2,1)S(1)} %add_convert_fusion.4), channel_id=1, source_target_pairs={{0,2},{1,3},{2,4},{3,5},{4,6},{5,7},{6,0},{7,1},{8,10},{9,11},{10,... | collective-permute-start | bytes 3342344 | tf_op jit(solution)/shard_map/ppermute | solution.py:346
  272.8 34.5 %collective-permute-start.42 = (bf16[544,1024]{1,0:T(8,128)(2,1)}, bf16[544,1024]{1,0:T(8,128)(2,1)}, u32[]{:S(2)}, u32[]{:S(2)}) collective-permute-start(bf16[544,1024]{1,0:T(8,128)(2,1)} %get-tuple-element.438), channel_id=1, source_target_pairs={{0,1},{1,0},{2,3},{3,2},{4,5},{5,4},{6,7},{7,6},{8,9},{9,8},{10,11... | collective-permute-start | bytes 3342344 | tf_op jit(solution)/shard_map/ppermute | solution.py:339
  305.2 79.2 %collective-permute-start.47 = (bf16[2,3,512,512]{3,2,1,0:T(8,128)(2,1)}, bf16[2,3,512,512]{3,2,1,0:T(8,128)(2,1)}, u32[]{:S(2)}, u32[]{:S(2)}) collective-permute-start(bf16[2,3,512,512]{3,2,1,0:T(8,128)(2,1)} %get-tuple-element.456), channel_id=1, source_target_pairs={{0,8},{8,0},{16,24},{24,16},{1,9},{9,1},{17,25},{25,17},{2,10},{10... | collective-permute-start | bytes 9437192 | tf_op jit(solution)/shard_map/ppermute | solution.py:342
  306.4 78.0 %collective-permute-start.48 = (bf16[2,3,512,512]{3,2,1,0:T(8,128)(2,1)}, bf16[2,3,512,512]{3,2,1,0:T(8,128)(2,1)S(1)}, u32[]{:S(2)}, u32[]{:S(2)}) collective-permute-start(bf16[2,3,512,512]{3,2,1,0:T(8,128)(2,1)} %get-tuple-element.457), channel_id=1, source_target_pairs={{0,16},{8,24},{16,0},{24,8},{1,17},{9,25},{17,1},{25,9},{2,18},{10... | collective-permute-start | bytes 9437192 | tf_op jit(solution)/shard_map/ppermute | solution.py:342
  340.5 43.9 %collective-permute-start.46 = (bf16[512,1024]{1,0:T(8,128)(2,1)}, bf16[512,1024]{1,0:T(8,128)(2,1)}, u32[]{:S(2)}, u32[]{:S(2)}) collective-permute-start(bf16[512,1024]{1,0:T(8,128)(2,1)} %add_convert_fusion.12), channel_id=1, source_target_pairs={{0,2},{1,3},{2,4},{3,5},{4,6},{5,7},{6,0},{7,1},{8,10},{9,11},{10,... | collective-permute-start | bytes 3145736 | tf_op jit(solution)/shard_map/ppermute | solution.py:346
  395.3 36.6 %collective-permute-start.50 = (bf16[2,3,256,512]{3,2,1,0:T(8,128)(2,1)}, bf16[2,3,256,512]{3,2,1,0:T(8,128)(2,1)S(1)}, u32[]{:S(2)}, u32[]{:S(2)}) collective-permute-start(bf16[2,3,256,512]{3,2,1,0:T(8,128)(2,1)} %get-tuple-element.482), channel_id=1, source_target_pairs={{0,16},{8,24},{16,0},{24,8},{1,17},{9,25},{17,1},{25,9},{2,18},{10... | collective-permute-start | bytes 4718600 | tf_op jit(solution)/shard_map/ppermute | solution.py:342
  396.4 36.3 %collective-permute-start.51 = (bf16[2,3,256,512]{3,2,1,0:T(8,128)(2,1)}, bf16[2,3,256,512]{3,2,1,0:T(8,128)(2,1)S(1)}, u32[]{:S(2)}, u32[]{:S(2)}) collective-permute-start(bf16[2,3,256,512]{3,2,1,0:T(8,128)(2,1)} %get-tuple-element.483), channel_id=1, source_target_pairs={{0,8},{8,0},{16,24},{24,16},{1,9},{9,1},{17,25},{25,17},{2,10},{10... | collective-permute-start | bytes 4718600 | tf_op jit(solution)/shard_map/ppermute | solution.py:342
  437.3 35.2 %collective-permute-start.56 = (bf16[2,3,256,512]{3,2,1,0:T(8,128)(2,1)S(1)}, bf16[2,3,256,512]{3,2,1,0:T(8,128)(2,1)S(1)}, u32[]{:S(2)}, u32[]{:S(2)}) collective-permute-start(bf16[2,3,256,512]{3,2,1,0:T(8,128)(2,1)S(1)} %add_convert_fusion.1.refs_0_), channel_id=1, source_target_pairs={{0,16},{8,24},{16,0},{24,8},{1,17},{9,25},{17,1},{25,9},{2,18},{10... | collective-permute-start | bytes 4718600 | tf_op jit(solution)/shard_map/ppermute | solution.py:342
  438.2 35.4 %collective-permute-start.57 = (bf16[2,3,256,512]{3,2,1,0:T(8,128)(2,1)}, bf16[2,3,256,512]{3,2,1,0:T(8,128)(2,1)}, u32[]{:S(2)}, u32[]{:S(2)}) collective-permute-start(bf16[2,3,256,512]{3,2,1,0:T(8,128)(2,1)} %add_convert_fusion.refs_3_), channel_id=1, source_target_pairs={{0,8},{8,0},{16,24},{24,16},{1,9},{9,1},{17,25},{25,17},{2,10},{10... | collective-permute-start | bytes 4718600 | tf_op jit(solution)/shard_map/ppermute | solution.py:342
  474.3 45.8 %collective-permute-start.63 = (bf16[2,3,256,512]{3,2,1,0:T(8,128)(2,1)S(1)}, bf16[2,3,256,512]{3,2,1,0:T(8,128)(2,1)}, u32[]{:S(2)}, u32[]{:S(2)}) collective-permute-start(bf16[2,3,256,512]{3,2,1,0:T(8,128)(2,1)S(1)} %add_convert_fusion.1.refs_0_), channel_id=1, source_target_pairs={{0,8},{8,0},{16,24},{24,16},{1,9},{9,1},{17,25},{25,17},{2,10},{10... | collective-permute-start | bytes 4718600 | tf_op jit(solution)/shard_map/ppermute | solution.py:342
  475.4 44.7 %collective-permute-start.64 = (bf16[2,3,256,512]{3,2,1,0:T(8,128)(2,1)}, bf16[2,3,256,512]{3,2,1,0:T(8,128)(2,1)}, u32[]{:S(2)}, u32[]{:S(2)}) collective-permute-start(bf16[2,3,256,512]{3,2,1,0:T(8,128)(2,1)} %add_convert_fusion.refs_3_), channel_id=1, source_target_pairs={{0,16},{8,24},{16,0},{24,8},{1,17},{9,25},{17,1},{25,9},{2,18},{10... | collective-permute-start | bytes 4718600 | tf_op jit(solution)/shard_map/ppermute | solution.py:342
  520.1 37.6 %collective-permute-start.65 = (bf16[2,3,256,512]{3,2,1,0:T(8,128)(2,1)}, bf16[2,3,256,512]{3,2,1,0:T(8,128)(2,1)}, u32[]{:S(2)}, u32[]{:S(2)}) collective-permute-start(bf16[2,3,256,512]{3,2,1,0:T(8,128)(2,1)} %copy-done.16), channel_id=1, source_target_pairs={{0,8},{8,0},{16,24},{24,16},{1,9},{9,1},{17,25},{25,17},{2,10},{10... | collective-permute-start | bytes 4718600 | tf_op jit(solution)/shard_map/ppermute | solution.py:342
  520.9 37.5 %collective-permute-start.66 = (bf16[2,3,256,512]{3,2,1,0:T(8,128)(2,1)}, bf16[2,3,256,512]{3,2,1,0:T(8,128)(2,1)}, u32[]{:S(2)}, u32[]{:S(2)}) collective-permute-start(bf16[2,3,256,512]{3,2,1,0:T(8,128)(2,1)} %collective-permute-done.57.refs_4_), channel_id=1, source_target_pairs={{0,16},{8,24},{16,0},{24,8},{1,17},{9,25},{17,1},{25,9},{2,18},{10... | collective-permute-start | bytes 4718600 | tf_op jit(solution)/shard_map/ppermute | solution.py:342
  529.5 35.0 %collective-permute-start.69 = (bf16[32,3328]{1,0:T(8,128)(2,1)S(1)}, bf16[32,3328]{1,0:T(8,128)(2,1)S(1)}, u32[]{:S(2)}, u32[]{:S(2)}) collective-permute-start(bf16[32,3328]{1,0:T(8,128)(2,1)S(1)} %add_convert_fusion.20.refs_0_), channel_id=1, source_target_pairs={{0,8},{8,0},{16,24},{24,16},{1,9},{9,1},{17,25},{25,17},{2,10},{10... | collective-permute-start | bytes 638984 | tf_op jit(solution)/shard_map/ppermute | solution.py:342
  529.6 34.8 %collective-permute-start.70 = (bf16[32,3328]{1,0:T(8,128)(2,1)S(1)}, bf16[32,3328]{1,0:T(8,128)(2,1)S(1)}, u32[]{:S(2)}, u32[]{:S(2)}) collective-permute-start(bf16[32,3328]{1,0:T(8,128)(2,1)S(1)} %add_convert_fusion.20.refs_0_), channel_id=1, source_target_pairs={{0,16},{8,24},{16,0},{24,8},{1,17},{9,25},{17,1},{25,9},{2,18},{10... | collective-permute-start | bytes 638984 | tf_op jit(solution)/shard_map/ppermute | solution.py:342
  (87 other events, 1085.4 us)

commit v5 on v4

--- a/solution.py
+++ b/solution.py
@@ -305,24 +305,20 @@
     )(bits, *[q for group in quarters for q in group], *(held or ()))
 
 
-def assemble_kernel(place,p_ref,*refs):
-    ins=refs[:-2]; o_ref,sem=refs[-2:]
-    copies=[]
+def assemble_kernel(p_ref,*refs):
+    ins=refs[:-1]; o_ref=refs[-1]
     for n,r in enumerate(ins):
         chips,sub,_=r.shape
         for k in range(chips):
             row=pl.multiple_of(p_ref[n*chips+k]*sub,sub)
-            copies.append(pltpu.make_async_copy(r.at[k],o_ref.at[pl.ds(row,sub),:],sem.at[n*chips+k]))
-    for c in copies: c.start()
-    for c in copies: c.wait()
+            o_ref[pl.ds(row,sub),:]=r[k]
 
 def assemble(places,pieces):
     n=len(pieces); chips,sub,W=pieces[0].shape
-    return pl.pallas_call(functools.partial(assemble_kernel,None),
+    return pl.pallas_call(assemble_kernel,
         grid_spec=pltpu.PrefetchScalarGridSpec(num_scalar_prefetch=1,grid=(1,),
-          in_specs=[pl.BlockSpec(memory_space=pl.ANY)]*n,
-          out_specs=pl.BlockSpec((n*chips*sub,W),lambda i,p:(0,0)),
-          scratch_shapes=[pltpu.SemaphoreType.DMA((n*chips,))]),
+          in_specs=[pl.BlockSpec(memory_space=pltpu.VMEM)]*n,
+          out_specs=pl.BlockSpec((n*chips*sub,W),lambda i,p:(0,0))),
         out_shape=jax.ShapeDtypeStruct((n*chips*sub,W),BF),cost_estimate=COST,
         compiler_params=pltpu.CompilerParams(vmem_limit_bytes=40<<20),
         name="assemble")(places,*pieces)
@@ -730,6 +726,7 @@
     stack_two = stacks[:, :, first_width:]
     slices_one = [stack_one] + [swap_dp(stack_one, r) for r in range(1, dp_count)]
     cotangent_steps.append(shift_chips(cotangent_steps[0], 1))
+    last_step = [shift_chips(cotangent_steps[0], chips - 1)] if chips > 2 else []
     routes_all = []
     for s in routes_shifts:
         routes_all += [s, swap_pair(s)]
@@ -762,10 +759,9 @@
     pieces_one, stack_two, cotangent_steps = tie(pieces_one, stack_two, cotangent_steps)
     for k in range(2, chips - 1):
         cotangent_steps.append(shift_chips(cotangent_steps[k - 1], 1))
-    if chips > 2:
-        cotangent_steps.append(shift_chips(cotangent_steps[0], chips - 1))
     attn_weights = assemble(places, pieces_one)
-    attn_weights, stack_two = tie(attn_weights, stack_two)
+    attn_weights, stack_two, last_step = tie(attn_weights, stack_two, last_step)
+    cotangent_steps += last_step
     slices_two = [stack_two] + [swap_dp(stack_two, r) for r in range(1, dp_count)]
     kv_heads = key_weight.shape[1] // (2 * HALF)
     query, key, value, mixed, lse = attend(

time: 578 us -> 571 us (0.988)
  waiting for transfers between devices: 191 us -> 202 us
  Pallas kernels: 249 us -> 239 us
  starting transfers between devices: 61.4 us -> 54.7 us
    pallas_call x2, Pallas kernels: 12.1 us -> 1.56 us  [assemble(): pl.pallas_call(assemble_kernel, grid_spec=pltpu.PrefetchScalarGridSpec(nu...]
    ppermute x21, waiting for transfers between devices: 116 us -> 123 us  [shift_chips(): return lax.ppermute(v, 'expert', [(i, (i + 2 * k) % n) for i in range(n)])]
  transfers between devices with their start and end apart: 72 -> 72, of which waited for: 29 -> 30; matrix products, arithmetic and copies ran while one was open for 6% -> 6% of each run, Pallas kernels for 42% -> 41%
where the time goes in v5:
time: 571 us; the launch traced here: 564 us
  Pallas kernels  239 us (42%)
  waiting for transfers between devices  202 us (35%)
  starting transfers between devices  54.7 us (10%)
  other arithmetic  34.3 us (6%)
  local copies, waits for them, and re-layouts  29 us (5%)
    ppermute x21, waiting for transfers between devices, shift_chips(): return lax.ppermute(v, 'expert', [(i, (i + 2 * k) % n) for i in range(n)])  123 us
    pallas_call x4, Pallas kernels, expert_step(): pl.pallas_call(functools.partial(step_kernel, aliased), grid_spec=pltpu.P...  110 us
    ppermute x22, waiting for transfers between devices, swap_dp(): lax.ppermute(v, 'dp', [(i, i ^ r) for i in range(lax.axis_size('dp'))])  61 us
    pallas_call x1, Pallas kernels, attend_back(): pl.pallas_call(functools.partial(attend_back_kernel, gain_at), grid_spec=...  34.3 us
    pallas_call x2, Pallas kernels, weight_grads(): pl.pallas_call(functools.partial(weight_kernel, parts), grid_spec=pltpu.P...  31.3 us
    ppermute x22, starting transfers between devices, swap_dp(): lax.ppermute(v, 'dp', [(i, i ^ r) for i in range(lax.axis_size('dp'))])  24.6 us
    ppermute x21, starting transfers between devices, shift_chips(): return lax.ppermute(v, 'expert', [(i, (i + 2 * k) % n) for i in range(n)])  23.5 us
    unnamed x89, local copies, waits for them, and re-layouts  21.5 us
  transfers between devices with their start and end apart: 72, of which 30 were waited for; matrix products, arithmetic and copies ran while one was open for 6% of the time, Pallas kernels for 41%

profile of v5, /device:TPU:0, one launch (start us, length us, event | category | flops | bytes accessed | tf_op | source)
XLA Modules:
  0.0 563.5 jit_solution(11597168486347555712)
XLA Ops:
  16.5 8.7 %collective-permute-done.3 = bf16[32,128]{1,0:T(8,128)(2,1)S(1)} collective-permute-done((bf16[32,128]{1,0:T(8,128)(2,1)S(1)}, bf16[32,128]{1,0:T(8,128)(2,1)S(1)}, u32[]{:S(2)}, u32[]{:S(2)}) %collective-permute-start.3) | collective-permute-done | bytes 8224 | tf_op jit(solution)/shard_map/ppermute | solution.py:342
  48.3 12.3 %collective-permute-done.11.refs_4_ = bf16[4,32,2176]{2,1,0:T(8,128)(2,1)S(1)} collective-permute-done((bf16[4,32,2176]{2,1,0:T(8,128)(2,1)S(1)}, bf16[4,32,2176]{2,1,0:T(8,128)(2,1)S(1)}, u32[]{:S(2)}, u32[]{:S(2)}) %collective-permute-start.11) | collective-permute-done | bytes 557088 | tf_op jit(solution)/shard_map/ppermute | solution.py:338
  74.8 14.4 %collective-permute-done.18.refs_3_ = bf16[512,1024]{1,0:T(8,128)(2,1)} collective-permute-done((bf16[512,1024]{1,0:T(8,128)(2,1)}, bf16[512,1024]{1,0:T(8,128)(2,1)}, u32[]{:S(2)}, u32[]{:S(2)}) %collective-permute-start.18) | collective-permute-done | bytes 1048608 | tf_op jit(solution)/shard_map/ppermute | solution.py:342
  93.5 17.2 %attend.1 = (bf16[512,1024]{1,0:T(8,128)(2,1)}, bf16[512,512]{1,0:T(8,128)(2,1)}, bf16[512,512]{1,0:T(8,128)(2,1)}, bf16[512,1024]{1,0:T(8,128)(2,1)}, f32[4,8,512]{2,1,0:T(8,128)}) custom-call(bf16[512,1024]{1,0:T(8,128)(2,1)} %h_ref.5, bf16[1024,2176]{1,0:T(8,128)(2,1)} %copy-done, bf16[1024,2176]{1,0:T(8,128)(2,1)} %copy-done, ...), custom_call_target="tpu_custom_call" | custom-call | flops 1048576 | bytes 1048576 | tf_op jit(solution)/shard_map/attend/pallas_call | solution.py:468
  122.1 4.9 project.1
  131.8 27.5 %expert_step.4 = (bf16[544,1024]{1,0:T(8,128)(2,1)}, bf16[544,1024]{1,0:T(8,128)(2,1)}, bf16[512,1024]{1,0:T(8,128)(2,1)}, bf16[512,1024]{1,0:T(8,128)(2,1)}, bf...) custom-call(s32[1]{0:T(128)} %bitcast.4.refs_0_, ...), custom_call_target="tpu_custom_call" | custom-call | flops 1048576 | bytes 1048576 | tf_op jit(solution)/shard_map/expert_step/pallas_call | solution.py:126
  165.2 27.5 %expert_step.5 = (bf16[544,1024]{1,0:T(8,128)(2,1)}, bf16[544,1024]{1,0:T(8,128)(2,1)}, bf16[512,1024]{1,0:T(8,128)(2,1)}, bf16[512,1024]{1,0:T(8,128)(2,1)}, bf...) custom-call(s32[1]{0:T(128)} %bitcast.4.refs_0_, ...), custom_call_target="tpu_custom_call", output_to_operand_aliasing={{4}: (12, {}), {5}: (13, {}), {6}: (14, {}), {7}: (15, {}),... | custom-call | flops 1048576 | bytes 1048576 | tf_op jit(solution)/shard_map/expert_step/pallas_call | solution.py:126
  198.3 27.5 %expert_step.6 = (bf16[544,1024]{1,0:T(8,128)(2,1)}, bf16[544,1024]{1,0:T(8,128)(2,1)}, bf16[512,1024]{1,0:T(8,128)(2,1)}, bf16[512,1024]{1,0:T(8,128)(2,1)}, bf...) custom-call(s32[1]{0:T(128)} %bitcast.4.refs_0_, ...), custom_call_target="tpu_custom_call", output_to_operand_aliasing={{4}: (12, {}), {5}: (13, {}), {6}: (14, {}), {7}: (15, {}),... | custom-call | flops 1048576 | bytes 1048576 | tf_op jit(solution)/shard_map/expert_step/pallas_call | solution.py:126
  233.3 27.5 %expert_step.7 = (bf16[544,1024]{1,0:T(8,128)(2,1)}, bf16[544,1024]{1,0:T(8,128)(2,1)}, bf16[512,1024]{1,0:T(8,128)(2,1)}, bf16[512,1024]{1,0:T(8,128)(2,1)}, bf...) custom-call(s32[1]{0:T(128)} %bitcast.4.refs_0_, ...), custom_call_target="tpu_custom_call", output_to_operand_aliasing={{4}: (12, {}), {5}: (13, {}), {6}: (14, {}), {7}: (15, {}),... | custom-call | flops 1048576 | bytes 1048576 | tf_op jit(solution)/shard_map/expert_step/pallas_call | solution.py:126
  265.9 15.7 %weight_grads.2 = (bf16[2,3,512,512]{3,2,1,0:T(8,128)(2,1)}, bf16[2,3,512,512]{3,2,1,0:T(8,128)(2,1)}) custom-call(s32[1]{0:T(128)} %bitcast.bit_ref, bf16[4,1536,1024]{2,1,0:T(8,128)(2,1)} %get-tuple-element.427.xs_ref, bf16[4,1536,1024]{2,1,0:T(8,128)(2,1)} %get-tuple-element.428.ge_ref, bf16[4,1536,512]{2,1,0:T(8,128)(2,1)} %get-tuple-element.429.hs_ref, ...), custom_call_target="tpu_custom_call" | custom-call | flops 1048576 | bytes 1048576 | tf_op jit(solution)/shard_map/weight_grads/pallas_call | solution.py:189
  281.6 15.6 %weight_grads.3 = (bf16[2,3,512,512]{3,2,1,0:T(8,128)(2,1)}, bf16[2,3,512,512]{3,2,1,0:T(8,128)(2,1)}) custom-call(s32[1]{0:T(128)} %bitcast.1.bit_ref, bf16[4,1536,1024]{2,1,0:T(8,128)(2,1)} %get-tuple-element.427.xs_ref, bf16[4,1536,1024]{2,1,0:T(8,128)(2,1)} %get-tuple-element.428.ge_ref, bf16[4,1536,512]{2,1,0:T(8,128)(2,1)} %get-tuple-element.429.hs_ref, ...), custom_call_target="tpu_custom_call" | custom-call | flops 1048576 | bytes 1048576 | tf_op jit(solution)/shard_map/weight_grads/pallas_call | solution.py:189
  306.4 26.4 %collective-permute-done.44 = bf16[544,1024]{1,0:T(8,128)(2,1)S(1)} collective-permute-done((bf16[544,1024]{1,0:T(8,128)(2,1)S(1)}, bf16[544,1024]{1,0:T(8,128)(2,1)S(1)}, u32[]{:S(2)}, u32[]{:S(2)}) %collective-permute-start.44) | collective-permute-done | bytes 1114144 | tf_op jit(solution)/shard_map/ppermute | solution.py:342
  334.5 9.6 %branch.1 = (f32[512,1024]{1,0:T(8,128)}, bf16[512,1024]{1,0:T(8,128)(2,1)}, bf16[1024,1152]{1,0:T(8,128)(2,1)}) custom-call(bf16[544,1024]{1,0:T(8,128)(2,1)} %add_convert_fusion.2.mg_ref, f32[512,1024]{1,0:T(8,128)} %get-tuple-element.448.res_ref, bf16[512,1024]{1,0:T(8,128)(2,1)} %get-tuple-element.449.refs_1_.moe_ref, ...), custom_call_target="tpu_custom_call" | custom-call | flops 1048576 | bytes 1048576 | tf_op jit(solution)/shard_map/branch/pallas_call | solution.py:532
  344.0 34.3 %attend_back.1 = (bf16[512,3328]{1,0:T(8,128)(2,1)}, bf16[512,3328]{1,0:T(8,128)(2,1)}, bf16[512,1024]{1,0:T(8,128)(2,1)}) custom-call(s32[8]{0:T(128)} %get-tuple-element.433.pos_ref, bf16[512,1024]{1,0:T(8,128)(2,1)} %h_ref.5, bf16[1024,2176]{1,0:T(8,128)(2,1)} %copy-done, bf16[1024,2176]{1,0:T(8,128)(2,1)} %copy-done, bf16[1024,2176]{1,0:T(8,128)(2,1)} %copy-done, ...), custom_call_target="tpu_custom_call" | custom-call | flops 1048576 | bytes 1048576 | tf_op jit(solution)/shard_map/attend_back/pallas_call | solution.py:642
  395.9 19.5 %collective-permute-done.52 = bf16[128,3328]{1,0:T(8,128)(2,1)S(1)} collective-permute-done((bf16[128,3328]{1,0:T(8,128)(2,1)S(1)}, bf16[128,3328]{1,0:T(8,128)(2,1)S(1)}, u32[]{:S(2)}, u32[]{:S(2)}) %collective-permute-start.52) | collective-permute-done | bytes 852000 | tf_op jit(solution)/shard_map/ppermute | solution.py:342
  415.3 10.5 %collective-permute-done.50 = bf16[2,3,256,512]{3,2,1,0:T(8,128)(2,1)S(1)} collective-permute-done((bf16[2,3,256,512]{3,2,1,0:T(8,128)(2,1)}, bf16[2,3,256,512]{3,2,1,0:T(8,128)(2,1)S(1)}, u32[]{:S(2)}, u32[]{:S(2)}) %collective-permute-start.50) | collective-permute-done | bytes 1572896 | tf_op jit(solution)/shard_map/ppermute | solution.py:338
  433.0 21.0 %collective-permute-done.58 = bf16[128,3328]{1,0:T(8,128)(2,1)S(1)} collective-permute-done((bf16[128,3328]{1,0:T(8,128)(2,1)S(1)}, bf16[128,3328]{1,0:T(8,128)(2,1)S(1)}, u32[]{:S(2)}, u32[]{:S(2)}) %collective-permute-start.58) | collective-permute-done | bytes 852000 | tf_op jit(solution)/shard_map/ppermute | solution.py:342
  454.0 12.0 %collective-permute-done.56.refs_1_ = bf16[2,3,256,512]{3,2,1,0:T(8,128)(2,1)S(1)} collective-permute-done((bf16[2,3,256,512]{3,2,1,0:T(8,128)(2,1)S(1)}, bf16[2,3,256,512]{3,2,1,0:T(8,128)(2,1)S(1)}, u32[]{:S(2)}, u32[]{:S(2)}) %collective-permute-start.56) | collective-permute-done | bytes 1572896 | tf_op jit(solution)/shard_map/ppermute | solution.py:338
  469.8 18.9 %collective-permute-done.59 = bf16[128,3328]{1,0:T(8,128)(2,1)S(1)} collective-permute-done((bf16[128,3328]{1,0:T(8,128)(2,1)S(1)}, bf16[128,3328]{1,0:T(8,128)(2,1)S(1)}, u32[]{:S(2)}, u32[]{:S(2)}) %collective-permute-start.59) | collective-permute-done | bytes 852000 | tf_op jit(solution)/shard_map/ppermute | solution.py:342
  493.5 13.2 %collective-permute-done.60 = bf16[32,3328]{1,0:T(8,128)(2,1)S(1)} collective-permute-done((bf16[32,3328]{1,0:T(8,128)(2,1)S(1)}, bf16[32,3328]{1,0:T(8,128)(2,1)S(1)}, u32[]{:S(2)}, u32[]{:S(2)}) %collective-permute-start.60) | collective-permute-done | bytes 213024 | tf_op jit(solution)/shard_map/ppermute | solution.py:338
  508.3 5.2 collective-permute-done.62
  523.4 12.2 %place_early.1 = (f32[4,1024,512]{2,1,0:T(8,128)}, f32[4,1024,512]{2,1,0:T(8,128)}, f32[4,512,1024]{2,1,0:T(8,128)}) custom-call(s32[4,2]{1,0:T(4,128)} %pad_add_fusion.bits_ref, bf16[2,3,256,512]{3,2,1,0:T(8,128)(2,1)} %copy-done.9, bf16[2,3,256,512]{3,2,1,0:T(8,128)(2,1)} %copy-done.16, bf16[2,3,256,512]{3,2,1,0:T(8,128)(2,1)} %collective-permute-done.63.refs_2_, ...), custom_call_target="tpu_custom_call" | custom-call | flops 1048576 | bytes 1048576 | tf_op jit(solution)/shard_map/place_early/pallas_call | solution.py:295
  535.6 6.6 %collective-permute-done.68 = bf16[512,1024]{1,0:T(8,128)(2,1)} collective-permute-done((bf16[512,1024]{1,0:T(8,128)(2,1)}, bf16[512,1024]{1,0:T(8,128)(2,1)}, u32[]{:S(2)}, u32[]{:S(2)}) %collective-permute-start.68) | collective-permute-done | bytes 1048608 | tf_op jit(solution)/shard_map/ppermute | solution.py:342
  551.8 6.0 %place_late.1 = (f32[4,1024,512]{2,1,0:T(8,128)}, f32[4,1024,512]{2,1,0:T(8,128)}, f32[4,512,1024]{2,1,0:T(8,128)}) custom-call(s32[4,2]{1,0:T(4,128)} %pad_add_fusion.bits_ref, bf16[2,3,256,512]{3,2,1,0:T(8,128)(2,1)} %collective-permute-done.65.refs_0_, ...), custom_call_target="tpu_custom_call", output_to_operand_aliasing={{0}: (3, {}), {1}: (4, {}), {2}: (5, {})} | custom-call | flops 1048576 | bytes 1048576 | tf_op jit(solution)/shard_map/place_late/pallas_call | solution.py:295
  (299 shorter events, 167.7 us)
Async XLA Ops:
  67.7 45.2 %collective-permute-start.22 = (bf16[512,1024]{1,0:T(8,128)(2,1)}, bf16[512,1024]{1,0:T(8,128)(2,1)}, u32[]{:S(2)}, u32[]{:S(2)}) collective-permute-start(bf16[512,1024]{1,0:T(8,128)(2,1)} %collective-permute-done.17.refs_3_), channel_id=1, source_target_pairs={{0,2},{1,3},{2,4},{3,5},{4,6},{5,7},{6,0},{7,1},{8,10},{9,11},{10,... | collective-permute-start | bytes 3145736 | tf_op jit(solution)/shard_map/ppermute | solution.py:342
  127.2 32.1 %collective-permute-start.31 = (bf16[512,1024]{1,0:T(8,128)(2,1)}, bf16[512,1024]{1,0:T(8,128)(2,1)S(1)}, u32[]{:S(2)}, u32[]{:S(2)}) collective-permute-start(bf16[512,1024]{1,0:T(8,128)(2,1)} %collective-permute-done.22.refs_3_), channel_id=1, source_target_pairs={{0,1},{1,0},{2,3},{3,2},{4,5},{5,4},{6,7},{7,6},{8,9},{9,8},{10,11... | collective-permute-start | bytes 3145736 | tf_op jit(solution)/shard_map/ppermute | solution.py:335
  159.3 33.5 %collective-permute-start.35 = (bf16[544,1024]{1,0:T(8,128)(2,1)}, bf16[544,1024]{1,0:T(8,128)(2,1)S(1)}, u32[]{:S(2)}, u32[]{:S(2)}) collective-permute-start(bf16[544,1024]{1,0:T(8,128)(2,1)} %get-tuple-element.364), channel_id=1, source_target_pairs={{0,1},{1,0},{2,3},{3,2},{4,5},{5,4},{6,7},{7,6},{8,9},{9,8},{10,11... | collective-permute-start | bytes 3342344 | tf_op jit(solution)/shard_map/ppermute | solution.py:335
  159.9 32.9 %collective-permute-start.34 = (bf16[512,1024]{1,0:T(8,128)(2,1)}, bf16[512,1024]{1,0:T(8,128)(2,1)S(1)}, u32[]{:S(2)}, u32[]{:S(2)}) collective-permute-start(bf16[512,1024]{1,0:T(8,128)(2,1)} %collective-permute-done.18.refs_3_), channel_id=1, source_target_pairs={{0,1},{1,0},{2,3},{3,2},{4,5},{5,4},{6,7},{7,6},{8,9},{9,8},{10,11... | collective-permute-start | bytes 3145736 | tf_op jit(solution)/shard_map/ppermute | solution.py:335
  160.0 32.7 %collective-permute-start.33 = (bf16[512,1024]{1,0:T(8,128)(2,1)}, bf16[512,1024]{1,0:T(8,128)(2,1)}, u32[]{:S(2)}, u32[]{:S(2)}) collective-permute-start(bf16[512,1024]{1,0:T(8,128)(2,1)} %collective-permute-done.30.refs_1_), channel_id=1, source_target_pairs={{0,2},{1,3},{2,4},{3,5},{4,6},{5,7},{6,0},{7,1},{8,10},{9,11},{10,... | collective-permute-start | bytes 3145736 | tf_op jit(solution)/shard_map/ppermute | solution.py:342
  193.7 32.1 %collective-permute-start.38 = (bf16[544,1024]{1,0:T(8,128)(2,1)}, bf16[544,1024]{1,0:T(8,128)(2,1)S(1)}, u32[]{:S(2)}, u32[]{:S(2)}) collective-permute-start(bf16[544,1024]{1,0:T(8,128)(2,1)} %get-tuple-element.386), channel_id=1, source_target_pairs={{0,1},{1,0},{2,3},{3,2},{4,5},{5,4},{6,7},{7,6},{8,9},{9,8},{10,11... | collective-permute-start | bytes 3342344 | tf_op jit(solution)/shard_map/ppermute | solution.py:335
  194.2 31.6 %collective-permute-start.37 = (bf16[512,1024]{1,0:T(8,128)(2,1)}, bf16[512,1024]{1,0:T(8,128)(2,1)}, u32[]{:S(2)}, u32[]{:S(2)}) collective-permute-start(bf16[512,1024]{1,0:T(8,128)(2,1)} %collective-permute-done.33.refs_1_), channel_id=1, source_target_pairs={{0,2},{1,3},{2,4},{3,5},{4,6},{5,7},{6,0},{7,1},{8,10},{9,11},{10,... | collective-permute-start | bytes 3145736 | tf_op jit(solution)/shard_map/ppermute | solution.py:342
  227.3 33.5 %collective-permute-start.40 = (bf16[544,1024]{1,0:T(8,128)(2,1)}, bf16[544,1024]{1,0:T(8,128)(2,1)S(1)}, u32[]{:S(2)}, u32[]{:S(2)}) collective-permute-start(bf16[544,1024]{1,0:T(8,128)(2,1)} %add_convert_fusion.5), channel_id=1, source_target_pairs={{0,2},{1,3},{2,4},{3,5},{4,6},{5,7},{6,0},{7,1},{8,10},{9,11},{10,... | collective-permute-start | bytes 3342344 | tf_op jit(solution)/shard_map/ppermute | solution.py:342
  228.7 32.1 %collective-permute-start.41 = (bf16[544,1024]{1,0:T(8,128)(2,1)}, bf16[544,1024]{1,0:T(8,128)(2,1)S(1)}, u32[]{:S(2)}, u32[]{:S(2)}) collective-permute-start(bf16[544,1024]{1,0:T(8,128)(2,1)} %get-tuple-element.412), channel_id=1, source_target_pairs={{0,1},{1,0},{2,3},{3,2},{4,5},{5,4},{6,7},{7,6},{8,9},{9,8},{10,11... | collective-permute-start | bytes 3342344 | tf_op jit(solution)/shard_map/ppermute | solution.py:335
  263.7 33.5 %collective-permute-start.43 = (bf16[544,1024]{1,0:T(8,128)(2,1)S(1)}, bf16[544,1024]{1,0:T(8,128)(2,1)S(1)}, u32[]{:S(2)}, u32[]{:S(2)}) collective-permute-start(bf16[544,1024]{1,0:T(8,128)(2,1)S(1)} %add_convert_fusion.4), channel_id=1, source_target_pairs={{0,2},{1,3},{2,4},{3,5},{4,6},{5,7},{6,0},{7,1},{8,10},{9,11},{10,... | collective-permute-start | bytes 3342344 | tf_op jit(solution)/shard_map/ppermute | solution.py:342
  265.9 35.4 %collective-permute-start.42 = (bf16[544,1024]{1,0:T(8,128)(2,1)}, bf16[544,1024]{1,0:T(8,128)(2,1)}, u32[]{:S(2)}, u32[]{:S(2)}) collective-permute-start(bf16[544,1024]{1,0:T(8,128)(2,1)} %get-tuple-element.440), channel_id=1, source_target_pairs={{0,1},{1,0},{2,3},{3,2},{4,5},{5,4},{6,7},{7,6},{8,9},{9,8},{10,11... | collective-permute-start | bytes 3342344 | tf_op jit(solution)/shard_map/ppermute | solution.py:335
  298.2 80.1 %collective-permute-start.47 = (bf16[2,3,512,512]{3,2,1,0:T(8,128)(2,1)}, bf16[2,3,512,512]{3,2,1,0:T(8,128)(2,1)}, u32[]{:S(2)}, u32[]{:S(2)}) collective-permute-start(bf16[2,3,512,512]{3,2,1,0:T(8,128)(2,1)} %get-tuple-element.458), channel_id=1, source_target_pairs={{0,8},{8,0},{16,24},{24,16},{1,9},{9,1},{17,25},{25,17},{2,10},{10... | collective-permute-start | bytes 9437192 | tf_op jit(solution)/shard_map/ppermute | solution.py:338
  299.8 78.6 %collective-permute-start.48 = (bf16[2,3,512,512]{3,2,1,0:T(8,128)(2,1)}, bf16[2,3,512,512]{3,2,1,0:T(8,128)(2,1)S(1)}, u32[]{:S(2)}, u32[]{:S(2)}) collective-permute-start(bf16[2,3,512,512]{3,2,1,0:T(8,128)(2,1)} %get-tuple-element.459), channel_id=1, source_target_pairs={{0,16},{8,24},{16,0},{24,8},{1,17},{9,25},{17,1},{25,9},{2,18},{10... | collective-permute-start | bytes 9437192 | tf_op jit(solution)/shard_map/ppermute | solution.py:338
  334.5 43.9 %collective-permute-start.46 = (bf16[512,1024]{1,0:T(8,128)(2,1)}, bf16[512,1024]{1,0:T(8,128)(2,1)}, u32[]{:S(2)}, u32[]{:S(2)}) collective-permute-start(bf16[512,1024]{1,0:T(8,128)(2,1)} %add_convert_fusion.12), channel_id=1, source_target_pairs={{0,2},{1,3},{2,4},{3,5},{4,6},{5,7},{6,0},{7,1},{8,10},{9,11},{10,... | collective-permute-start | bytes 3145736 | tf_op jit(solution)/shard_map/ppermute | solution.py:342
  389.3 36.6 %collective-permute-start.50 = (bf16[2,3,256,512]{3,2,1,0:T(8,128)(2,1)}, bf16[2,3,256,512]{3,2,1,0:T(8,128)(2,1)S(1)}, u32[]{:S(2)}, u32[]{:S(2)}) collective-permute-start(bf16[2,3,256,512]{3,2,1,0:T(8,128)(2,1)} %get-tuple-element.484), channel_id=1, source_target_pairs={{0,16},{8,24},{16,0},{24,8},{1,17},{9,25},{17,1},{25,9},{2,18},{10... | collective-permute-start | bytes 4718600 | tf_op jit(solution)/shard_map/ppermute | solution.py:338
  389.7 36.3 %collective-permute-start.51 = (bf16[2,3,256,512]{3,2,1,0:T(8,128)(2,1)}, bf16[2,3,256,512]{3,2,1,0:T(8,128)(2,1)S(1)}, u32[]{:S(2)}, u32[]{:S(2)}) collective-permute-start(bf16[2,3,256,512]{3,2,1,0:T(8,128)(2,1)} %get-tuple-element.485), channel_id=1, source_target_pairs={{0,8},{8,0},{16,24},{24,16},{1,9},{9,1},{17,25},{25,17},{2,10},{10... | collective-permute-start | bytes 4718600 | tf_op jit(solution)/shard_map/ppermute | solution.py:338
  430.7 35.3 %collective-permute-start.56 = (bf16[2,3,256,512]{3,2,1,0:T(8,128)(2,1)S(1)}, bf16[2,3,256,512]{3,2,1,0:T(8,128)(2,1)S(1)}, u32[]{:S(2)}, u32[]{:S(2)}) collective-permute-start(bf16[2,3,256,512]{3,2,1,0:T(8,128)(2,1)S(1)} %add_convert_fusion.1.refs_0_), channel_id=1, source_target_pairs={{0,16},{8,24},{16,0},{24,8},{1,17},{9,25},{17,1},{25,9},{2,18},{10... | collective-permute-start | bytes 4718600 | tf_op jit(solution)/shard_map/ppermute | solution.py:338
  432.2 35.3 %collective-permute-start.57 = (bf16[2,3,256,512]{3,2,1,0:T(8,128)(2,1)}, bf16[2,3,256,512]{3,2,1,0:T(8,128)(2,1)}, u32[]{:S(2)}, u32[]{:S(2)}) collective-permute-start(bf16[2,3,256,512]{3,2,1,0:T(8,128)(2,1)} %add_convert_fusion.refs_3_), channel_id=1, source_target_pairs={{0,8},{8,0},{16,24},{24,16},{1,9},{9,1},{17,25},{25,17},{2,10},{10... | collective-permute-start | bytes 4718600 | tf_op jit(solution)/shard_map/ppermute | solution.py:338
  467.9 45.6 %collective-permute-start.63 = (bf16[2,3,256,512]{3,2,1,0:T(8,128)(2,1)S(1)}, bf16[2,3,256,512]{3,2,1,0:T(8,128)(2,1)}, u32[]{:S(2)}, u32[]{:S(2)}) collective-permute-start(bf16[2,3,256,512]{3,2,1,0:T(8,128)(2,1)S(1)} %add_convert_fusion.1.refs_0_), channel_id=1, source_target_pairs={{0,8},{8,0},{16,24},{24,16},{1,9},{9,1},{17,25},{25,17},{2,10},{10... | collective-permute-start | bytes 4718600 | tf_op jit(solution)/shard_map/ppermute | solution.py:338
  468.6 44.9 %collective-permute-start.64 = (bf16[2,3,256,512]{3,2,1,0:T(8,128)(2,1)}, bf16[2,3,256,512]{3,2,1,0:T(8,128)(2,1)}, u32[]{:S(2)}, u32[]{:S(2)}) collective-permute-start(bf16[2,3,256,512]{3,2,1,0:T(8,128)(2,1)} %add_convert_fusion.refs_3_), channel_id=1, source_target_pairs={{0,16},{8,24},{16,0},{24,8},{1,17},{9,25},{17,1},{25,9},{2,18},{10... | collective-permute-start | bytes 4718600 | tf_op jit(solution)/shard_map/ppermute | solution.py:338
  513.5 37.7 %collective-permute-start.65 = (bf16[2,3,256,512]{3,2,1,0:T(8,128)(2,1)}, bf16[2,3,256,512]{3,2,1,0:T(8,128)(2,1)}, u32[]{:S(2)}, u32[]{:S(2)}) collective-permute-start(bf16[2,3,256,512]{3,2,1,0:T(8,128)(2,1)} %copy-done.16), channel_id=1, source_target_pairs={{0,8},{8,0},{16,24},{24,16},{1,9},{9,1},{17,25},{25,17},{2,10},{10... | collective-permute-start | bytes 4718600 | tf_op jit(solution)/shard_map/ppermute | solution.py:338
  513.9 38.0 %collective-permute-start.66 = (bf16[2,3,256,512]{3,2,1,0:T(8,128)(2,1)}, bf16[2,3,256,512]{3,2,1,0:T(8,128)(2,1)}, u32[]{:S(2)}, u32[]{:S(2)}) collective-permute-start(bf16[2,3,256,512]{3,2,1,0:T(8,128)(2,1)} %collective-permute-done.57.refs_4_), channel_id=1, source_target_pairs={{0,16},{8,24},{16,0},{24,8},{1,17},{9,25},{17,1},{25,9},{2,18},{10... | collective-permute-start | bytes 4718600 | tf_op jit(solution)/shard_map/ppermute | solution.py:338
  521.7 36.1 %collective-permute-start.69 = (bf16[32,3328]{1,0:T(8,128)(2,1)S(1)}, bf16[32,3328]{1,0:T(8,128)(2,1)S(1)}, u32[]{:S(2)}, u32[]{:S(2)}) collective-permute-start(bf16[32,3328]{1,0:T(8,128)(2,1)S(1)} %add_convert_fusion.20.refs_0_), channel_id=1, source_target_pairs={{0,8},{8,0},{16,24},{24,16},{1,9},{9,1},{17,25},{25,17},{2,10},{10... | collective-permute-start | bytes 638984 | tf_op jit(solution)/shard_map/ppermute | solution.py:338
  523.4 34.4 %collective-permute-start.70 = (bf16[32,3328]{1,0:T(8,128)(2,1)S(1)}, bf16[32,3328]{1,0:T(8,128)(2,1)S(1)}, u32[]{:S(2)}, u32[]{:S(2)}) collective-permute-start(bf16[32,3328]{1,0:T(8,128)(2,1)S(1)} %add_convert_fusion.20.refs_0_), channel_id=1, source_target_pairs={{0,16},{8,24},{16,0},{24,8},{1,17},{9,25},{17,1},{25,9},{2,18},{10... | collective-permute-start | bytes 638984 | tf_op jit(solution)/shard_map/ppermute | solution.py:338
  (87 other events, 1085.0 us)

commit v6 on v5

--- a/solution.py
+++ b/solution.py
@@ -837,8 +837,11 @@
         halves.append((first_of, one, two, bit_one, bit_two, keep))
         sends.append(send)
     moved, sends = tie(moved, sends)
+    if first_hop < chips:
+        total, sends = tie(sum_of(*grad_parts[first_hop], moved), sends)
+        moved = shift_chips(total, 1)
     gots = [swap_dp(send, h[1]) for h, send in zip(halves, sends)]
-    for k in range(first_hop, chips):
+    for k in range(first_hop + 1, chips):
         moved = shift_chips(sum_of(*grad_parts[k], moved), 1)
     moe_grad = sum_of(*grad_parts[0], moved)
     out_sum = (out_parts[1][0].astype(F32) + swap_pair(out_parts[1][1]).astype(F32)).astype(BF)

time: 571 us -> 569 us (level)
    unnamed x89 -> x91, local copies, waits for them, and re-layouts: 21.5 us -> 20.6 us
where the time goes in v6:
time: 569 us; the launch traced here: 562 us
  Pallas kernels  239 us (42%)
  waiting for transfers between devices  201 us (35%)
  starting transfers between devices  55.4 us (10%)
  other arithmetic  33.8 us (6%)
  local copies, waits for them, and re-layouts  28.1 us (5%)
    ppermute x21, waiting for transfers between devices, shift_chips(): return lax.ppermute(v, 'expert', [(i, (i + 2 * k) % n) for i in range(n)])  121 us
    pallas_call x4, Pallas kernels, expert_step(): pl.pallas_call(functools.partial(step_kernel, aliased), grid_spec=pltpu.P...  110 us
    ppermute x22, waiting for transfers between devices, swap_dp(): lax.ppermute(v, 'dp', [(i, i ^ r) for i in range(lax.axis_size('dp'))])  61.1 us
    pallas_call x1, Pallas kernels, attend_back(): pl.pallas_call(functools.partial(attend_back_kernel, gain_at), grid_spec=...  34.3 us
    pallas_call x2, Pallas kernels, weight_grads(): pl.pallas_call(functools.partial(weight_kernel, parts), grid_spec=pltpu.P...  31.4 us
    ppermute x21, starting transfers between devices, shift_chips(): return lax.ppermute(v, 'expert', [(i, (i + 2 * k) % n) for i in range(n)])  24.8 us
    ppermute x22, starting transfers between devices, swap_dp(): lax.ppermute(v, 'dp', [(i, i ^ r) for i in range(lax.axis_size('dp'))])  24.1 us
    unnamed x91, local copies, waits for them, and re-layouts  20.6 us
  transfers between devices with their start and end apart: 72, of which 30 were waited for; matrix products, arithmetic and copies ran while one was open for 6% of the time, Pallas kernels for 41%

profile of v6, /device:TPU:0, one launch (start us, length us, event | category | flops | bytes accessed | tf_op | source)
XLA Modules:
  0.0 562.0 jit_solution(13900774206825730424)
XLA Ops:
  16.5 8.7 %collective-permute-done.3 = bf16[32,128]{1,0:T(8,128)(2,1)S(1)} collective-permute-done((bf16[32,128]{1,0:T(8,128)(2,1)S(1)}, bf16[32,128]{1,0:T(8,128)(2,1)S(1)}, u32[]{:S(2)}, u32[]{:S(2)}) %collective-permute-start.3) | collective-permute-done | bytes 8224 | tf_op jit(solution)/shard_map/ppermute | solution.py:342
  48.3 12.3 %collective-permute-done.11.refs_4_ = bf16[4,32,2176]{2,1,0:T(8,128)(2,1)S(1)} collective-permute-done((bf16[4,32,2176]{2,1,0:T(8,128)(2,1)S(1)}, bf16[4,32,2176]{2,1,0:T(8,128)(2,1)S(1)}, u32[]{:S(2)}, u32[]{:S(2)}) %collective-permute-start.11) | collective-permute-done | bytes 557088 | tf_op jit(solution)/shard_map/ppermute | solution.py:338
  74.8 14.3 %collective-permute-done.18.refs_3_ = bf16[512,1024]{1,0:T(8,128)(2,1)} collective-permute-done((bf16[512,1024]{1,0:T(8,128)(2,1)}, bf16[512,1024]{1,0:T(8,128)(2,1)}, u32[]{:S(2)}, u32[]{:S(2)}) %collective-permute-start.18) | collective-permute-done | bytes 1048608 | tf_op jit(solution)/shard_map/ppermute | solution.py:342
  93.5 17.2 %attend.1 = (bf16[512,1024]{1,0:T(8,128)(2,1)}, bf16[512,512]{1,0:T(8,128)(2,1)}, bf16[512,512]{1,0:T(8,128)(2,1)}, bf16[512,1024]{1,0:T(8,128)(2,1)}, f32[4,8,512]{2,1,0:T(8,128)}) custom-call(bf16[512,1024]{1,0:T(8,128)(2,1)} %h_ref.5, bf16[1024,2176]{1,0:T(8,128)(2,1)} %copy-done, bf16[1024,2176]{1,0:T(8,128)(2,1)} %copy-done, ...), custom_call_target="tpu_custom_call" | custom-call | flops 1048576 | bytes 1048576 | tf_op jit(solution)/shard_map/attend/pallas_call | solution.py:468
  122.1 4.9 project.1
  132.0 27.5 %expert_step.4 = (bf16[544,1024]{1,0:T(8,128)(2,1)}, bf16[544,1024]{1,0:T(8,128)(2,1)}, bf16[512,1024]{1,0:T(8,128)(2,1)}, bf16[512,1024]{1,0:T(8,128)(2,1)}, bf...) custom-call(s32[1]{0:T(128)} %bitcast.4.refs_0_, ...), custom_call_target="tpu_custom_call" | custom-call | flops 1048576 | bytes 1048576 | tf_op jit(solution)/shard_map/expert_step/pallas_call | solution.py:126
  165.3 27.5 %expert_step.5 = (bf16[544,1024]{1,0:T(8,128)(2,1)}, bf16[544,1024]{1,0:T(8,128)(2,1)}, bf16[512,1024]{1,0:T(8,128)(2,1)}, bf16[512,1024]{1,0:T(8,128)(2,1)}, bf...) custom-call(s32[1]{0:T(128)} %bitcast.4.refs_0_, ...), custom_call_target="tpu_custom_call", output_to_operand_aliasing={{4}: (12, {}), {5}: (13, {}), {6}: (14, {}), {7}: (15, {}),... | custom-call | flops 1048576 | bytes 1048576 | tf_op jit(solution)/shard_map/expert_step/pallas_call | solution.py:126
  198.4 27.5 %expert_step.6 = (bf16[544,1024]{1,0:T(8,128)(2,1)}, bf16[544,1024]{1,0:T(8,128)(2,1)}, bf16[512,1024]{1,0:T(8,128)(2,1)}, bf16[512,1024]{1,0:T(8,128)(2,1)}, bf...) custom-call(s32[1]{0:T(128)} %bitcast.4.refs_0_, ...), custom_call_target="tpu_custom_call", output_to_operand_aliasing={{4}: (12, {}), {5}: (13, {}), {6}: (14, {}), {7}: (15, {}),... | custom-call | flops 1048576 | bytes 1048576 | tf_op jit(solution)/shard_map/expert_step/pallas_call | solution.py:126
  233.6 27.5 %expert_step.7 = (bf16[544,1024]{1,0:T(8,128)(2,1)}, bf16[544,1024]{1,0:T(8,128)(2,1)}, bf16[512,1024]{1,0:T(8,128)(2,1)}, bf16[512,1024]{1,0:T(8,128)(2,1)}, bf...) custom-call(s32[1]{0:T(128)} %bitcast.4.refs_0_, ...), custom_call_target="tpu_custom_call", output_to_operand_aliasing={{4}: (12, {}), {5}: (13, {}), {6}: (14, {}), {7}: (15, {}),... | custom-call | flops 1048576 | bytes 1048576 | tf_op jit(solution)/shard_map/expert_step/pallas_call | solution.py:126
  265.8 15.7 %weight_grads.2 = (bf16[2,3,512,512]{3,2,1,0:T(8,128)(2,1)}, bf16[2,3,512,512]{3,2,1,0:T(8,128)(2,1)}) custom-call(s32[1]{0:T(128)} %bitcast.bit_ref, bf16[4,1536,1024]{2,1,0:T(8,128)(2,1)} %get-tuple-element.430.xs_ref, bf16[4,1536,1024]{2,1,0:T(8,128)(2,1)} %get-tuple-element.431.ge_ref, bf16[4,1536,512]{2,1,0:T(8,128)(2,1)} %get-tuple-element.432.hs_ref, ...), custom_call_target="tpu_custom_call" | custom-call | flops 1048576 | bytes 1048576 | tf_op jit(solution)/shard_map/weight_grads/pallas_call | solution.py:189
  281.5 15.6 %weight_grads.3 = (bf16[2,3,512,512]{3,2,1,0:T(8,128)(2,1)}, bf16[2,3,512,512]{3,2,1,0:T(8,128)(2,1)}) custom-call(s32[1]{0:T(128)} %bitcast.1.bit_ref, bf16[4,1536,1024]{2,1,0:T(8,128)(2,1)} %get-tuple-element.430.xs_ref, bf16[4,1536,1024]{2,1,0:T(8,128)(2,1)} %get-tuple-element.431.ge_ref, bf16[4,1536,512]{2,1,0:T(8,128)(2,1)} %get-tuple-element.432.hs_ref, ...), custom_call_target="tpu_custom_call" | custom-call | flops 1048576 | bytes 1048576 | tf_op jit(solution)/shard_map/weight_grads/pallas_call | solution.py:189
  306.5 24.7 %collective-permute-done.44 = bf16[544,1024]{1,0:T(8,128)(2,1)S(1)} collective-permute-done((bf16[544,1024]{1,0:T(8,128)(2,1)S(1)}, bf16[544,1024]{1,0:T(8,128)(2,1)S(1)}, u32[]{:S(2)}, u32[]{:S(2)}) %collective-permute-start.44) | collective-permute-done | bytes 1114144 | tf_op jit(solution)/shard_map/ppermute | solution.py:342
  332.9 9.6 %branch.1 = (f32[512,1024]{1,0:T(8,128)}, bf16[512,1024]{1,0:T(8,128)(2,1)}, bf16[1024,1152]{1,0:T(8,128)(2,1)}) custom-call(bf16[544,1024]{1,0:T(8,128)(2,1)} %add_convert_fusion.2.mg_ref, f32[512,1024]{1,0:T(8,128)} %get-tuple-element.454.res_ref, bf16[512,1024]{1,0:T(8,128)(2,1)} %get-tuple-element.455.refs_1_.moe_ref, ...), custom_call_target="tpu_custom_call" | custom-call | flops 1048576 | bytes 1048576 | tf_op jit(solution)/shard_map/branch/pallas_call | solution.py:532
  342.5 34.3 %attend_back.1 = (bf16[512,3328]{1,0:T(8,128)(2,1)}, bf16[512,3328]{1,0:T(8,128)(2,1)}, bf16[512,1024]{1,0:T(8,128)(2,1)}) custom-call(s32[8]{0:T(128)} %get-tuple-element.436.pos_ref, bf16[512,1024]{1,0:T(8,128)(2,1)} %h_ref.5, bf16[1024,2176]{1,0:T(8,128)(2,1)} %copy-done, bf16[1024,2176]{1,0:T(8,128)(2,1)} %copy-done, bf16[1024,2176]{1,0:T(8,128)(2,1)} %copy-done, ...), custom_call_target="tpu_custom_call" | custom-call | flops 1048576 | bytes 1048576 | tf_op jit(solution)/shard_map/attend_back/pallas_call | solution.py:642
  394.4 19.4 %collective-permute-done.52 = bf16[128,3328]{1,0:T(8,128)(2,1)S(1)} collective-permute-done((bf16[128,3328]{1,0:T(8,128)(2,1)S(1)}, bf16[128,3328]{1,0:T(8,128)(2,1)S(1)}, u32[]{:S(2)}, u32[]{:S(2)}) %collective-permute-start.52) | collective-permute-done | bytes 852000 | tf_op jit(solution)/shard_map/ppermute | solution.py:342
  413.8 10.5 %collective-permute-done.50 = bf16[2,3,256,512]{3,2,1,0:T(8,128)(2,1)S(1)} collective-permute-done((bf16[2,3,256,512]{3,2,1,0:T(8,128)(2,1)}, bf16[2,3,256,512]{3,2,1,0:T(8,128)(2,1)S(1)}, u32[]{:S(2)}, u32[]{:S(2)}) %collective-permute-start.50) | collective-permute-done | bytes 1572896 | tf_op jit(solution)/shard_map/ppermute | solution.py:338
  431.6 20.8 %collective-permute-done.58 = bf16[128,3328]{1,0:T(8,128)(2,1)S(1)} collective-permute-done((bf16[128,3328]{1,0:T(8,128)(2,1)S(1)}, bf16[128,3328]{1,0:T(8,128)(2,1)S(1)}, u32[]{:S(2)}, u32[]{:S(2)}) %collective-permute-start.58) | collective-permute-done | bytes 852000 | tf_op jit(solution)/shard_map/ppermute | solution.py:342
  452.4 12.0 %collective-permute-done.56.refs_1_ = bf16[2,3,256,512]{3,2,1,0:T(8,128)(2,1)S(1)} collective-permute-done((bf16[2,3,256,512]{3,2,1,0:T(8,128)(2,1)S(1)}, bf16[2,3,256,512]{3,2,1,0:T(8,128)(2,1)S(1)}, u32[]{:S(2)}, u32[]{:S(2)}) %collective-permute-start.56) | collective-permute-done | bytes 1572896 | tf_op jit(solution)/shard_map/ppermute | solution.py:338
  468.3 18.8 %collective-permute-done.59 = bf16[128,3328]{1,0:T(8,128)(2,1)S(1)} collective-permute-done((bf16[128,3328]{1,0:T(8,128)(2,1)S(1)}, bf16[128,3328]{1,0:T(8,128)(2,1)S(1)}, u32[]{:S(2)}, u32[]{:S(2)}) %collective-permute-start.59) | collective-permute-done | bytes 852000 | tf_op jit(solution)/shard_map/ppermute | solution.py:342
  491.9 13.2 %collective-permute-done.60 = bf16[32,3328]{1,0:T(8,128)(2,1)S(1)} collective-permute-done((bf16[32,3328]{1,0:T(8,128)(2,1)S(1)}, bf16[32,3328]{1,0:T(8,128)(2,1)S(1)}, u32[]{:S(2)}, u32[]{:S(2)}) %collective-permute-start.60) | collective-permute-done | bytes 213024 | tf_op jit(solution)/shard_map/ppermute | solution.py:338
  506.9 5.1 collective-permute-done.62
  521.8 12.3 %place_early.1 = (f32[4,1024,512]{2,1,0:T(8,128)}, f32[4,1024,512]{2,1,0:T(8,128)}, f32[4,512,1024]{2,1,0:T(8,128)}) custom-call(s32[4,2]{1,0:T(4,128)} %pad_add_fusion.bits_ref, bf16[2,3,256,512]{3,2,1,0:T(8,128)(2,1)} %copy-done.9, bf16[2,3,256,512]{3,2,1,0:T(8,128)(2,1)} %copy-done.16, bf16[2,3,256,512]{3,2,1,0:T(8,128)(2,1)} %collective-permute-done.63.refs_2_, ...), custom_call_target="tpu_custom_call" | custom-call | flops 1048576 | bytes 1048576 | tf_op jit(solution)/shard_map/place_early/pallas_call | solution.py:295
  534.1 6.5 %collective-permute-done.68 = bf16[512,1024]{1,0:T(8,128)(2,1)} collective-permute-done((bf16[512,1024]{1,0:T(8,128)(2,1)}, bf16[512,1024]{1,0:T(8,128)(2,1)}, u32[]{:S(2)}, u32[]{:S(2)}) %collective-permute-start.68) | collective-permute-done | bytes 1048608 | tf_op jit(solution)/shard_map/ppermute | solution.py:342
  550.3 6.0 %place_late.1 = (f32[4,1024,512]{2,1,0:T(8,128)}, f32[4,1024,512]{2,1,0:T(8,128)}, f32[4,512,1024]{2,1,0:T(8,128)}) custom-call(s32[4,2]{1,0:T(4,128)} %pad_add_fusion.bits_ref, bf16[2,3,256,512]{3,2,1,0:T(8,128)(2,1)} %collective-permute-done.65.refs_0_, ...), custom_call_target="tpu_custom_call", output_to_operand_aliasing={{0}: (3, {}), {1}: (4, {}), {2}: (5, {})} | custom-call | flops 1048576 | bytes 1048576 | tf_op jit(solution)/shard_map/place_late/pallas_call | solution.py:295
  (301 shorter events, 168.1 us)
Async XLA Ops:
  67.7 45.2 %collective-permute-start.22 = (bf16[512,1024]{1,0:T(8,128)(2,1)}, bf16[512,1024]{1,0:T(8,128)(2,1)}, u32[]{:S(2)}, u32[]{:S(2)}) collective-permute-start(bf16[512,1024]{1,0:T(8,128)(2,1)} %collective-permute-done.17.refs_3_), channel_id=1, source_target_pairs={{0,2},{1,3},{2,4},{3,5},{4,6},{5,7},{6,0},{7,1},{8,10},{9,11},{10,... | collective-permute-start | bytes 3145736 | tf_op jit(solution)/shard_map/ppermute | solution.py:342
  127.2 32.3 %collective-permute-start.31 = (bf16[512,1024]{1,0:T(8,128)(2,1)}, bf16[512,1024]{1,0:T(8,128)(2,1)S(1)}, u32[]{:S(2)}, u32[]{:S(2)}) collective-permute-start(bf16[512,1024]{1,0:T(8,128)(2,1)} %collective-permute-done.22.refs_3_), channel_id=1, source_target_pairs={{0,1},{1,0},{2,3},{3,2},{4,5},{5,4},{6,7},{7,6},{8,9},{9,8},{10,11... | collective-permute-start | bytes 3145736 | tf_op jit(solution)/shard_map/ppermute | solution.py:335
  159.5 33.3 %collective-permute-start.35 = (bf16[544,1024]{1,0:T(8,128)(2,1)}, bf16[544,1024]{1,0:T(8,128)(2,1)S(1)}, u32[]{:S(2)}, u32[]{:S(2)}) collective-permute-start(bf16[544,1024]{1,0:T(8,128)(2,1)} %get-tuple-element.367), channel_id=1, source_target_pairs={{0,1},{1,0},{2,3},{3,2},{4,5},{5,4},{6,7},{7,6},{8,9},{9,8},{10,11... | collective-permute-start | bytes 3342344 | tf_op jit(solution)/shard_map/ppermute | solution.py:335
  160.1 32.7 %collective-permute-start.34 = (bf16[512,1024]{1,0:T(8,128)(2,1)}, bf16[512,1024]{1,0:T(8,128)(2,1)S(1)}, u32[]{:S(2)}, u32[]{:S(2)}) collective-permute-start(bf16[512,1024]{1,0:T(8,128)(2,1)} %collective-permute-done.18.refs_3_), channel_id=1, source_target_pairs={{0,1},{1,0},{2,3},{3,2},{4,5},{5,4},{6,7},{7,6},{8,9},{9,8},{10,11... | collective-permute-start | bytes 3145736 | tf_op jit(solution)/shard_map/ppermute | solution.py:335
  160.2 32.7 %collective-permute-start.33 = (bf16[512,1024]{1,0:T(8,128)(2,1)}, bf16[512,1024]{1,0:T(8,128)(2,1)}, u32[]{:S(2)}, u32[]{:S(2)}) collective-permute-start(bf16[512,1024]{1,0:T(8,128)(2,1)} %collective-permute-done.30.refs_1_), channel_id=1, source_target_pairs={{0,2},{1,3},{2,4},{3,5},{4,6},{5,7},{6,0},{7,1},{8,10},{9,11},{10,... | collective-permute-start | bytes 3145736 | tf_op jit(solution)/shard_map/ppermute | solution.py:342
  193.8 32.1 %collective-permute-start.38 = (bf16[544,1024]{1,0:T(8,128)(2,1)}, bf16[544,1024]{1,0:T(8,128)(2,1)S(1)}, u32[]{:S(2)}, u32[]{:S(2)}) collective-permute-start(bf16[544,1024]{1,0:T(8,128)(2,1)} %get-tuple-element.389), channel_id=1, source_target_pairs={{0,1},{1,0},{2,3},{3,2},{4,5},{5,4},{6,7},{7,6},{8,9},{9,8},{10,11... | collective-permute-start | bytes 3342344 | tf_op jit(solution)/shard_map/ppermute | solution.py:335
  194.4 31.6 %collective-permute-start.37 = (bf16[512,1024]{1,0:T(8,128)(2,1)}, bf16[512,1024]{1,0:T(8,128)(2,1)}, u32[]{:S(2)}, u32[]{:S(2)}) collective-permute-start(bf16[512,1024]{1,0:T(8,128)(2,1)} %collective-permute-done.33.refs_1_), channel_id=1, source_target_pairs={{0,2},{1,3},{2,4},{3,5},{4,6},{5,7},{6,0},{7,1},{8,10},{9,11},{10,... | collective-permute-start | bytes 3145736 | tf_op jit(solution)/shard_map/ppermute | solution.py:342
  227.4 33.7 %collective-permute-start.40 = (bf16[544,1024]{1,0:T(8,128)(2,1)}, bf16[544,1024]{1,0:T(8,128)(2,1)S(1)}, u32[]{:S(2)}, u32[]{:S(2)}) collective-permute-start(bf16[544,1024]{1,0:T(8,128)(2,1)} %add_convert_fusion.5), channel_id=1, source_target_pairs={{0,2},{1,3},{2,4},{3,5},{4,6},{5,7},{6,0},{7,1},{8,10},{9,11},{10,... | collective-permute-start | bytes 3342344 | tf_op jit(solution)/shard_map/ppermute | solution.py:342
  229.0 32.1 %collective-permute-start.41 = (bf16[544,1024]{1,0:T(8,128)(2,1)}, bf16[544,1024]{1,0:T(8,128)(2,1)S(1)}, u32[]{:S(2)}, u32[]{:S(2)}) collective-permute-start(bf16[544,1024]{1,0:T(8,128)(2,1)} %get-tuple-element.415), channel_id=1, source_target_pairs={{0,1},{1,0},{2,3},{3,2},{4,5},{5,4},{6,7},{7,6},{8,9},{9,8},{10,11... | collective-permute-start | bytes 3342344 | tf_op jit(solution)/shard_map/ppermute | solution.py:335
  264.1 33.1 %collective-permute-start.43 = (bf16[544,1024]{1,0:T(8,128)(2,1)S(1)}, bf16[544,1024]{1,0:T(8,128)(2,1)S(1)}, u32[]{:S(2)}, u32[]{:S(2)}) collective-permute-start(bf16[544,1024]{1,0:T(8,128)(2,1)S(1)} %add_convert_fusion.4), channel_id=1, source_target_pairs={{0,2},{1,3},{2,4},{3,5},{4,6},{5,7},{6,0},{7,1},{8,10},{9,11},{10,... | collective-permute-start | bytes 3342344 | tf_op jit(solution)/shard_map/ppermute | solution.py:342
  265.8 31.4 %collective-permute-start.42 = (bf16[544,1024]{1,0:T(8,128)(2,1)}, bf16[544,1024]{1,0:T(8,128)(2,1)}, u32[]{:S(2)}, u32[]{:S(2)}) collective-permute-start(bf16[544,1024]{1,0:T(8,128)(2,1)} %get-tuple-element.443), channel_id=1, source_target_pairs={{0,1},{1,0},{2,3},{3,2},{4,5},{5,4},{6,7},{7,6},{8,9},{9,8},{10,11... | collective-permute-start | bytes 3342344 | tf_op jit(solution)/shard_map/ppermute | solution.py:335
  299.3 77.6 %collective-permute-start.47 = (bf16[2,3,512,512]{3,2,1,0:T(8,128)(2,1)}, bf16[2,3,512,512]{3,2,1,0:T(8,128)(2,1)}, u32[]{:S(2)}, u32[]{:S(2)}) collective-permute-start(bf16[2,3,512,512]{3,2,1,0:T(8,128)(2,1)} %get-tuple-element.464), channel_id=1, source_target_pairs={{0,8},{8,0},{16,24},{24,16},{1,9},{9,1},{17,25},{25,17},{2,10},{10... | collective-permute-start | bytes 9437192 | tf_op jit(solution)/shard_map/ppermute | solution.py:338
  300.9 76.0 %collective-permute-start.48 = (bf16[2,3,512,512]{3,2,1,0:T(8,128)(2,1)}, bf16[2,3,512,512]{3,2,1,0:T(8,128)(2,1)S(1)}, u32[]{:S(2)}, u32[]{:S(2)}) collective-permute-start(bf16[2,3,512,512]{3,2,1,0:T(8,128)(2,1)} %get-tuple-element.465), channel_id=1, source_target_pairs={{0,16},{8,24},{16,0},{24,8},{1,17},{9,25},{17,1},{25,9},{2,18},{10... | collective-permute-start | bytes 9437192 | tf_op jit(solution)/shard_map/ppermute | solution.py:338
  332.9 43.9 %collective-permute-start.46 = (bf16[512,1024]{1,0:T(8,128)(2,1)}, bf16[512,1024]{1,0:T(8,128)(2,1)}, u32[]{:S(2)}, u32[]{:S(2)}) collective-permute-start(bf16[512,1024]{1,0:T(8,128)(2,1)} %add_convert_fusion.12), channel_id=1, source_target_pairs={{0,2},{1,3},{2,4},{3,5},{4,6},{5,7},{6,0},{7,1},{8,10},{9,11},{10,... | collective-permute-start | bytes 3145736 | tf_op jit(solution)/shard_map/ppermute | solution.py:342
  387.7 36.6 %collective-permute-start.50 = (bf16[2,3,256,512]{3,2,1,0:T(8,128)(2,1)}, bf16[2,3,256,512]{3,2,1,0:T(8,128)(2,1)S(1)}, u32[]{:S(2)}, u32[]{:S(2)}) collective-permute-start(bf16[2,3,256,512]{3,2,1,0:T(8,128)(2,1)} %get-tuple-element.490), channel_id=1, source_target_pairs={{0,16},{8,24},{16,0},{24,8},{1,17},{9,25},{17,1},{25,9},{2,18},{10... | collective-permute-start | bytes 4718600 | tf_op jit(solution)/shard_map/ppermute | solution.py:338
  388.2 36.3 %collective-permute-start.51 = (bf16[2,3,256,512]{3,2,1,0:T(8,128)(2,1)}, bf16[2,3,256,512]{3,2,1,0:T(8,128)(2,1)S(1)}, u32[]{:S(2)}, u32[]{:S(2)}) collective-permute-start(bf16[2,3,256,512]{3,2,1,0:T(8,128)(2,1)} %get-tuple-element.491), channel_id=1, source_target_pairs={{0,8},{8,0},{16,24},{24,16},{1,9},{9,1},{17,25},{25,17},{2,10},{10... | collective-permute-start | bytes 4718600 | tf_op jit(solution)/shard_map/ppermute | solution.py:338
  429.1 35.3 %collective-permute-start.56 = (bf16[2,3,256,512]{3,2,1,0:T(8,128)(2,1)S(1)}, bf16[2,3,256,512]{3,2,1,0:T(8,128)(2,1)S(1)}, u32[]{:S(2)}, u32[]{:S(2)}) collective-permute-start(bf16[2,3,256,512]{3,2,1,0:T(8,128)(2,1)S(1)} %add_convert_fusion.1.refs_0_), channel_id=1, source_target_pairs={{0,16},{8,24},{16,0},{24,8},{1,17},{9,25},{17,1},{25,9},{2,18},{10... | collective-permute-start | bytes 4718600 | tf_op jit(solution)/shard_map/ppermute | solution.py:338
  430.7 35.3 %collective-permute-start.57 = (bf16[2,3,256,512]{3,2,1,0:T(8,128)(2,1)}, bf16[2,3,256,512]{3,2,1,0:T(8,128)(2,1)}, u32[]{:S(2)}, u32[]{:S(2)}) collective-permute-start(bf16[2,3,256,512]{3,2,1,0:T(8,128)(2,1)} %add_convert_fusion.refs_3_), channel_id=1, source_target_pairs={{0,8},{8,0},{16,24},{24,16},{1,9},{9,1},{17,25},{25,17},{2,10},{10... | collective-permute-start | bytes 4718600 | tf_op jit(solution)/shard_map/ppermute | solution.py:338
  466.3 45.6 %collective-permute-start.63 = (bf16[2,3,256,512]{3,2,1,0:T(8,128)(2,1)S(1)}, bf16[2,3,256,512]{3,2,1,0:T(8,128)(2,1)}, u32[]{:S(2)}, u32[]{:S(2)}) collective-permute-start(bf16[2,3,256,512]{3,2,1,0:T(8,128)(2,1)S(1)} %add_convert_fusion.1.refs_0_), channel_id=1, source_target_pairs={{0,8},{8,0},{16,24},{24,16},{1,9},{9,1},{17,25},{25,17},{2,10},{10... | collective-permute-start | bytes 4718600 | tf_op jit(solution)/shard_map/ppermute | solution.py:338
  467.2 44.7 %collective-permute-start.64 = (bf16[2,3,256,512]{3,2,1,0:T(8,128)(2,1)}, bf16[2,3,256,512]{3,2,1,0:T(8,128)(2,1)}, u32[]{:S(2)}, u32[]{:S(2)}) collective-permute-start(bf16[2,3,256,512]{3,2,1,0:T(8,128)(2,1)} %add_convert_fusion.refs_3_), channel_id=1, source_target_pairs={{0,16},{8,24},{16,0},{24,8},{1,17},{9,25},{17,1},{25,9},{2,18},{10... | collective-permute-start | bytes 4718600 | tf_op jit(solution)/shard_map/ppermute | solution.py:338
  512.0 37.7 %collective-permute-start.65 = (bf16[2,3,256,512]{3,2,1,0:T(8,128)(2,1)}, bf16[2,3,256,512]{3,2,1,0:T(8,128)(2,1)}, u32[]{:S(2)}, u32[]{:S(2)}) collective-permute-start(bf16[2,3,256,512]{3,2,1,0:T(8,128)(2,1)} %copy-done.16), channel_id=1, source_target_pairs={{0,8},{8,0},{16,24},{24,16},{1,9},{9,1},{17,25},{25,17},{2,10},{10... | collective-permute-start | bytes 4718600 | tf_op jit(solution)/shard_map/ppermute | solution.py:338
  512.4 37.9 %collective-permute-start.66 = (bf16[2,3,256,512]{3,2,1,0:T(8,128)(2,1)}, bf16[2,3,256,512]{3,2,1,0:T(8,128)(2,1)}, u32[]{:S(2)}, u32[]{:S(2)}) collective-permute-start(bf16[2,3,256,512]{3,2,1,0:T(8,128)(2,1)} %collective-permute-done.57.refs_4_), channel_id=1, source_target_pairs={{0,16},{8,24},{16,0},{24,8},{1,17},{9,25},{17,1},{25,9},{2,18},{10... | collective-permute-start | bytes 4718600 | tf_op jit(solution)/shard_map/ppermute | solution.py:338
  520.9 35.4 %collective-permute-start.69 = (bf16[32,3328]{1,0:T(8,128)(2,1)S(1)}, bf16[32,3328]{1,0:T(8,128)(2,1)S(1)}, u32[]{:S(2)}, u32[]{:S(2)}) collective-permute-start(bf16[32,3328]{1,0:T(8,128)(2,1)S(1)} %add_convert_fusion.20.refs_0_), channel_id=1, source_target_pairs={{0,8},{8,0},{16,24},{24,16},{1,9},{9,1},{17,25},{25,17},{2,10},{10... | collective-permute-start | bytes 638984 | tf_op jit(solution)/shard_map/ppermute | solution.py:338
  521.0 35.3 %collective-permute-start.70 = (bf16[32,3328]{1,0:T(8,128)(2,1)S(1)}, bf16[32,3328]{1,0:T(8,128)(2,1)S(1)}, u32[]{:S(2)}, u32[]{:S(2)}) collective-permute-start(bf16[32,3328]{1,0:T(8,128)(2,1)S(1)} %add_convert_fusion.20.refs_0_), channel_id=1, source_target_pairs={{0,16},{8,24},{16,0},{24,8},{1,17},{9,25},{17,1},{25,9},{2,18},{10... | collective-permute-start | bytes 638984 | tf_op jit(solution)/shard_map/ppermute | solution.py:338
  (88 other events, 1109.9 us)
